TPU v7x, 32 devices: a whole 2x2x4 slice. The times are simulated.
32 devices in a mesh: groups: 2 (over y), chan: 4 (over z), space: 2 (over x), pair: 2 (over core).
Axes of the slice: x: 2, y: 2, z: 4, core: 2. Of those that a mesh axis runs over, the one named last changes fastest.
Arguments:
- grad_out: bfloat16 [512, 32, 1024], P('chan', ('groups', 'space', 'pair')), parts along dimension 1, may hold values from -6 to 6
- conv_weight: bfloat16 [27, 512, 512], P(None, 'chan'), may hold values from -0.0546875 to 0.0546875
- pre_act: bfloat16 [32, 1024, 512], P(('groups', 'space', 'pair'), 'chan'), parts along dimension 0, may hold values from -6 to 6
- down_weight: bfloat16 [8, 256, 512], replicated, may hold values from -0.25 to 0.25
Outputs:
- grad_fine: bfloat16 [32, 1024, 8, 256], P(('groups', 'space', 'pair'), 'chan'), parts along dimension 0
There are 2 independent parts, one for each index of `groups`. A program takes and returns all parts, laid end to end along the dimension named above; an argument that names none is the same for every part. Nothing has to cross between parts.
All inputs are finite; a program needn't handle non-finite values.
Results may differ from a plain program's by a relative error of at most 0.025.
Values may be sent and summed in bfloat16 or wider, within the bound.
No kernel may reach another device: no remote copies, remote signals or barrier semaphores. Data moves between devices by JAX's collectives and lax.ppermute only.
A program may use at most 64 MiB of HBM per device.

v0:
```python
import math

import jax
import jax.numpy as jnp
from jax import lax
from jax.sharding import PartitionSpec as P

NZ = 8


def with_halo(cells, sides, width):
    for axis, dim in sides:
        count = lax.axis_size(axis)
        ends = count - 1
        head = lax.slice_in_dim(cells, 0, width, axis=dim)
        tail = lax.slice_in_dim(cells, cells.shape[dim] - width, cells.shape[dim], axis=dim)
        cells = jnp.concatenate(
            [
                lax.ppermute(tail, axis, [(i, (i + 1) % count) for i in range(ends)]),
                cells,
                lax.ppermute(head, axis, [((i + 1) % count, i) for i in range(ends)]),
            ],
            axis=dim,
        )
    return cells


def shifted_stack(padded, depth):
    extent = padded.shape[1] - 2
    plane_len = padded.shape[2]
    widened = jnp.pad(padded, ((0, 0), (0, 0), (depth + 1, depth + 1)))
    z_index = jnp.arange(plane_len, dtype=jnp.int32) % depth
    pieces = []
    for step_x in (-1, 0, 1):
        x_rows = widened[:, 1 - step_x : 1 - step_x + extent, :]
        for step_y in (-1, 0, 1):
            for step_z in (-1, 0, 1):
                offset = step_y * depth + step_z
                piece = x_rows[:, :, depth + 1 - offset : depth + 1 - offset + plane_len]
                inside = (z_index - step_z >= 0) & (z_index - step_z < depth)
                pieces.append(jnp.where(inside, piece, jnp.zeros_like(piece)))
    return jnp.stack(pieces)


def gelu_slope(values):
    return 0.5 * (1.0 + jax.scipy.special.erf(values / math.sqrt(2.0))) + values * jnp.exp(
        -0.5 * values * values
    ) / math.sqrt(2.0 * math.pi)


def body(grad_out, conv_weight, pre_act, down_weight):
    padded = with_halo(grad_out, ((("space", "pair"), 1),), 1)
    stacked = shifted_stack(padded, NZ)
    partial_sum = lax.dot_general(
        stacked, conv_weight, (((0, 1), (0, 1)), ((), ())), preferred_element_type=jnp.float32
    )
    owned = lax.psum_scatter(
        partial_sum.astype(jnp.bfloat16), "chan", scatter_dimension=2, tiled=True
    )
    grad_act = lax.all_to_all(owned, "chan", split_axis=1, concat_axis=2, tiled=True)
    values = pre_act.astype(jnp.float32)
    grad_pre = (grad_act.astype(jnp.float32) * gelu_slope(values)).astype(jnp.bfloat16)
    result = lax.dot_general(
        grad_pre, down_weight, (((2,), (2,)), ((), ())), preferred_element_type=jnp.float32
    )
    return result.astype(jnp.bfloat16)


def solution(mesh):
    in_specs = (
        P("chan", ("groups", "space", "pair"), None),
        P(None, "chan", None),
        P(("groups", "space", "pair"), "chan", None),
        P(),
    )
    out_specs = P(("groups", "space", "pair"), "chan", None, None)
    return jax.shard_map(body, mesh=mesh, in_specs=in_specs, out_specs=out_specs, check_vma=False)
```

profile of v0, /device:TPU:0, one launch (start us, length us, event | category | flops | bytes accessed | tf_op | source)
XLA Modules:
  0.0 204.0 jit_solution(13061538225299000226)
XLA Ops:
  6.5 2.8 %copy.39 = bf16[128,4,1024]{0,2,1:T(8,128)(2,1)} copy(bf16[128,4,1024]{2,1,0:T(4,128)(2,1)} %param.4) | data formatting | bytes 2097152 | tf_op args[0]
  9.3 1.2 fusion.98
  10.5 2.4 %collective-permute-start = (bf16[128,1,1024]{0,2,1:T(8,128)(2,1)S(1)}, bf16[128,1,1024]{0,2,1:T(8,128)(2,1)S(1)}, u32[]{:S(2)}, u32[]{:S(2)}) collective-permute-start(bf16[128,1,1024]{0,2,1:T(8,128)(2,1)S(1)} %get-tuple-element.5), channel_id=1, source_target_pairs={{0,1},{1,2},{2,3},{4,5},{5,6},{6,7},{8,9},{9,10},{10,11},{12,13},{... | collective-permute-start | bytes 786440 | tf_op jit(solution)/shard_map/ppermute | solution.py:19
  12.9 1.3 collective-permute-start.1
  14.2 4.2 %collective-permute-done.1 = bf16[128,1,1024]{0,2,1:T(8,128)(2,1)S(1)} collective-permute-done((bf16[128,1,1024]{0,2,1:T(8,128)(2,1)S(1)}, bf16[128,1,1024]{0,2,1:T(8,128)(2,1)S(1)}, u32[]{:S(2)}, u32[]{:S(2)}) %collective-permute-start.1) | collective-permute-done | bytes 262176 | tf_op jit(solution)/shard_map/ppermute | solution.py:21
  18.4 1.6 fusion.18
  23.1 0.6 fusion.59
  23.7 0.6 fusion.57
  24.8 0.6 fusion.53
  25.4 0.6 fusion.51
  29.8 0.6 fusion.37
  30.4 0.6 fusion.35
  33.1 0.8 fusion.24
  35.0 17.0 %bitcast_convert_fusion = bf16[4,1024,512]{2,1,0:T(8,128)(2,1)} fusion(bf16[27,128,4,1024]{1,3,0,2:T(8,128)(2,1)S(1)} %fusion.20, bf16[27,128,512]{2,1,0:T(8,128)(2,1)S(1)} %copy-done), kind=kOutput, calls=%fused_computation | convolution fusion | flops 14497611776 | bytes 36044800 | tf_op jit(solution)/shard_map/dot_general | solution.py:54
  52.0 8.0 %copy.76 = bf16[4,1024,512]{1,0,2:T(4,128)(2,1)} copy(bf16[4,1024,512]{2,1,0:T(8,128)(2,1)} %bitcast_convert_fusion) | data formatting | bytes 8388608
  60.0 6.5 %copy.79 = bf16[64,8,4,1024]{3,1,2,0:T(8,128)(2,1)} copy(bf16[64,8,4,1024]{3,2,1,0:T(4,128)(2,1)} %bitcast.184) | data formatting | bytes 8388608
  66.5 81.7 %reduce-scatter.4.cloned.1.call-done = bf16[128,4096]{1,0:T(8,128)(2,1)} async-done(((bf16[512,4096]{1,0:T(8,128)(2,1)}), bf16[128,4096]{1,0:T(8,128)(2,1)}) %reduce-scatter.4.cloned.1.call-update) | async-done | bytes 1048592
  148.2 1.8 reshape.11
  150.0 1.5 copy.71
  151.5 29.8 %all_to_all.4 = bf16[4,1024,128]{2,0,1:T(4,128)(2,1)S(1)} all-to-all(bf16[4,1024,128]{2,0,1:T(4,128)(2,1)S(1)} %copy.71), channel_id=1, replica_groups=mesh['groups'=2,'chan'=4,'space'=2,'pair'=2] {'chan'}, dimensions={1} | all-to-all | bytes 2097152 | tf_op jit(solution)/shard_map/all_to_all | solution.py:60
  181.4 2.7 %copy.72 = f32[4,256,4,128]{3,2,1,0:T(4,128)} copy(f32[4,256,4,128]{3,0,1,2:T(4,128)S(1)} %convert_bitcast_fusion) | data formatting | bytes 4194304 | tf_op jit(solution)/shard_map/convert_element_type | solution.py:62
  184.1 3.3 %reshape.4 = f32[4,256,512]{2,1,0:T(8,128)} reshape(f32[4,256,4,128]{3,2,1,0:T(4,128)} %copy.72) | data formatting | bytes 4194304 | tf_op jit(solution)/shard_map/convert_element_type | solution.py:62
  187.4 5.3 %convolution_convert_fusion = bf16[4,256,8,256]{3,1,2,0:T(8,128)(2,1)S(1)} fusion(bf16[8,256,512]{2,1,0:T(8,128)(2,1)} %param.7, f32[4,256,512]{2,1,0:T(8,128)} %reshape.4, bf16[4,256,512]{2,1,0:T(8,128)(2,1)} %param.6), kind=kOutput, calls=%fused_computation.10 | convolution fusion | flops 2155347968 | bytes 9437184 | tf_op jit(solution)/shard_map/dot_general | solution.py:63
  192.7 4.5 %copy.73 = bf16[4,256,8,256]{3,2,1,0:T(8,128)(2,1)} copy(bf16[4,256,8,256]{3,1,2,0:T(8,128)(2,1)S(1)} %convolution_convert_fusion) | data formatting | bytes 8388608 | tf_op jit(solution)/shard_map/convert_element_type | solution.py:66
  (33 shorter events, 10.5 us)
Async XLA Ops:
  6.5 28.4 %copy-start = (bf16[27,128,512]{2,1,0:T(8,128)(2,1)S(1)}, bf16[27,128,512]{2,1,0:T(8,128)(2,1)}, u32[]{:S(2)}) copy-start(bf16[27,128,512]{2,1,0:T(8,128)(2,1)} %param.5) | copy-start | bytes 10616836
  6.5 141.6 %reduce-scatter.4.cloned.1.call-start = ((), (), s32[]{:S(2)}) async-start(), calls=%async_computation.2 | async-start | bytes 5242880
  9.3 12.8 %copy-start.2 = (bf16[128,4,1024]{0,2,1:T(8,128)(2,1)S(1)}, bf16[128,4,1024]{0,2,1:T(8,128)(2,1)}, u32[]{:S(2)}) copy-start(bf16[128,4,1024]{0,2,1:T(8,128)(2,1)} %copy.39) | copy-start | bytes 3145732
  10.5 3.7 %collective-permute-start = (bf16[128,1,1024]{0,2,1:T(8,128)(2,1)S(1)}, bf16[128,1,1024]{0,2,1:T(8,128)(2,1)S(1)}, u32[]{:S(2)}, u32[]{:S(2)}) collective-permute-start(bf16[128,1,1024]{0,2,1:T(8,128)(2,1)S(1)} %get-tuple-element.5), channel_id=1, source_target_pairs={{0,1},{1,2},{2,3},{4,5},{5,6},{6,7},{8,9},{9,10},{10,11},{12,13},{... | collective-permute-start | bytes 786440 | tf_op jit(solution)/shard_map/ppermute | solution.py:19
  12.9 5.5 %collective-permute-start.1 = (bf16[128,1,1024]{0,2,1:T(8,128)(2,1)S(1)}, bf16[128,1,1024]{0,2,1:T(8,128)(2,1)S(1)}, u32[]{:S(2)}, u32[]{:S(2)}) collective-permute-start(bf16[128,1,1024]{0,2,1:T(8,128)(2,1)S(1)} %get-tuple-element.6), channel_id=1, source_target_pairs={{1,0},{2,1},{3,2},{5,4},{6,5},{7,6},{9,8},{10,9},{11,10},{13,12},{... | collective-permute-start | bytes 786440 | tf_op jit(solution)/shard_map/ppermute | solution.py:21
  184.1 13.1 %copy-start.1 = (bf16[27,128,512]{2,1,0:T(8,128)(2,1)S(1)}, bf16[27,128,512]{2,1,0:T(8,128)(2,1)}, u32[]{:S(2)}) copy-start(bf16[27,128,512]{2,1,0:T(8,128)(2,1)} %param.5) | copy-start | bytes 10616836
Sparse Core Ops, SparseCore 0:
  66.6 81.4 reduce-scatter.3
where the time goes:
time: 204 us
  waiting for transfers between devices  85.8 us (42%)
  local copies, waits for them, and re-layouts  32.2 us (16%)
  blocking collectives  29.8 us (15%)
  matrix products  22.4 us (11%)
  other arithmetic  16.5 us (8%)
  between operations  13.7 us (7%)
  starting transfers between devices  3.67 us (2%)
    unnamed x2, waiting for transfers between devices  81.7 us
    all_to_all x1, blocking collectives, body(): lax.all_to_all(owned, 'chan', split_axis=1, concat_axis=2, tiled=True)  29.8 us
    unnamed x10, local copies, waits for them, and re-layouts  19.1 us
    dot_general x1, matrix products, body(): lax.dot_general(stacked, conv_weight, (((0, 1), (0, 1)), ((), ())), prefe...  17 us
    unnamed x26, other arithmetic  14.2 us
    convert_element_type x2, local copies, waits for them, and re-layouts, body(): grad_act.astype(jnp.float32) * gelu_slope(values)  5.93 us
    dot_general x1, matrix products, body(): lax.dot_general(grad_pre, down_weight, (((2,), (2,)), ((), ())), preferre...  5.33 us
    convert_element_type x1, local copies, waits for them, and re-layouts, body(): return result.astype(jnp.bfloat16)  4.47 us
  transfers between devices with their start and end apart: 3, of which 2 were waited for; matrix products, arithmetic and copies ran while one was open for 0% of the time, Pallas kernels for 0%

commit v1 on v0

--- a/solution.py
+++ b/solution.py
@@ -54,10 +54,9 @@
     partial_sum = lax.dot_general(
         stacked, conv_weight, (((0, 1), (0, 1)), ((), ())), preferred_element_type=jnp.float32
     )
-    owned = lax.psum_scatter(
-        partial_sum.astype(jnp.bfloat16), "chan", scatter_dimension=2, tiled=True
+    grad_act = lax.psum_scatter(
+        partial_sum.astype(jnp.bfloat16), "chan", scatter_dimension=1, tiled=True
     )
-    grad_act = lax.all_to_all(owned, "chan", split_axis=1, concat_axis=2, tiled=True)
     values = pre_act.astype(jnp.float32)
     grad_pre = (grad_act.astype(jnp.float32) * gelu_slope(values)).astype(jnp.bfloat16)
     result = lax.dot_general(

time: 204 us -> 215 us (1.054); the launches traced: 204 us -> 212 us
  other arithmetic: 16.5 us -> 70.8 us
  blocking collectives: 29.8 us -> 0 us
  local copies, waits for them, and re-layouts: 32.2 us -> 7.07 us
  matrix products: 22.4 us -> 27.8 us
  waiting for transfers between devices: 85.8 us -> 88.6 us
    reduce_scatter x0 -> x1, waiting for transfers between devices: none -> 84.1 us  [body(): lax.psum_scatter(partial_sum.astype(jnp.bfloat16), 'chan', scatter_dimens...]
    unnamed x2 -> x1, waiting for transfers between devices: 81.7 us -> 0.02 us
    unnamed x26, other arithmetic: 14.2 us -> 63.5 us
    all_to_all x1 -> x0, blocking collectives: 29.8 us -> none  [body(): lax.all_to_all(owned, 'chan', split_axis=1, concat_axis=2, tiled=True)]
    unnamed x10 -> x4, local copies, waits for them, and re-layouts: 19.1 us -> 0.01 us
    convert_element_type x2 -> x0, local copies, waits for them, and re-layouts: 5.93 us -> none  [body(): grad_act.astype(jnp.float32) * gelu_slope(values)]
    dot_general x1, matrix products: 17 us -> 22.8 us  [body(): lax.dot_general(stacked, conv_weight, (((0, 1), (0, 1)), ((), ())), prefe...]
    concatenate x1, other arithmetic: 1.64 us -> 5.86 us  [with_halo(): jnp.concatenate([lax.ppermute(tail, axis, [(i, (i + 1) % count) for i in...]
  transfers between devices with their start and end apart: 3 -> 3, of which waited for: 2 -> 3; matrix products, arithmetic and copies ran while one was open for 0% -> 0% of each run, Pallas kernels for 0% -> 0%
where the time goes in v1:
time: 215 us; the launch traced here: 212 us
  waiting for transfers between devices  88.6 us (41%)
  other arithmetic  70.8 us (33%)
  matrix products  27.8 us (13%)
  between operations  13.7 us (6%)
  local copies, waits for them, and re-layouts  7.07 us (3%)
  starting transfers between devices  3.68 us (2%)
    reduce_scatter x1, waiting for transfers between devices, body(): lax.psum_scatter(partial_sum.astype(jnp.bfloat16), 'chan', scatter_dimens...  84.1 us
    unnamed x26, other arithmetic  63.5 us
    dot_general x1, matrix products, body(): lax.dot_general(stacked, conv_weight, (((0, 1), (0, 1)), ((), ())), prefe...  22.8 us
    concatenate x1, other arithmetic, with_halo(): jnp.concatenate([lax.ppermute(tail, axis, [(i, (i + 1) % count) for i in...  5.86 us
    dot_general x1, matrix products, body(): lax.dot_general(grad_pre, down_weight, (((2,), (2,)), ((), ())), preferre...  5.07 us
    convert_element_type x1, local copies, waits for them, and re-layouts, body(): return result.astype(jnp.bfloat16)  4.47 us
    ppermute x1, waiting for transfers between devices, with_halo(): lax.ppermute(head, axis, [((i + 1) % count, i) for i in range(ends)])  4.39 us
  transfers between devices with their start and end apart: 3, of which 3 were waited for; matrix products, arithmetic and copies ran while one was open for 0% of the time, Pallas kernels for 0%

profile of v1, /device:TPU:0, one launch (start us, length us, event | category | flops | bytes accessed | tf_op | source)
XLA Modules:
  0.0 211.7 jit_solution(7096933128114898558)
XLA Ops:
  6.5 2.6 %fusion.101 = (bf16[128,1,1024]{2,1,0:T(2,128)(2,1)S(1)}, bf16[128,1,1024]{2,1,0:T(2,128)(2,1)S(1)}) fusion(bf16[128,4,1024]{2,1,0:T(4,128)(2,1)} %param.4), kind=kLoop, calls=%fused_computation.133 | loop fusion | bytes 1048576 | tf_op jit(solution)/shard_map/slice | solution.py:16
  13.0 4.4 %collective-permute-done.1 = bf16[128,1,1024]{2,1,0:T(2,128)(2,1)S(1)} collective-permute-done((bf16[128,1,1024]{2,1,0:T(2,128)(2,1)S(1)}, bf16[128,1,1024]{2,1,0:T(2,128)(2,1)S(1)}, u32[]{:S(2)}, u32[]{:S(2)}) %collective-permute-start.1) | collective-permute-done | bytes 262176 | tf_op jit(solution)/shard_map/ppermute | solution.py:21
  17.4 5.9 %fusion.12 = bf16[128,6,1042]{2,1,0:T(8,128)(2,1)S(1)} fusion(bf16[128,1,1024]{2,1,0:T(2,128)(2,1)S(1)} %collective-permute-done.1, bf16[128,4,1024]{2,1,0:T(4,128)(2,1)} %param.4, bf16[128,1,1024]{2,1,0:T(2,128)(2,1)S(1)} %collective-permute-done), kind=kLoop, calls=%fused_computation.16 | loop fusion | flops 9603072 | bytes 3173376 | tf_op jit(solution)/shard_map/concatenate | solution.py:17
  25.5 2.5 %fusion.73 = bf16[27,128,4,1024]{3,2,1,0:T(4,128)(2,1)} fusion(bf16[27,128,4,1024]{3,2,1,0:T(4,128)(2,1)} %fusion.75, bf16[128,6,1042]{2,1,0:T(8,128)(2,1)S(1)} %fusion.12, pred[1024]{0:T(1024)(128)(4,1)S(1)} %fusion.94), kind=kLoop, calls=%fused_computation.102 | loop fusion | flops 524288 | bytes 2098176
  28.1 2.5 %fusion.71 = bf16[27,128,4,1024]{3,2,1,0:T(4,128)(2,1)} fusion(bf16[27,128,4,1024]{3,2,1,0:T(4,128)(2,1)} %fusion.73, bf16[128,6,1042]{2,1,0:T(8,128)(2,1)S(1)} %fusion.12, pred[1024]{0:T(1024)(128)(4,1)S(1)} %fusion.92), kind=kLoop, calls=%fused_computation.99 | loop fusion | flops 524288 | bytes 2098176
  30.5 2.5 %fusion.69 = bf16[27,128,4,1024]{3,2,1,0:T(4,128)(2,1)} fusion(bf16[27,128,4,1024]{3,2,1,0:T(4,128)(2,1)} %fusion.71, bf16[128,6,1042]{2,1,0:T(8,128)(2,1)S(1)} %fusion.12, pred[1024]{0:T(1024)(128)(4,1)S(1)} %fusion.93), kind=kLoop, calls=%fused_computation.96 | loop fusion | flops 524288 | bytes 2098176
  33.0 3.7 %fusion.67 = bf16[27,128,4,1024]{3,2,1,0:T(4,128)(2,1)} fusion(bf16[27,128,4,1024]{3,2,1,0:T(4,128)(2,1)} %fusion.69, bf16[128,1,1024]{2,1,0:T(2,128)(2,1)S(1)} %collective-permute-done.1, bf16[128,4,1024]{2,1,0:T(4,128)(2,1)} %param.4, pred[1024]{0:T(1024)(128)(4,1)S(1)} %fusion.94), kind=kLoop, calls=%fused_computation.93 | loop fusion | flops 2621440 | bytes 2360320
  36.7 2.5 %fusion.64 = bf16[27,128,4,1024]{3,2,1,0:T(4,128)(2,1)} fusion(bf16[27,128,4,1024]{3,2,1,0:T(4,128)(2,1)} %fusion.67, bf16[128,6,1042]{2,1,0:T(8,128)(2,1)S(1)} %fusion.12, pred[1024]{0:T(1024)(128)(4,1)S(1)} %fusion.92), kind=kLoop, calls=%fused_computation.89 | loop fusion | flops 524288 | bytes 2098176
  39.2 2.5 %fusion.62 = bf16[27,128,4,1024]{3,2,1,0:T(4,128)(2,1)} fusion(bf16[27,128,4,1024]{3,2,1,0:T(4,128)(2,1)} %fusion.64, bf16[128,6,1042]{2,1,0:T(8,128)(2,1)S(1)} %fusion.12, pred[1024]{0:T(1024)(128)(4,1)S(1)} %fusion.93), kind=kLoop, calls=%fused_computation.86 | loop fusion | flops 524288 | bytes 2098176
  41.7 2.7 %fusion.60 = bf16[27,128,4,1024]{3,2,1,0:T(4,128)(2,1)} fusion(bf16[27,128,4,1024]{3,2,1,0:T(4,128)(2,1)} %fusion.62, bf16[128,6,1042]{2,1,0:T(8,128)(2,1)S(1)} %fusion.12, pred[1024]{0:T(1024)(128)(4,1)S(1)} %fusion.94), kind=kLoop, calls=%fused_computation.83 | loop fusion | flops 524288 | bytes 2098176
  48.6 2.5 %fusion.54 = bf16[27,128,4,1024]{3,2,1,0:T(4,128)(2,1)} fusion(bf16[27,128,4,1024]{3,2,1,0:T(4,128)(2,1)} %fusion.56, bf16[128,6,1042]{2,1,0:T(8,128)(2,1)S(1)} %fusion.12, pred[1024]{0:T(1024)(128)(4,1)S(1)} %fusion.94), kind=kLoop, calls=%fused_computation.74 | loop fusion | flops 524288 | bytes 2098176
  51.0 2.5 %fusion.52 = bf16[27,128,4,1024]{3,2,1,0:T(4,128)(2,1)} fusion(bf16[27,128,4,1024]{3,2,1,0:T(4,128)(2,1)} %fusion.54, bf16[128,6,1042]{2,1,0:T(8,128)(2,1)S(1)} %fusion.12, pred[1024]{0:T(1024)(128)(4,1)S(1)} %fusion.92), kind=kLoop, calls=%fused_computation.71 | loop fusion | flops 524288 | bytes 2098176
  53.5 2.5 %fusion.50 = bf16[27,128,4,1024]{3,2,1,0:T(4,128)(2,1)} fusion(bf16[27,128,4,1024]{3,2,1,0:T(4,128)(2,1)} %fusion.52, bf16[128,6,1042]{2,1,0:T(8,128)(2,1)S(1)} %fusion.12, pred[1024]{0:T(1024)(128)(4,1)S(1)} %fusion.93), kind=kLoop, calls=%fused_computation.68 | loop fusion | flops 524288 | bytes 2098176
  57.5 2.5 %fusion.48 = bf16[27,128,4,1024]{3,2,1,0:T(4,128)(2,1)} fusion(bf16[27,128,4,1024]{3,2,1,0:T(4,128)(2,1)} %bitcast_dynamic-update-slice_fusion, bf16[128,6,1042]{2,1,0:T(8,128)(2,1)S(1)} %fusion.12, pred[1024]{0:T(1024)(128)(4,1)S(1)} %fusion.92), kind=kLoop, calls=%fused_computation.65 | loop fusion | flops 524288 | bytes 2098176
  60.0 2.5 %fusion.46 = bf16[27,128,4,1024]{3,2,1,0:T(4,128)(2,1)} fusion(bf16[27,128,4,1024]{3,2,1,0:T(4,128)(2,1)} %fusion.48, bf16[128,6,1042]{2,1,0:T(8,128)(2,1)S(1)} %fusion.12, pred[1024]{0:T(1024)(128)(4,1)S(1)} %fusion.93), kind=kLoop, calls=%fused_computation.62 | loop fusion | flops 524288 | bytes 2098176
  62.5 2.7 %fusion.44 = bf16[27,128,4,1024]{3,2,1,0:T(4,128)(2,1)} fusion(bf16[27,128,4,1024]{3,2,1,0:T(4,128)(2,1)} %fusion.46, bf16[128,6,1042]{2,1,0:T(8,128)(2,1)S(1)} %fusion.12, pred[1024]{0:T(1024)(128)(4,1)S(1)} %fusion.94), kind=kLoop, calls=%fused_computation.59 | loop fusion | flops 524288 | bytes 2098176
  74.3 2.5 %fusion.34 = bf16[27,128,4,1024]{3,2,1,0:T(4,128)(2,1)} fusion(bf16[27,128,4,1024]{3,2,1,0:T(4,128)(2,1)} %fusion.36, bf16[128,6,1042]{2,1,0:T(8,128)(2,1)S(1)} %fusion.12, pred[1024]{0:T(1024)(128)(4,1)S(1)} %fusion.93), kind=kLoop, calls=%fused_computation.44 | loop fusion | flops 524288 | bytes 2098176
  79.0 2.5 %fusion.29 = bf16[27,128,4,1024]{3,2,1,0:T(4,128)(2,1)} fusion(bf16[27,128,4,1024]{3,2,1,0:T(4,128)(2,1)} %fusion.32, bf16[128,6,1042]{2,1,0:T(8,128)(2,1)S(1)} %fusion.12, pred[1024]{0:T(1024)(128)(4,1)S(1)} %fusion.92), kind=kLoop, calls=%fused_computation.37 | loop fusion | flops 524288 | bytes 2098176
  81.4 2.5 %fusion.27 = bf16[27,128,4,1024]{3,2,1,0:T(4,128)(2,1)} fusion(bf16[27,128,4,1024]{3,2,1,0:T(4,128)(2,1)} %fusion.29, bf16[128,6,1042]{2,1,0:T(8,128)(2,1)S(1)} %fusion.12, pred[1024]{0:T(1024)(128)(4,1)S(1)} %fusion.93), kind=kLoop, calls=%fused_computation.34 | loop fusion | flops 524288 | bytes 2098176
  83.9 2.8 %fusion.25 = bf16[27,128,4,1024]{3,2,1,0:T(4,128)(2,1)} fusion(bf16[27,128,4,1024]{3,2,1,0:T(4,128)(2,1)} %fusion.27, bf16[128,6,1042]{2,1,0:T(8,128)(2,1)S(1)} %fusion.12, pred[1024]{0:T(1024)(128)(4,1)S(1)} %fusion.94), kind=kLoop, calls=%fused_computation.31 | loop fusion | flops 524288 | bytes 2098176
  88.2 22.8 %bitcast_convert_fusion = bf16[4,1024,512]{2,1,0:T(8,128)(2,1)} fusion(bf16[27,128,512]{2,1,0:T(8,128)(2,1)S(1)} %copy-done, bf16[27,128,4,1024]{3,2,1,0:T(4,128)(2,1)} %fusion.23), kind=kOutput, calls=%fused_computation.2 | convolution fusion | flops 14497611776 | bytes 36044800 | tf_op jit(solution)/shard_map/dot_general | solution.py:54
  111.0 84.1 %reduce-scatter.2.cloned.1.call-done = bf16[4,256,512]{2,1,0:T(8,128)(2,1)} async-done(((bf16[4,1024,512]{2,1,0:T(8,128)(2,1)}), bf16[4,256,512]{2,1,0:T(8,128)(2,1)}) %reduce-scatter.2.cloned.1.call-update) | async-done | bytes 1048592 | tf_op jit(solution)/shard_map/reduce_scatter | solution.py:57
  195.1 5.1 %convolution_convert_fusion = bf16[4,256,8,256]{3,1,2,0:T(8,128)(2,1)S(1)} fusion(bf16[8,256,512]{2,1,0:T(8,128)(2,1)} %param.7, bf16[4,256,512]{2,1,0:T(8,128)(2,1)} %param.6, bf16[4,256,512]{2,1,0:T(8,128)(2,1)} %reduce-scatter.2.cloned.1.call-done), kind=kOutput, calls=%fused_computation.14 | convolution fusion | flops 2155872256 | bytes 8388608 | tf_op jit(solution)/shard_map/dot_general | solution.py:62
  200.2 4.5 %copy.5 = bf16[4,256,8,256]{3,2,1,0:T(8,128)(2,1)} copy(bf16[4,256,8,256]{3,1,2,0:T(8,128)(2,1)S(1)} %convolution_convert_fusion) | data formatting | bytes 8388608 | tf_op jit(solution)/shard_map/convert_element_type | solution.py:65
  (22 shorter events, 24.5 us)
Async XLA Ops:
  6.5 81.7 %copy-start = (bf16[27,128,512]{2,1,0:T(8,128)(2,1)S(1)}, bf16[27,128,512]{2,1,0:T(8,128)(2,1)}, u32[]{:S(2)}) copy-start(bf16[27,128,512]{2,1,0:T(8,128)(2,1)} %param.5) | copy-start | bytes 10616836
  6.5 188.6 %reduce-scatter.2.cloned.1.call-start = ((), (), s32[]{:S(2)}) async-start(), calls=%async_computation.1 | async-start | bytes 5242880 | tf_op jit(solution)/shard_map/reduce_scatter | solution.py:57
  6.5 49.5 %copy-start.1 = (bf16[128,4,1024]{2,1,0:T(4,128)(2,1)S(1)}, bf16[128,4,1024]{2,1,0:T(4,128)(2,1)}, u32[]{:S(2)}) copy-start(bf16[128,4,1024]{2,1,0:T(4,128)(2,1)} %param.4) | copy-start | bytes 3145732
  9.1 3.9 %collective-permute-start = (bf16[128,1,1024]{2,1,0:T(2,128)(2,1)S(1)}, bf16[128,1,1024]{2,1,0:T(2,128)(2,1)S(1)}, u32[]{:S(2)}, u32[]{:S(2)}) collective-permute-start(bf16[128,1,1024]{2,1,0:T(2,128)(2,1)S(1)} %get-tuple-element.5), channel_id=1, source_target_pairs={{0,1},{1,2},{2,3},{4,5},{5,6},{6,7},{8,9},{9,10},{10,11},{12,13},{... | collective-permute-start | bytes 786440 | tf_op jit(solution)/shard_map/ppermute | solution.py:19
  11.5 5.9 %collective-permute-start.1 = (bf16[128,1,1024]{2,1,0:T(2,128)(2,1)S(1)}, bf16[128,1,1024]{2,1,0:T(2,128)(2,1)S(1)}, u32[]{:S(2)}, u32[]{:S(2)}) collective-permute-start(bf16[128,1,1024]{2,1,0:T(2,128)(2,1)S(1)} %get-tuple-element.6), channel_id=1, source_target_pairs={{1,0},{2,1},{3,2},{5,4},{6,5},{7,6},{9,8},{10,9},{11,10},{13,12},{... | collective-permute-start | bytes 786440 | tf_op jit(solution)/shard_map/ppermute | solution.py:21
Sparse Core Ops, SparseCore 0:
  111.1 83.9 reduce-scatter.1

commit v2 on v0

--- a/solution.py
+++ b/solution.py
@@ -1,11 +1,22 @@
+import functools
 import math
 
 import jax
 import jax.numpy as jnp
 from jax import lax
+from jax.experimental import pallas as pl
+from jax.experimental.pallas import tpu as pltpu
 from jax.sharding import PartitionSpec as P
 
 NZ = 8
+PLANAR = ("groups", "space", "pair")
+SLAB = ("space", "pair")
+
+
+def gelu_slope(values):
+    return 0.5 * (1.0 + jax.scipy.special.erf(values / math.sqrt(2.0))) + values * jnp.exp(
+        -0.5 * values * values
+    ) / math.sqrt(2.0 * math.pi)
 
 
 def with_halo(cells, sides, width):
@@ -42,14 +53,8 @@
     return jnp.stack(pieces)
 
 
-def gelu_slope(values):
-    return 0.5 * (1.0 + jax.scipy.special.erf(values / math.sqrt(2.0))) + values * jnp.exp(
-        -0.5 * values * values
-    ) / math.sqrt(2.0 * math.pi)
-
-
-def body(grad_out, conv_weight, pre_act, down_weight):
-    padded = with_halo(grad_out, ((("space", "pair"), 1),), 1)
+def general_body(grad_out, conv_weight, pre_act, down_weight):
+    padded = with_halo(grad_out, ((SLAB, 1),), 1)
     stacked = shifted_stack(padded, NZ)
     partial_sum = lax.dot_general(
         stacked, conv_weight, (((0, 1), (0, 1)), ((), ())), preferred_element_type=jnp.float32
@@ -66,12 +71,226 @@
     return result.astype(jnp.bfloat16)
 
 
+def conv_kernel(where_ref, main_ref, low_ref, high_ref, *refs, pieces, added):
+    weights = refs[:pieces]
+    start_ref = refs[pieces] if added else None
+    out_ref, copies, table, sems = refs[pieces + int(added) :]
+    extent = main_ref.shape[1]
+    rows = main_ref.shape[2]
+    width = main_ref.shape[3]
+    cells = rows - 2 * NZ
+    share = table.shape[0] // pieces
+    if pieces == 1:
+        spots = [0]
+    else:
+        q = where_ref[0]
+        first = 2 + 2 * (q & 1)
+        second = 6 - first
+        spots = [q, q ^ first, q ^ second, q ^ 6, q ^ 1, q ^ 1 ^ second, q ^ 1 ^ first, q ^ 7]
+    loads = []
+    for n in range(pieces):
+        row = spots[n] * share if pieces == 1 else pl.multiple_of(spots[n] * share, 16)
+        loads.append(
+            pltpu.make_async_copy(weights[n], table.at[pl.ds(row, share), :], sems.at[n])
+        )
+
+    @pl.when(pl.program_id(0) == 0)
+    def _():
+        for load in loads:
+            load.start()
+
+    depth_at = lax.broadcasted_iota(jnp.int32, (rows, width), 0) % NZ
+    for x in range(extent + 2):
+        if x == 0:
+            plane = low_ref[0, 0]
+        elif x == extent + 1:
+            plane = high_ref[0, 0]
+        else:
+            plane = main_ref[0, x - 1]
+        plane = plane.astype(jnp.float32)
+        for step_z in (-1, 0, 1):
+            if step_z == 1:
+                moved = jnp.where(depth_at >= 1, pltpu.roll(plane, 1, 0), 0.0)
+            elif step_z == -1:
+                moved = jnp.where(depth_at < NZ - 1, pltpu.roll(plane, rows - 1, 0), 0.0)
+            else:
+                moved = plane
+            for step_y in (-1, 0, 1):
+                at = NZ * (1 - step_y)
+                lane = (3 * (step_y + 1) + step_z + 1) * width
+                copies[x, :, lane : lane + width] = moved[at : at + cells].astype(jnp.bfloat16)
+
+    @pl.when(pl.program_id(0) == 0)
+    def _():
+        for load in loads:
+            load.wait()
+
+    total = start_ref[0] if added else None
+    for step_x in (-1, 0, 1):
+        left = copies[1 - step_x : 1 - step_x + extent].reshape(extent * cells, 9 * width)
+        right = table[(step_x + 1) * 9 * width : (step_x + 2) * 9 * width]
+        term = jnp.dot(left, right, preferred_element_type=jnp.float32)
+        total = term if total is None else total + term
+    out_ref[0] = total.astype(out_ref.dtype)
+
+
+def conv_blocks(where, main, low, high, weights, start, slot, kind):
+    count, extent, rows, width = main.shape
+    cells = extent * (rows - 2 * NZ)
+    wide = weights[0].shape[1]
+    table_rows = sum(v.shape[0] for v in weights)
+    in_specs = [
+        pl.BlockSpec(memory_space=pltpu.SMEM),
+        pl.BlockSpec((1, extent, rows, width), lambda i: (i, 0, 0, 0)),
+        pl.BlockSpec((1, 1, rows, width), lambda i: (i, 0, 0, 0)),
+        pl.BlockSpec((1, 1, rows, width), lambda i: (i, 0, 0, 0)),
+    ] + [pl.BlockSpec(memory_space=pl.ANY)] * len(weights)
+    operands = [where, main, low, high, *weights]
+    if start is not None:
+        in_specs.append(pl.BlockSpec((1, cells, wide), lambda i: (slot + i, 0, 0)))
+        operands.append(start)
+    return pl.pallas_call(
+        functools.partial(conv_kernel, pieces=len(weights), added=start is not None),
+        grid=(count,),
+        in_specs=in_specs,
+        out_specs=pl.BlockSpec((1, cells, wide), lambda i: (i, 0, 0)),
+        out_shape=jax.ShapeDtypeStruct((count, cells, wide), kind),
+        scratch_shapes=[
+            pltpu.VMEM((extent + 2, rows - 2 * NZ, 9 * width), jnp.bfloat16),
+            pltpu.VMEM((table_rows, wide), jnp.bfloat16),
+            pltpu.SemaphoreType.DMA((len(weights),)),
+        ],
+        compiler_params=pltpu.CompilerParams(vmem_limit_bytes=40 * 2**20),
+        cost_estimate=pl.CostEstimate(
+            flops=2 * count * cells * table_rows * wide,
+            transcendentals=0,
+            bytes_accessed=2 * table_rows * wide + count * cells * wide * 6,
+        ),
+        name="conv_blocks",
+    )(*operands)
+
+
+def down_kernel(mine_ref, theirs_ref, slope_ref, weight_ref, out_ref, spread):
+    act = (mine_ref[0] + theirs_ref[0].astype(jnp.float32)).astype(jnp.bfloat16)
+    pre = (act.astype(jnp.float32) * slope_ref[0]).astype(jnp.bfloat16)
+    cells = pre.shape[0]
+    offsets, fine = out_ref.shape[2], out_ref.shape[3]
+    lanes = spread.shape[2]
+    for e in range(offsets):
+        grown = lax.dot_general(
+            pre,
+            weight_ref[e],
+            (((1,), (1,)), ((), ())),
+            preferred_element_type=jnp.float32,
+        )
+        for h in range(fine // lanes):
+            spread[h, e * cells : (e + 1) * cells] = grown[:, h * lanes : (h + 1) * lanes]
+    for p in range(cells):
+        for h in range(fine // lanes):
+            out_ref[0, p, :, h * lanes : (h + 1) * lanes] = spread[
+                h, pl.ds(p, offsets, stride=cells), :
+            ].astype(out_ref.dtype)
+
+
+def down_blocks(mine, theirs, slope, weight):
+    extent, cells, wide = slope.shape
+    offsets, fine, _ = weight.shape
+    return pl.pallas_call(
+        down_kernel,
+        grid=(extent,),
+        in_specs=[
+            pl.BlockSpec((1, cells, wide), lambda i: (i, 0, 0)),
+            pl.BlockSpec((1, cells, wide), lambda i: (i, 0, 0)),
+            pl.BlockSpec((1, cells, wide), lambda i: (i, 0, 0)),
+            pl.BlockSpec((offsets, fine, wide), lambda i: (0, 0, 0)),
+        ],
+        out_specs=pl.BlockSpec((1, cells, offsets, fine), lambda i: (i, 0, 0, 0)),
+        out_shape=jax.ShapeDtypeStruct((extent, cells, offsets, fine), jnp.bfloat16),
+        scratch_shapes=[pltpu.VMEM((fine // 128, offsets * cells, 128), jnp.float32)],
+        compiler_params=pltpu.CompilerParams(vmem_limit_bytes=32 * 2**20),
+        cost_estimate=pl.CostEstimate(
+            flops=2 * extent * cells * wide * offsets * fine,
+            transcendentals=0,
+            bytes_accessed=extent * cells * (wide * 10 + offsets * fine * 2),
+        ),
+        name="down_blocks",
+    )(mine, theirs, slope, weight)
+
+
+def planar_moves(swap):
+    return [(q, swap(q)) for q in range(8)]
+
+
+def two_level_body(grad_out, conv_weight, pre_act, down_weight):
+    width, extent, plane = grad_out.shape
+    taps, _, wide = conv_weight.shape
+    block = plane // 4
+    k = lax.axis_index("chan")
+    q = lax.axis_index(PLANAR)
+    far = [(i, i ^ 2) for i in range(4)]
+    near = [(i, i ^ 1) for i in range(4)]
+    first = planar_moves(lambda d: d ^ (2 if d & 1 == 0 else 4))
+    second = planar_moves(lambda d: d ^ (4 if d & 1 == 0 else 2))
+    up = [(i, i + 1) for i in range(3)]
+    down = [(i + 1, i) for i in range(3)]
+    other = [(0, 1), (1, 0)]
+
+    table = conv_weight.reshape(taps * width, wide)
+    share = taps * width // 8
+    piece = lax.dynamic_slice_in_dim(table, q * share, share, 0)
+    got = lax.ppermute(piece, "chan", far)
+    got_a = lax.ppermute(got, PLANAR, first)
+    got_b = lax.ppermute(got, PLANAR, second)
+    got_c = lax.ppermute(got_a, PLANAR, second)
+    mine = [got, got_a, got_b, got_c]
+    far_weights = mine + [lax.ppermute(v, "pair", other) for v in mine]
+
+    cells = jnp.pad(jnp.transpose(grad_out, (1, 2, 0)), ((0, 0), (NZ, NZ), (0, 0)))
+
+    def window(which):
+        return lax.dynamic_slice_in_dim(cells, which * block, block + 2 * NZ, 1)[None]
+
+    def margins(part):
+        low = lax.ppermute(part[:, extent - 1 :], SLAB, up)
+        high = lax.ppermute(part[:, :1], SLAB, down)
+        return low, high
+
+    own = jnp.concatenate([window(k ^ 1), window(k)], 0)
+    own_low, own_high = margins(own)
+    far_one = lax.ppermute(window(k ^ 3), "chan", far)
+    far_two = lax.ppermute(window(k ^ 2), "chan", far)
+    one_low, one_high = margins(far_one)
+    two_low, two_high = margins(far_two)
+
+    slope = gelu_slope(pre_act.astype(jnp.float32))
+
+    where = jnp.reshape(q, (1,)).astype(jnp.int32)
+    begun = conv_blocks(where, own, own_low, own_high, [table], None, 0, jnp.float32)
+    sent = conv_blocks(
+        where, far_one, one_low, one_high, far_weights, begun, 0, jnp.bfloat16
+    )
+    theirs = lax.ppermute(sent, "chan", near)
+    kept = conv_blocks(where, far_two, two_low, two_high, far_weights, begun, 1, jnp.float32)
+    shape = (extent, block, wide)
+    return down_blocks(kept.reshape(shape), theirs.reshape(shape), slope, down_weight)
+
+
 def solution(mesh):
-    in_specs = (
-        P("chan", ("groups", "space", "pair"), None),
-        P(None, "chan", None),
-        P(("groups", "space", "pair"), "chan", None),
-        P(),
-    )
-    out_specs = P(("groups", "space", "pair"), "chan", None, None)
-    return jax.shard_map(body, mesh=mesh, in_specs=in_specs, out_specs=out_specs, check_vma=False)
+    sizes = dict(mesh.shape)
+    four = sizes["chan"] == 4 and all(sizes[axis] == 2 for axis in PLANAR)
+
+    def run(grad_out, conv_weight, pre_act, down_weight):
+        split = grad_out.shape[0] // sizes["chan"]
+        body = two_level_body if four and split == 128 else general_body
+        in_specs = (
+            P("chan", ("groups", "space", "pair"), None),
+            P(None, "chan", None),
+            P(("groups", "space", "pair"), "chan", None),
+            P(),
+        )
+        out_specs = P(("groups", "space", "pair"), "chan", None, None)
+        return jax.shard_map(
+            body, mesh=mesh, in_specs=in_specs, out_specs=out_specs, check_vma=False
+        )(grad_out, conv_weight, pre_act, down_weight)
+
+    return run

time: 204 us -> 110 us (0.54)
  waiting for transfers between devices: 85.8 us -> 40.7 us
  Pallas kernels: 0 us -> 33.6 us
  blocking collectives: 29.8 us -> 0 us
  matrix products: 22.4 us -> 0 us
  local copies, waits for them, and re-layouts: 32.2 us -> 10.2 us
  starting transfers between devices: 3.67 us -> 23.5 us
  other arithmetic: 16.5 us -> 1.6 us
  between operations: 13.7 us -> 0.23 us
    unnamed x2 -> x0, waiting for transfers between devices: 81.7 us -> none
    ppermute x2 -> x17, waiting for transfers between devices: 4.17 us -> 40.7 us  [the longest x1 19.6 us: two_level_body(): got = lax.ppermute(piece, 'chan', far)]
    pallas_call x0 -> x4, Pallas kernels: none -> 33.6 us  [the longest x3 23.6 us: conv_blocks(): pl.pallas_call(functools.partial(conv_kernel, pieces=len(weights), added=...]
    all_to_all x1 -> x0, blocking collectives: 29.8 us -> none  [body(): lax.all_to_all(owned, 'chan', split_axis=1, concat_axis=2, tiled=True)]
    dot_general x2 -> x0, matrix products: 22.4 us -> none  [the longest x1 17 us: body(): lax.dot_general(stacked, conv_weight, (((0, 1), (0, 1)), ((), ())), prefe...]
    ppermute x2 -> x17, starting transfers between devices: 3.66 us -> 23.5 us  [the longest x3 4.49 us: margins(): low = lax.ppermute(part[:, extent - 1:], SLAB, up)]
    unnamed x10, local copies, waits for them, and re-layouts: 19.1 us -> 4.21 us
    unnamed x26 -> x0, other arithmetic: 14.2 us -> none
  transfers between devices with their start and end apart: 3 -> 17, of which waited for: 2 -> 6; matrix products, arithmetic and copies ran while one was open for 0% -> 6% of each run, Pallas kernels for 0% -> 21%
where the time goes in v2:
time: 110 us
  waiting for transfers between devices  40.7 us (37%)
  Pallas kernels  33.6 us (31%)
  starting transfers between devices  23.5 us (21%)
  local copies, waits for them, and re-layouts  10.2 us (9%)
  other arithmetic  1.6 us (1%)
    pallas_call x3, Pallas kernels, conv_blocks(): pl.pallas_call(functools.partial(conv_kernel, pieces=len(weights), added=...  23.6 us
    ppermute x1, waiting for transfers between devices, two_level_body(): got = lax.ppermute(piece, 'chan', far)  19.6 us
    pallas_call x1, Pallas kernels, down_blocks(): pl.pallas_call(down_kernel, grid=(extent,), in_specs=[pl.BlockSpec((1, ce...  10.1 us
    ppermute x1, waiting for transfers between devices, two_level_body(): theirs = lax.ppermute(sent, 'chan', near)  5.94 us
    ppermute x1, waiting for transfers between devices, two_level_body(): far_two = lax.ppermute(window(k ^ 2), 'chan', far)  5.77 us
    ppermute x1, waiting for transfers between devices, two_level_body(): far_one = lax.ppermute(window(k ^ 3), 'chan', far)  4.99 us
    dynamic_slice x5, local copies, waits for them, and re-layouts, window(): lax.dynamic_slice_in_dim(cells, which * block, block + 2 * NZ, 1)[None]  4.93 us
    ppermute x3, starting transfers between devices, margins(): low = lax.ppermute(part[:, extent - 1:], SLAB, up)  4.49 us
  transfers between devices with their start and end apart: 17, of which 6 were waited for; matrix products, arithmetic and copies ran while one was open for 6% of the time, Pallas kernels for 21%

profile of v2, /device:TPU:0, one launch (start us, length us, event | category | flops | bytes accessed | tf_op | source)
XLA Modules:
  0.0 109.9 jit_solution(12383616586843320722)
XLA Ops:
  1.0 4.1 %collective-permute-start.3 = (bf16[432,512]{1,0:T(8,128)(2,1)S(1)}, bf16[432,512]{1,0:T(8,128)(2,1)S(1)}, u32[]{:S(2)}, u32[]{:S(2)}) collective-permute-start(bf16[432,512]{1,0:T(8,128)(2,1)S(1)} %constant_dynamic-slice_fusion), channel_id=1, source_target_pairs={{0,8},{4,12},{8,0},{12,4},{1,9},{5,13},{9,1},{13,5},{2,10},{6,14},... | collective-permute-start | bytes 1327112 | tf_op jit(solution)/shard_map/ppermute | solution.py:241
  5.1 19.6 %collective-permute-done.3.refs_0_ = bf16[432,512]{1,0:T(8,128)(2,1)S(1)} collective-permute-done((bf16[432,512]{1,0:T(8,128)(2,1)S(1)}, bf16[432,512]{1,0:T(8,128)(2,1)S(1)}, u32[]{:S(2)}, u32[]{:S(2)}) %collective-permute-start.3) | collective-permute-done | bytes 442400 | tf_op jit(solution)/shard_map/ppermute | solution.py:241
  24.8 1.5 %collective-permute-start.4 = (bf16[432,512]{1,0:T(8,128)(2,1)S(1)}, bf16[432,512]{1,0:T(8,128)(2,1)S(1)}, u32[]{:S(2)}, u32[]{:S(2)}) collective-permute-start(bf16[432,512]{1,0:T(8,128)(2,1)S(1)} %collective-permute-done.3.refs_0_), channel_id=1, source_target_pairs={{0,2},{1,17},{2,0},{3,19},{16,18},{17,1},{18,16},{19,3},{4,6},{5,2... | collective-permute-start | bytes 1327112 | tf_op jit(solution)/shard_map/ppermute | solution.py:242
  26.3 3.1 %pad_dynamic-slice_fusion = (bf16[4,272,128]{1,0,2:T(4,128)(2,1)S(1)}, bf16[4,272,128]{1,0,2:T(4,128)(2,1)S(1)}, bf16[4,272,128]{1,0,2:T(4,128)(2,1)S(1)}, bf16[4,272,128]{1,0,2:T(4,128)(2,1)S(1)}) fusion(s32[]{:T(128)S(6)} %select_n.19, bf16[4,1024,128]{1,0,2:T(4,128)(2,1)} %bitcast.17, s32[]{:T(128)S(6)} %select_n.17, s32[]{:T(128)S(6)} %select_n.18, ...), kind=kLoop, calls=%fused_computation.15 | loop fusion | bytes 2162704 | tf_op jit(solution)/shard_map/dynamic_slice | solution.py:251
  31.0 1.6 %collective-permute-start.5 = (bf16[432,512]{1,0:T(8,128)(2,1)S(1)}, bf16[432,512]{1,0:T(8,128)(2,1)S(1)}, u32[]{:S(2)}, u32[]{:S(2)}) collective-permute-start(bf16[432,512]{1,0:T(8,128)(2,1)S(1)} %collective-permute-done.3.refs_0_), channel_id=1, source_target_pairs={{0,16},{1,3},{2,18},{3,1},{16,0},{17,19},{18,2},{19,17},{4,20},{5,... | collective-permute-start | bytes 1327112 | tf_op jit(solution)/shard_map/ppermute | solution.py:243
  33.8 2.4 %collective-permute-start.6 = (bf16[432,512]{1,0:T(8,128)(2,1)S(1)}, bf16[432,512]{1,0:T(8,128)(2,1)S(1)}, u32[]{:S(2)}, u32[]{:S(2)}) collective-permute-start(bf16[432,512]{1,0:T(8,128)(2,1)S(1)} %collective-permute-done.4.refs_1_), channel_id=1, source_target_pairs={{0,16},{1,3},{2,18},{3,1},{16,0},{17,19},{18,2},{19,17},{4,20},{5,... | collective-permute-start | bytes 1327112 | tf_op jit(solution)/shard_map/ppermute | solution.py:244
  36.9 1.3 %collective-permute-start.11 = (bf16[2,1,272,128]{3,2,1,0:T(8,128)(2,1)}, bf16[2,1,272,128]{3,2,1,0:T(8,128)(2,1)S(1)}, u32[]{:S(2)}, u32[]{:S(2)}) collective-permute-start(bf16[2,1,272,128]{3,2,1,0:T(8,128)(2,1)} %get-tuple-element.10), channel_id=1, source_target_pairs={{0,1},{1,2},{2,3},{4,5},{5,6},{6,7},{8,9},{9,10},{10,11},{12,13},{... | collective-permute-start | bytes 417800 | tf_op jit(solution)/shard_map/ppermute | solution.py:254
  38.2 1.3 %collective-permute-start.12 = (bf16[2,1,272,128]{3,2,1,0:T(8,128)(2,1)}, bf16[2,1,272,128]{3,2,1,0:T(8,128)(2,1)S(1)}, u32[]{:S(2)}, u32[]{:S(2)}) collective-permute-start(bf16[2,1,272,128]{3,2,1,0:T(8,128)(2,1)} %get-tuple-element.9), channel_id=1, source_target_pairs={{1,0},{2,1},{3,2},{5,4},{6,5},{7,6},{9,8},{10,9},{11,10},{13,12},{... | collective-permute-start | bytes 417800 | tf_op jit(solution)/shard_map/ppermute | solution.py:255
  39.8 5.0 %collective-permute-done.13.main_ref = bf16[1,4,272,128]{3,2,1,0:T(8,128)(2,1)S(1)} collective-permute-done((bf16[1,4,272,128]{3,2,1,0:T(8,128)(2,1)}, bf16[1,4,272,128]{3,2,1,0:T(8,128)(2,1)S(1)}, u32[]{:S(2)}, u32[]{:S(2)}) %collective-permute-start.13) | collective-permute-done | bytes 278560 | tf_op jit(solution)/shard_map/ppermute | solution.py:260
  44.8 1.3 %collective-permute-start.14 = (bf16[1,1,272,128]{3,2,1,0:T(8,128)(2,1)S(1)}, bf16[1,1,272,128]{3,2,1,0:T(8,128)(2,1)S(1)}, u32[]{:S(2)}, u32[]{:S(2)}) collective-permute-start(bf16[1,1,272,128]{3,2,1,0:T(8,128)(2,1)S(1)} %get-tuple-element.12), channel_id=1, source_target_pairs={{0,1},{1,2},{2,3},{4,5},{5,6},{6,7},{8,9},{9,10},{10,11},{12,13},{... | collective-permute-start | bytes 208904 | tf_op jit(solution)/shard_map/ppermute | solution.py:254
  46.1 1.3 %collective-permute-start.15 = (bf16[1,1,272,128]{3,2,1,0:T(8,128)(2,1)S(1)}, bf16[1,1,272,128]{3,2,1,0:T(8,128)(2,1)S(1)}, u32[]{:S(2)}, u32[]{:S(2)}) collective-permute-start(bf16[1,1,272,128]{3,2,1,0:T(8,128)(2,1)S(1)} %get-tuple-element.11), channel_id=1, source_target_pairs={{1,0},{2,1},{3,2},{5,4},{6,5},{7,6},{9,8},{10,9},{11,10},{13,12},{... | collective-permute-start | bytes 208904 | tf_op jit(solution)/shard_map/ppermute | solution.py:255
  47.5 2.9 %collective-permute-start.7 = (bf16[432,512]{1,0:T(8,128)(2,1)S(1)}, bf16[432,512]{1,0:T(8,128)(2,1)S(1)}, u32[]{:S(2)}, u32[]{:S(2)}) collective-permute-start(bf16[432,512]{1,0:T(8,128)(2,1)S(1)} %collective-permute-done.3.refs_0_), channel_id=1, source_target_pairs={{0,1},{1,0},{2,3},{3,2},{4,5},{5,4},{6,7},{7,6},{8,9},{9,8},{10,11... | collective-permute-start | bytes 1327112 | tf_op jit(solution)/shard_map/ppermute | solution.py:246
  51.0 2.0 %copy-done.1 = bf16[27,128,512]{2,1,0:T(8,128)(2,1)S(1)} copy-done((bf16[27,128,512]{2,1,0:T(8,128)(2,1)S(1)}, bf16[27,128,512]{2,1,0:T(8,128)(2,1)}, u32[]{:S(2)}) %copy-start.1) | copy-done | bytes 3538968
  53.0 9.9 %conv_blocks.3.refs_8_ = f32[2,1024,512]{2,1,0:T(8,128)S(1)} custom-call(s32[1]{0:T(128)} %bitcast.where_ref, bf16[2,4,272,128]{3,2,1,0:T(8,128)(2,1)S(1)} %pad_maximum_fusion.main_ref, bf16[2,1,272,128]{3,2,1,0:T(8,128)(2,1)S(1)} %collective-permute-done.11.low_ref, bf16[2,1,272,128]{3,2,1,0:T(8,128)(2,1)S(1)} %collective-permute-done.12.high_ref, ...), custom_call_target="tpu_custom_call" | custom-call | flops 7247757312 | bytes 9830400 | tf_op jit(solution)/shard_map/conv_blocks/pallas_call | solution.py:152
  63.0 6.9 %conv_blocks.5 = bf16[1,1024,512]{2,1,0:T(8,128)(2,1)S(1)} custom-call(s32[1]{0:T(128)} %bitcast.where_ref, bf16[1,4,272,128]{3,2,1,0:T(8,128)(2,1)S(1)} %collective-permute-done.13.main_ref, bf16[1,1,272,128]{3,2,1,0:T(8,128)(2,1)S(1)} %collective-permute-done.14.low_ref, bf16[1,1,272,128]{3,2,1,0:T(8,128)(2,1)S(1)} %collective-permute-done.15.high_ref, ...), custom_call_target="tpu_custom_call" | custom-call | flops 3623878656 | bytes 6684672 | tf_op jit(solution)/shard_map/conv_blocks/pallas_call | solution.py:152
  69.9 1.8 %collective-permute-start.16 = (bf16[1,1024,512]{2,1,0:T(8,128)(2,1)S(1)}, bf16[1,1024,512]{2,1,0:T(8,128)(2,1)S(1)}, u32[]{:S(2)}, u32[]{:S(2)}) collective-permute-start(bf16[1,1024,512]{2,1,0:T(8,128)(2,1)S(1)} %conv_blocks.5), channel_id=1, source_target_pairs={{0,4},{4,0},{8,12},{12,8},{1,5},{5,1},{9,13},{13,9},{2,6},{6,2},{1... | collective-permute-start | bytes 3145736 | tf_op jit(solution)/shard_map/ppermute | solution.py:272
  71.7 5.8 %collective-permute-done.main_ref = bf16[1,4,272,128]{3,2,1,0:T(8,128)(2,1)S(1)} collective-permute-done((bf16[1,4,272,128]{3,2,1,0:T(8,128)(2,1)S(1)}, bf16[1,4,272,128]{3,2,1,0:T(8,128)(2,1)S(1)}, u32[]{:S(2)}, u32[]{:S(2)}) %collective-permute-start) | collective-permute-done | bytes 278560 | tf_op jit(solution)/shard_map/ppermute | solution.py:261
  77.5 1.9 %collective-permute-start.1 = (bf16[1,1,272,128]{3,2,1,0:T(8,128)(2,1)S(1)}, bf16[1,1,272,128]{3,2,1,0:T(8,128)(2,1)S(1)}, u32[]{:S(2)}, u32[]{:S(2)}) collective-permute-start(bf16[1,1,272,128]{3,2,1,0:T(8,128)(2,1)S(1)} %get-tuple-element.14), channel_id=1, source_target_pairs={{0,1},{1,2},{2,3},{4,5},{5,6},{6,7},{8,9},{9,10},{10,11},{12,13},{... | collective-permute-start | bytes 208904 | tf_op jit(solution)/shard_map/ppermute | solution.py:254
  79.4 1.5 %collective-permute-start.2 = (bf16[1,1,272,128]{3,2,1,0:T(8,128)(2,1)S(1)}, bf16[1,1,272,128]{3,2,1,0:T(8,128)(2,1)S(1)}, u32[]{:S(2)}, u32[]{:S(2)}) collective-permute-start(bf16[1,1,272,128]{3,2,1,0:T(8,128)(2,1)S(1)} %get-tuple-element.13), channel_id=1, source_target_pairs={{1,0},{2,1},{3,2},{5,4},{6,5},{7,6},{9,8},{10,9},{11,10},{13,12},{... | collective-permute-start | bytes 208904 | tf_op jit(solution)/shard_map/ppermute | solution.py:255
  81.7 3.1 %collective-permute-done.2.high_ref = bf16[1,1,272,128]{3,2,1,0:T(8,128)(2,1)S(1)} collective-permute-done((bf16[1,1,272,128]{3,2,1,0:T(8,128)(2,1)S(1)}, bf16[1,1,272,128]{3,2,1,0:T(8,128)(2,1)S(1)}, u32[]{:S(2)}, u32[]{:S(2)}) %collective-permute-start.2) | collective-permute-done | bytes 69664 | tf_op jit(solution)/shard_map/ppermute | solution.py:255
  84.8 2.2 %copy-done.3 = f32[2,1024,512]{2,1,0:T(8,128)S(1)} copy-done((f32[2,1024,512]{2,1,0:T(8,128)S(1)}, f32[2,1024,512]{2,1,0:T(8,128)}, u32[]{:S(2)}) %copy-start.3) | copy-done | bytes 4194328
  87.0 6.9 %conv_blocks.4 = f32[1,1024,512]{2,1,0:T(8,128)S(1)} custom-call(s32[1]{0:T(128)} %bitcast.where_ref, bf16[1,4,272,128]{3,2,1,0:T(8,128)(2,1)S(1)} %collective-permute-done.main_ref, bf16[1,1,272,128]{3,2,1,0:T(8,128)(2,1)S(1)} %collective-permute-done.1.low_ref, bf16[1,1,272,128]{3,2,1,0:T(8,128)(2,1)S(1)} %collective-permute-done.2.high_ref, ...), custom_call_target="tpu_custom_call" | custom-call | flops 3623878656 | bytes 6684672 | tf_op jit(solution)/shard_map/conv_blocks/pallas_call | solution.py:152
  93.9 5.9 %collective-permute-done.16 = bf16[1,1024,512]{2,1,0:T(8,128)(2,1)S(1)} collective-permute-done((bf16[1,1024,512]{2,1,0:T(8,128)(2,1)S(1)}, bf16[1,1024,512]{2,1,0:T(8,128)(2,1)S(1)}, u32[]{:S(2)}, u32[]{:S(2)}) %collective-permute-start.16) | collective-permute-done | bytes 1048608 | tf_op jit(solution)/shard_map/ppermute | solution.py:272
  99.8 10.1 %down_blocks.1 = bf16[4,256,8,256]{3,2,1,0:T(8,128)(2,1)} custom-call(f32[4,256,512]{2,1,0:T(8,128)S(1)} %bitcast.9, bf16[4,256,512]{2,1,0:T(8,128)(2,1)S(1)} %bitcast.10, f32[4,256,512]{2,1,0:T(8,128)S(1)} %fusion.3.slope_ref, bf16[8,256,512]{2,1,0:T(8,128)(2,1)S(1)} %copy-done), custom_call_target="tpu_custom_call" | custom-call | flops 2147483648 | bytes 9437184 | tf_op jit(solution)/shard_map/down_blocks/pallas_call | solution.py:198
  (35 shorter events, 6.4 us)
Async XLA Ops:
  1.0 23.7 %collective-permute-start.3 = (bf16[432,512]{1,0:T(8,128)(2,1)S(1)}, bf16[432,512]{1,0:T(8,128)(2,1)S(1)}, u32[]{:S(2)}, u32[]{:S(2)}) collective-permute-start(bf16[432,512]{1,0:T(8,128)(2,1)S(1)} %constant_dynamic-slice_fusion), channel_id=1, source_target_pairs={{0,8},{4,12},{8,0},{12,4},{1,9},{5,13},{9,1},{13,5},{2,10},{6,14},... | collective-permute-start | bytes 1327112 | tf_op jit(solution)/shard_map/ppermute | solution.py:241
  24.8 9.0 %collective-permute-start.4 = (bf16[432,512]{1,0:T(8,128)(2,1)S(1)}, bf16[432,512]{1,0:T(8,128)(2,1)S(1)}, u32[]{:S(2)}, u32[]{:S(2)}) collective-permute-start(bf16[432,512]{1,0:T(8,128)(2,1)S(1)} %collective-permute-done.3.refs_0_), channel_id=1, source_target_pairs={{0,2},{1,17},{2,0},{3,19},{16,18},{17,1},{18,16},{19,3},{4,6},{5,2... | collective-permute-start | bytes 1327112 | tf_op jit(solution)/shard_map/ppermute | solution.py:242
  30.4 14.4 %collective-permute-start.13 = (bf16[1,4,272,128]{3,2,1,0:T(8,128)(2,1)}, bf16[1,4,272,128]{3,2,1,0:T(8,128)(2,1)S(1)}, u32[]{:S(2)}, u32[]{:S(2)}) collective-permute-start(bf16[1,4,272,128]{3,2,1,0:T(8,128)(2,1)} %bitcast.7), channel_id=1, source_target_pairs={{0,8},{4,12},{8,0},{12,4},{1,9},{5,13},{9,1},{13,5},{2,10},{6,14},... | collective-permute-start | bytes 835592 | tf_op jit(solution)/shard_map/ppermute | solution.py:260
  31.0 19.5 %collective-permute-start.5 = (bf16[432,512]{1,0:T(8,128)(2,1)S(1)}, bf16[432,512]{1,0:T(8,128)(2,1)S(1)}, u32[]{:S(2)}, u32[]{:S(2)}) collective-permute-start(bf16[432,512]{1,0:T(8,128)(2,1)S(1)} %collective-permute-done.3.refs_0_), channel_id=1, source_target_pairs={{0,16},{1,3},{2,18},{3,1},{16,0},{17,19},{18,2},{19,17},{4,20},{5,... | collective-permute-start | bytes 1327112 | tf_op jit(solution)/shard_map/ppermute | solution.py:243
  33.8 17.1 %collective-permute-start.6 = (bf16[432,512]{1,0:T(8,128)(2,1)S(1)}, bf16[432,512]{1,0:T(8,128)(2,1)S(1)}, u32[]{:S(2)}, u32[]{:S(2)}) collective-permute-start(bf16[432,512]{1,0:T(8,128)(2,1)S(1)} %collective-permute-done.4.refs_1_), channel_id=1, source_target_pairs={{0,16},{1,3},{2,18},{3,1},{16,0},{17,19},{18,2},{19,17},{4,20},{5,... | collective-permute-start | bytes 1327112 | tf_op jit(solution)/shard_map/ppermute | solution.py:244
  36.9 9.3 %collective-permute-start.11 = (bf16[2,1,272,128]{3,2,1,0:T(8,128)(2,1)}, bf16[2,1,272,128]{3,2,1,0:T(8,128)(2,1)S(1)}, u32[]{:S(2)}, u32[]{:S(2)}) collective-permute-start(bf16[2,1,272,128]{3,2,1,0:T(8,128)(2,1)} %get-tuple-element.10), channel_id=1, source_target_pairs={{0,1},{1,2},{2,3},{4,5},{5,6},{6,7},{8,9},{9,10},{10,11},{12,13},{... | collective-permute-start | bytes 417800 | tf_op jit(solution)/shard_map/ppermute | solution.py:254
  38.2 9.3 %collective-permute-start.12 = (bf16[2,1,272,128]{3,2,1,0:T(8,128)(2,1)}, bf16[2,1,272,128]{3,2,1,0:T(8,128)(2,1)S(1)}, u32[]{:S(2)}, u32[]{:S(2)}) collective-permute-start(bf16[2,1,272,128]{3,2,1,0:T(8,128)(2,1)} %get-tuple-element.9), channel_id=1, source_target_pairs={{1,0},{2,1},{3,2},{5,4},{6,5},{7,6},{9,8},{10,9},{11,10},{13,12},{... | collective-permute-start | bytes 417800 | tf_op jit(solution)/shard_map/ppermute | solution.py:255
  44.8 5.6 %collective-permute-start.14 = (bf16[1,1,272,128]{3,2,1,0:T(8,128)(2,1)S(1)}, bf16[1,1,272,128]{3,2,1,0:T(8,128)(2,1)S(1)}, u32[]{:S(2)}, u32[]{:S(2)}) collective-permute-start(bf16[1,1,272,128]{3,2,1,0:T(8,128)(2,1)S(1)} %get-tuple-element.12), channel_id=1, source_target_pairs={{0,1},{1,2},{2,3},{4,5},{5,6},{6,7},{8,9},{9,10},{10,11},{12,13},{... | collective-permute-start | bytes 208904 | tf_op jit(solution)/shard_map/ppermute | solution.py:254
  46.1 16.7 %collective-permute-start.15 = (bf16[1,1,272,128]{3,2,1,0:T(8,128)(2,1)S(1)}, bf16[1,1,272,128]{3,2,1,0:T(8,128)(2,1)S(1)}, u32[]{:S(2)}, u32[]{:S(2)}) collective-permute-start(bf16[1,1,272,128]{3,2,1,0:T(8,128)(2,1)S(1)} %get-tuple-element.11), channel_id=1, source_target_pairs={{1,0},{2,1},{3,2},{5,4},{6,5},{7,6},{9,8},{10,9},{11,10},{13,12},{... | collective-permute-start | bytes 208904 | tf_op jit(solution)/shard_map/ppermute | solution.py:255
  47.5 15.5 %collective-permute-start.7 = (bf16[432,512]{1,0:T(8,128)(2,1)S(1)}, bf16[432,512]{1,0:T(8,128)(2,1)S(1)}, u32[]{:S(2)}, u32[]{:S(2)}) collective-permute-start(bf16[432,512]{1,0:T(8,128)(2,1)S(1)} %collective-permute-done.3.refs_0_), channel_id=1, source_target_pairs={{0,1},{1,0},{2,3},{3,2},{4,5},{5,4},{6,7},{7,6},{8,9},{9,8},{10,11... | collective-permute-start | bytes 1327112 | tf_op jit(solution)/shard_map/ppermute | solution.py:246
  50.4 12.6 %collective-permute-start.8 = (bf16[432,512]{1,0:T(8,128)(2,1)S(1)}, bf16[432,512]{1,0:T(8,128)(2,1)S(1)}, u32[]{:S(2)}, u32[]{:S(2)}) collective-permute-start(bf16[432,512]{1,0:T(8,128)(2,1)S(1)} %collective-permute-done.4.refs_1_), channel_id=1, source_target_pairs={{0,1},{1,0},{2,3},{3,2},{4,5},{5,4},{6,7},{7,6},{8,9},{9,8},{10,11... | collective-permute-start | bytes 1327112 | tf_op jit(solution)/shard_map/ppermute | solution.py:246
  50.5 12.5 %collective-permute-start.9 = (bf16[432,512]{1,0:T(8,128)(2,1)S(1)}, bf16[432,512]{1,0:T(8,128)(2,1)S(1)}, u32[]{:S(2)}, u32[]{:S(2)}) collective-permute-start(bf16[432,512]{1,0:T(8,128)(2,1)S(1)} %collective-permute-done.5.refs_2_), channel_id=1, source_target_pairs={{0,1},{1,0},{2,3},{3,2},{4,5},{5,4},{6,7},{7,6},{8,9},{9,8},{10,11... | collective-permute-start | bytes 1327112 | tf_op jit(solution)/shard_map/ppermute | solution.py:246
  50.9 12.1 %collective-permute-start.10 = (bf16[432,512]{1,0:T(8,128)(2,1)S(1)}, bf16[432,512]{1,0:T(8,128)(2,1)S(1)}, u32[]{:S(2)}, u32[]{:S(2)}) collective-permute-start(bf16[432,512]{1,0:T(8,128)(2,1)S(1)} %collective-permute-done.6.refs_3_), channel_id=1, source_target_pairs={{0,1},{1,0},{2,3},{3,2},{4,5},{5,4},{6,7},{7,6},{8,9},{9,8},{10,11... | collective-permute-start | bytes 1327112 | tf_op jit(solution)/shard_map/ppermute | solution.py:246
  51.0 2.0 %copy-start.1 = (bf16[27,128,512]{2,1,0:T(8,128)(2,1)S(1)}, bf16[27,128,512]{2,1,0:T(8,128)(2,1)}, u32[]{:S(2)}) copy-start(bf16[27,128,512]{2,1,0:T(8,128)(2,1)} %param.5) | copy-start | bytes 10616836
  62.8 7.0 %copy-start.2 = (f32[2,1024,512]{2,1,0:T(8,128)}, f32[2,1024,512]{2,1,0:T(8,128)S(1)}, u32[]{:S(2)}) copy-start(f32[2,1024,512]{2,1,0:T(8,128)S(1)} %conv_blocks.3.refs_8_) | copy-start | bytes 12582916
  62.9 18.0 %copy-start.4 = (bf16[4,256,512]{2,1,0:T(8,128)(2,1)S(1)}, bf16[4,256,512]{2,1,0:T(8,128)(2,1)}, u32[]{:S(2)}) copy-start(bf16[4,256,512]{2,1,0:T(8,128)(2,1)} %param.6) | copy-start | bytes 3145732
  62.9 14.6 %collective-permute-start = (bf16[1,4,272,128]{3,2,1,0:T(8,128)(2,1)S(1)}, bf16[1,4,272,128]{3,2,1,0:T(8,128)(2,1)S(1)}, u32[]{:S(2)}, u32[]{:S(2)}) collective-permute-start(bf16[1,4,272,128]{3,2,1,0:T(8,128)(2,1)S(1)} %bitcast.18), channel_id=1, source_target_pairs={{0,8},{4,12},{8,0},{12,4},{1,9},{5,13},{9,1},{13,5},{2,10},{6,14},... | collective-permute-start | bytes 835592 | tf_op jit(solution)/shard_map/ppermute | solution.py:261
  69.9 29.9 %collective-permute-start.16 = (bf16[1,1024,512]{2,1,0:T(8,128)(2,1)S(1)}, bf16[1,1024,512]{2,1,0:T(8,128)(2,1)S(1)}, u32[]{:S(2)}, u32[]{:S(2)}) collective-permute-start(bf16[1,1024,512]{2,1,0:T(8,128)(2,1)S(1)} %conv_blocks.5), channel_id=1, source_target_pairs={{0,4},{4,0},{8,12},{12,8},{1,5},{5,1},{9,13},{13,9},{2,6},{6,2},{1... | collective-permute-start | bytes 3145736 | tf_op jit(solution)/shard_map/ppermute | solution.py:272
  77.5 4.3 %collective-permute-start.1 = (bf16[1,1,272,128]{3,2,1,0:T(8,128)(2,1)S(1)}, bf16[1,1,272,128]{3,2,1,0:T(8,128)(2,1)S(1)}, u32[]{:S(2)}, u32[]{:S(2)}) collective-permute-start(bf16[1,1,272,128]{3,2,1,0:T(8,128)(2,1)S(1)} %get-tuple-element.14), channel_id=1, source_target_pairs={{0,1},{1,2},{2,3},{4,5},{5,6},{6,7},{8,9},{9,10},{10,11},{12,13},{... | collective-permute-start | bytes 208904 | tf_op jit(solution)/shard_map/ppermute | solution.py:254
  79.4 5.4 %collective-permute-start.2 = (bf16[1,1,272,128]{3,2,1,0:T(8,128)(2,1)S(1)}, bf16[1,1,272,128]{3,2,1,0:T(8,128)(2,1)S(1)}, u32[]{:S(2)}, u32[]{:S(2)}) collective-permute-start(bf16[1,1,272,128]{3,2,1,0:T(8,128)(2,1)S(1)} %get-tuple-element.13), channel_id=1, source_target_pairs={{1,0},{2,1},{3,2},{5,4},{6,5},{7,6},{9,8},{10,9},{11,10},{13,12},{... | collective-permute-start | bytes 208904 | tf_op jit(solution)/shard_map/ppermute | solution.py:255
  81.7 18.1 %copy-start = (bf16[8,256,512]{2,1,0:T(8,128)(2,1)S(1)}, bf16[8,256,512]{2,1,0:T(8,128)(2,1)}, u32[]{:S(2)}) copy-start(bf16[8,256,512]{2,1,0:T(8,128)(2,1)} %weight_ref.1) | copy-start | bytes 6291460
  84.8 2.2 %copy-start.3 = (f32[2,1024,512]{2,1,0:T(8,128)S(1)}, f32[2,1024,512]{2,1,0:T(8,128)}, u32[]{:S(2)}) copy-start(f32[2,1024,512]{2,1,0:T(8,128)} %copy-done.2) | copy-start | bytes 12582916

commit v3 on v0

--- a/solution.py
+++ b/solution.py
@@ -1,11 +1,23 @@
+import functools
 import math
 
 import jax
 import jax.numpy as jnp
 from jax import lax
+from jax.experimental import pallas as pl
+from jax.experimental.pallas import tpu as pltpu
 from jax.sharding import PartitionSpec as P
 
 NZ = 8
+PLANAR = ("groups", "space", "pair")
+SLAB = ("space", "pair")
+COST = (4 * 10**9, 4 * 10**9, 8 * 10**9)
+
+
+def gelu_slope(values):
+    return 0.5 * (1.0 + jax.scipy.special.erf(values / math.sqrt(2.0))) + values * jnp.exp(
+        -0.5 * values * values
+    ) / math.sqrt(2.0 * math.pi)
 
 
 def with_halo(cells, sides, width):
@@ -42,14 +54,8 @@
     return jnp.stack(pieces)
 
 
-def gelu_slope(values):
-    return 0.5 * (1.0 + jax.scipy.special.erf(values / math.sqrt(2.0))) + values * jnp.exp(
-        -0.5 * values * values
-    ) / math.sqrt(2.0 * math.pi)
-
-
-def body(grad_out, conv_weight, pre_act, down_weight):
-    padded = with_halo(grad_out, ((("space", "pair"), 1),), 1)
+def general_body(grad_out, conv_weight, pre_act, down_weight):
+    padded = with_halo(grad_out, ((SLAB, 1),), 1)
     stacked = shifted_stack(padded, NZ)
     partial_sum = lax.dot_general(
         stacked, conv_weight, (((0, 1), (0, 1)), ((), ())), preferred_element_type=jnp.float32
@@ -66,12 +72,241 @@
     return result.astype(jnp.bfloat16)
 
 
+def piece_order(q):
+    first = 2 + 2 * (q & 1)
+    second = 6 - first
+    return [q, q ^ first, q ^ second, q ^ 6, q ^ 1, q ^ 1 ^ second, q ^ 1 ^ first, q ^ 7]
+
+
+def conv_kernel(where_ref, *refs, sources, added):
+    refs = list(refs)
+    groups = []
+    for pieces in sources:
+        groups.append((refs[:3], refs[3 : 3 + pieces]))
+        del refs[: 3 + pieces]
+    start_ref = refs.pop(0) if added else None
+    out_ref, copies = refs[:2]
+    tables, sems = refs[2 : 2 + len(sources)], refs[2 + len(sources) :]
+    extent, rows, width = groups[0][0][0].shape
+    cells = rows - 2 * NZ
+
+    loads = []
+    for (_, weights), table, sem in zip(groups, tables, sems):
+        if len(weights) == 1:
+            loads.append([pltpu.make_async_copy(weights[0], table, sem.at[0])])
+            continue
+        order = piece_order(where_ref[0])
+        mine, base = [], 0
+        for n, piece in enumerate(weights):
+            share = piece.shape[0]
+            row = pl.multiple_of(base + order[n % 8] * share, 16)
+            mine.append(
+                pltpu.make_async_copy(piece, table.at[pl.ds(row, share), :], sem.at[n])
+            )
+            if n % 8 == 7:
+                base += 8 * share
+        loads.append(mine)
+    for mine in loads:
+        for load in mine:
+            load.start()
+
+    depth_at = lax.broadcasted_iota(jnp.int32, (rows, width), 0) % NZ
+    total = start_ref[...] if added else None
+    for ((main_ref, low_ref, high_ref), _), table, mine in zip(groups, tables, loads):
+        for x in range(extent + 2):
+            if x == 0:
+                plane = low_ref[...]
+            elif x == extent + 1:
+                plane = high_ref[...]
+            else:
+                plane = main_ref[x - 1]
+            plane = plane.astype(jnp.float32)
+            for step_z in (-1, 0, 1):
+                if step_z == 1:
+                    moved = jnp.where(depth_at >= 1, pltpu.roll(plane, 1, 0), 0.0)
+                elif step_z == -1:
+                    moved = jnp.where(depth_at < NZ - 1, pltpu.roll(plane, rows - 1, 0), 0.0)
+                else:
+                    moved = plane
+                for step_y in (-1, 0, 1):
+                    at = NZ * (1 - step_y)
+                    lane = (3 * (step_y + 1) + step_z + 1) * width
+                    copies[x, :, lane : lane + width] = moved[at : at + cells].astype(
+                        jnp.bfloat16
+                    )
+        for load in mine:
+            load.wait()
+        for step_x in (-1, 0, 1):
+            left = copies[1 - step_x : 1 - step_x + extent].reshape(extent * cells, 9 * width)
+            right = table[(step_x + 1) * 9 * width : (step_x + 2) * 9 * width]
+            term = jnp.dot(left, right, preferred_element_type=jnp.float32)
+            total = term if total is None else total + term
+    out_ref[...] = total.astype(out_ref.dtype)
+
+
+def conv_blocks(where, sources, start, kind, flops):
+    extent, rows, width = sources[0][0].shape
+    wide = sources[0][3][0].shape[1]
+    taps = 27
+    cells = extent * (rows - 2 * NZ)
+    in_specs = [pl.BlockSpec(memory_space=pltpu.SMEM)]
+    operands = [where]
+    for main, low, high, weights in sources:
+        in_specs += [pl.BlockSpec(memory_space=pltpu.VMEM)] * 3
+        in_specs += [pl.BlockSpec(memory_space=pl.ANY)] * len(weights)
+        operands += [main, low, high, *weights]
+    if start is not None:
+        in_specs.append(pl.BlockSpec(memory_space=pltpu.VMEM))
+        operands.append(start)
+    return pl.pallas_call(
+        functools.partial(
+            conv_kernel, sources=[len(v[3]) for v in sources], added=start is not None
+        ),
+        in_specs=in_specs,
+        out_specs=pl.BlockSpec(memory_space=pltpu.VMEM),
+        out_shape=jax.ShapeDtypeStruct((cells, wide), kind),
+        scratch_shapes=[pltpu.VMEM((extent + 2, rows - 2 * NZ, 9 * width), jnp.bfloat16)]
+        + [pltpu.VMEM((taps * width, wide), jnp.bfloat16)] * len(sources)
+        + [pltpu.SemaphoreType.DMA((len(v[3]),)) for v in sources],
+        compiler_params=pltpu.CompilerParams(vmem_limit_bytes=28 * 2**20),
+        cost_estimate=pl.CostEstimate(flops=flops, transcendentals=0, bytes_accessed=flops // 400),
+        name="conv_blocks",
+    )(*operands)
+
+
+def down_kernel(mine_ref, theirs_ref, slope_ref, weight_ref, out_ref):
+    act = (mine_ref[0] + theirs_ref[0].astype(jnp.float32)).astype(jnp.bfloat16)
+    pre = (act.astype(jnp.float32) * slope_ref[0]).astype(jnp.bfloat16)
+    grown = [
+        lax.dot_general(
+            pre,
+            weight_ref[e],
+            (((1,), (1,)), ((), ())),
+            preferred_element_type=jnp.float32,
+        ).astype(out_ref.dtype)
+        for e in range(weight_ref.shape[0])
+    ]
+    out_ref[0] = jnp.swapaxes(jnp.stack(grown), 0, 1)
+
+
+def down_blocks(mine, theirs, slope, weight):
+    extent, cells, wide = slope.shape
+    offsets, fine, _ = weight.shape
+    return pl.pallas_call(
+        down_kernel,
+        grid=(extent,),
+        in_specs=[
+            pl.BlockSpec((1, cells, wide), lambda i: (i, 0, 0)),
+            pl.BlockSpec((1, cells, wide), lambda i: (i, 0, 0)),
+            pl.BlockSpec((1, cells, wide), lambda i: (i, 0, 0)),
+            pl.BlockSpec((offsets, fine, wide), lambda i: (0, 0, 0)),
+        ],
+        out_specs=pl.BlockSpec((1, cells, offsets, fine), lambda i: (i, 0, 0, 0)),
+        out_shape=jax.ShapeDtypeStruct((extent, cells, offsets, fine), jnp.bfloat16),
+        compiler_params=pltpu.CompilerParams(vmem_limit_bytes=20 * 2**20),
+        name="down_blocks",
+    )(mine, theirs, slope, weight)
+
+
+def planar_moves(swap):
+    return [(q, swap(q)) for q in range(8)]
+
+
+def two_level_body(grad_out, conv_weight, pre_act, down_weight):
+    width, extent, plane = grad_out.shape
+    taps, _, wide = conv_weight.shape
+    block = plane // 4
+    k = lax.axis_index("chan")
+    q = lax.axis_index(PLANAR)
+    far = [(i, i ^ 2) for i in range(4)]
+    near = [(i, i ^ 1) for i in range(4)]
+    first = planar_moves(lambda d: d ^ (2 if d & 1 == 0 else 4))
+    second = planar_moves(lambda d: d ^ (4 if d & 1 == 0 else 2))
+    up = [(i, i + 1) for i in range(3)]
+    down = [(i + 1, i) for i in range(3)]
+    other = [(0, 1), (1, 0)]
+
+    def after(value, *others):
+        return lax.optimization_barrier((value, *others))[0]
+
+    def margins(part):
+        low = lax.ppermute(part[:, extent - 1 :], SLAB, up)
+        high = lax.ppermute(part[:, :1], SLAB, down)
+        return low, high
+
+    table = conv_weight.reshape(taps * width, wide)
+    share = taps * width // 8
+    piece = lax.dynamic_slice_in_dim(table, q * share, share, 0)
+    got = lax.ppermute(piece, "chan", far)
+
+    cells = jnp.pad(
+        jnp.transpose(after(grad_out, piece), (1, 2, 0)), ((0, 0), (NZ, NZ), (0, 0))
+    )
+
+    def window(which):
+        return lax.dynamic_slice_in_dim(cells, which * block, block + 2 * NZ, 1)
+
+    where = jnp.reshape(q, (1,)).astype(jnp.int32)
+    own_one, own_two = window(k ^ 1), window(k)
+    own_low, own_high = margins(jnp.stack([own_one, own_two]))
+    begun = conv_blocks(
+        where, [(own_one, own_low[0, 0], own_high[0, 0], [table])], None, jnp.float32, COST[0]
+    )
+    slope = gelu_slope(after(pre_act, piece).astype(jnp.float32))
+    got, window_one, window_two = lax.optimization_barrier(
+        (got, window(k ^ 3), window(k ^ 2), begun, slope)
+    )[:3]
+    far_one = lax.ppermute(window_one, "chan", far)
+    got_a = lax.ppermute(got, PLANAR, first)
+    got_b = lax.ppermute(got, PLANAR, second)
+    got_c = lax.ppermute(got_a, PLANAR, second)
+    got_b = after(got_b, far_one)
+    one_low, one_high = margins(far_one[None])
+    far_two = lax.ppermute(after(window_two, far_one), "chan", far)
+    got_c, one_low, one_high = lax.optimization_barrier((got_c, one_low, one_high))
+    mine = [got, got_a, got_b, got_c]
+    pieces = mine + [lax.ppermute(v, "pair", other) for v in mine]
+
+    sent = conv_blocks(
+        where,
+        [(far_one, one_low[0, 0], one_high[0, 0], pieces)],
+        begun,
+        jnp.bfloat16,
+        COST[1],
+    )
+    theirs = lax.ppermute(sent, "chan", near)
+    far_two = after(far_two, sent)
+    two_low, two_high = margins(far_two[None])
+    kept = conv_blocks(
+        where,
+        [
+            (own_two, own_low[1, 0], own_high[1, 0], [table]),
+            (far_two, two_low[0, 0], two_high[0, 0], pieces),
+        ],
+        None,
+        jnp.float32,
+        COST[2],
+    )
+    shape = (extent, block, wide)
+    return down_blocks(kept.reshape(shape), theirs.reshape(shape), slope, down_weight)
+
+
 def solution(mesh):
-    in_specs = (
-        P("chan", ("groups", "space", "pair"), None),
-        P(None, "chan", None),
-        P(("groups", "space", "pair"), "chan", None),
-        P(),
-    )
-    out_specs = P(("groups", "space", "pair"), "chan", None, None)
-    return jax.shard_map(body, mesh=mesh, in_specs=in_specs, out_specs=out_specs, check_vma=False)
+    sizes = dict(mesh.shape)
+    four = sizes["chan"] == 4 and all(sizes[axis] == 2 for axis in PLANAR)
+
+    def run(grad_out, conv_weight, pre_act, down_weight):
+        split = grad_out.shape[0] // sizes["chan"]
+        body = two_level_body if four and split == 128 else general_body
+        in_specs = (
+            P("chan", ("groups", "space", "pair"), None),
+            P(None, "chan", None),
+            P(("groups", "space", "pair"), "chan", None),
+            P(),
+        )
+        out_specs = P(("groups", "space", "pair"), "chan", None, None)
+        return jax.shard_map(
+            body, mesh=mesh, in_specs=in_specs, out_specs=out_specs, check_vma=False
+        )(grad_out, conv_weight, pre_act, down_weight)
+
+    return run

time: 204 us -> 90.2 us (0.44)
  waiting for transfers between devices: 85.8 us -> 33 us
  blocking collectives: 29.8 us -> 0 us
  local copies, waits for them, and re-layouts: 32.2 us -> 3.21 us
  Pallas kernels: 0 us -> 28.3 us
  matrix products: 22.4 us -> 0 us
  starting transfers between devices: 3.67 us -> 24.4 us
  other arithmetic: 16.5 us -> 0.84 us
  between operations: 13.7 us -> 0.2 us
    unnamed x2 -> x0, waiting for transfers between devices: 81.7 us -> none
    all_to_all x1 -> x0, blocking collectives: 29.8 us -> none  [body(): lax.all_to_all(owned, 'chan', split_axis=1, concat_axis=2, tiled=True)]
    ppermute x2 -> x17, waiting for transfers between devices: 4.17 us -> 33 us  [the longest x1 9.93 us: two_level_body(): got_a = lax.ppermute(got, PLANAR, first)]
    pallas_call x0 -> x4, Pallas kernels: none -> 28.3 us  [the longest x3 23.5 us: conv_blocks(): pl.pallas_call(functools.partial(conv_kernel, sources=[len(v[3]) for v in...]
    dot_general x2 -> x0, matrix products: 22.4 us -> none  [the longest x1 17 us: body(): lax.dot_general(stacked, conv_weight, (((0, 1), (0, 1)), ((), ())), prefe...]
    ppermute x2 -> x17, starting transfers between devices: 3.66 us -> 24.4 us  [the longest x3 9.29 us: margins(): low = lax.ppermute(part[:, extent - 1:], SLAB, up)]
    unnamed x10 -> x6, local copies, waits for them, and re-layouts: 19.1 us -> 0.01 us
    unnamed x26 -> x0, other arithmetic: 14.2 us -> none
  transfers between devices with their start and end apart: 3 -> 17, of which waited for: 2 -> 11; matrix products, arithmetic and copies ran while one was open for 0% -> 3% of each run, Pallas kernels for 0% -> 26%
where the time goes in v3:
time: 90.2 us; the launch traced here: 89.9 us
  waiting for transfers between devices  33 us (37%)
  Pallas kernels  28.3 us (31%)
  starting transfers between devices  24.4 us (27%)
  local copies, waits for them, and re-layouts  3.21 us (4%)
    pallas_call x3, Pallas kernels, conv_blocks(): pl.pallas_call(functools.partial(conv_kernel, sources=[len(v[3]) for v in...  23.5 us
    ppermute x1, waiting for transfers between devices, two_level_body(): got_a = lax.ppermute(got, PLANAR, first)  9.93 us
    ppermute x3, starting transfers between devices, margins(): low = lax.ppermute(part[:, extent - 1:], SLAB, up)  9.29 us
    ppermute x1, waiting for transfers between devices, two_level_body(): got = lax.ppermute(piece, 'chan', far)  6.71 us
    ppermute x1, waiting for transfers between devices, two_level_body(): theirs = lax.ppermute(sent, 'chan', near)  5.75 us
    ppermute x1, waiting for transfers between devices, two_level_body(): far_two = lax.ppermute(after(window_two, far_one), 'chan', far)  5.72 us
    pallas_call x1, Pallas kernels, down_blocks(): pl.pallas_call(down_kernel, grid=(extent,), in_specs=[pl.BlockSpec((1, ce...  4.77 us
    ppermute x3, starting transfers between devices, margins(): high = lax.ppermute(part[:, :1], SLAB, down)  4.14 us
  transfers between devices with their start and end apart: 17, of which 11 were waited for; matrix products, arithmetic and copies ran while one was open for 3% of the time, Pallas kernels for 26%

profile of v3, /device:TPU:0, one launch (start us, length us, event | category | flops | bytes accessed | tf_op | source)
XLA Modules:
  0.0 89.9 jit_solution(10379896924439024107)
XLA Ops:
  0.0 1.0 %constant_dynamic-slice_fusion = bf16[432,512]{1,0:T(8,128)(2,1)S(1)} fusion(bf16[3456,512]{1,0:T(8,128)(2,1)} %bitcast.27, s32[]{:T(128)S(6)} %select_n.15), kind=kLoop, calls=%fused_computation.20 | loop fusion | bytes 884740 | tf_op jit(solution)/shard_map/dynamic_slice | solution.py:239
  1.0 4.1 %collective-permute-start.2 = (bf16[432,512]{1,0:T(8,128)(2,1)S(1)}, bf16[432,512]{1,0:T(8,128)(2,1)S(1)}, u32[]{:S(2)}, u32[]{:S(2)}) collective-permute-start(bf16[432,512]{1,0:T(8,128)(2,1)S(1)} %constant_dynamic-slice_fusion), channel_id=1, source_target_pairs={{0,8},{4,12},{8,0},{12,4},{1,9},{5,13},{9,1},{13,5},{2,10},{6,14},... | collective-permute-start | bytes 1327112 | tf_op jit(solution)/shard_map/ppermute | solution.py:240
  5.1 2.0 %copy.5 = bf16[128,4,1024]{0,2,1:T(8,128)(2,1)S(1)} copy(bf16[128,4,1024]{2,1,0:T(4,128)(2,1)} %param.4) | data formatting | bytes 2097152 | tf_op jit(solution)/shard_map/optimization_barrier | solution.py:230
  7.3 1.6 %collective-permute-start.1 = (bf16[2,1,272,128]{3,2,1,0:T(8,128)(2,1)S(1)}, bf16[2,1,272,128]{3,2,1,0:T(8,128)(2,1)S(1)}, u32[]{:S(2)}, u32[]{:S(2)}) collective-permute-start(bf16[2,1,272,128]{3,2,1,0:T(8,128)(2,1)S(1)} %get-tuple-element.31), channel_id=1, source_target_pairs={{1,0},{2,1},{3,2},{5,4},{6,5},{7,6},{9,8},{10,9},{11,10},{13,12},{... | collective-permute-start | bytes 417800 | tf_op jit(solution)/shard_map/ppermute | solution.py:234
  8.9 3.0 %collective-permute-start = (bf16[2,1,272,128]{3,2,1,0:T(8,128)(2,1)S(1)}, bf16[2,1,272,128]{3,2,1,0:T(8,128)(2,1)S(1)}, u32[]{:S(2)}, u32[]{:S(2)}) collective-permute-start(bf16[2,1,272,128]{3,2,1,0:T(8,128)(2,1)S(1)} %get-tuple-element.32), channel_id=1, source_target_pairs={{0,1},{1,2},{2,3},{4,5},{5,6},{6,7},{8,9},{9,10},{10,11},{12,13},{... | collective-permute-start | bytes 417800 | tf_op jit(solution)/shard_map/ppermute | solution.py:233
  12.0 0.8 fusion.3.slope_ref
  12.9 5.1 %conv_blocks.3.refs_11_ = f32[1024,512]{1,0:T(8,128)S(1)} custom-call(s32[1]{0:T(128)} %bitcast.where_ref, bf16[4,272,128]{2,1,0:T(8,128)(2,1)S(1)} %get-tuple-element.28.refs_0_, bf16[272,128]{1,0:T(8,128)(2,1)S(1)} %get-tuple-element.39.refs_1_, bf16[272,128]{1,0:T(8,128)(2,1)S(1)} %get-tuple-element.37.refs_2_, bf16[3456,512]{1,0:T(8,128)(2,1)S(1)} %bitcast.28), custom_call_target="tpu_custom_call" | custom-call | flops 4000000000 | bytes 10000000 | tf_op jit(solution)/shard_map/conv_blocks/pallas_call | solution.py:161
  18.1 6.7 %collective-permute-done.2.refs_3_.refs_7_ = bf16[432,512]{1,0:T(8,128)(2,1)S(1)} collective-permute-done((bf16[432,512]{1,0:T(8,128)(2,1)S(1)}, bf16[432,512]{1,0:T(8,128)(2,1)S(1)}, u32[]{:S(2)}, u32[]{:S(2)}) %collective-permute-start.2) | collective-permute-done | bytes 442400 | tf_op jit(solution)/shard_map/ppermute | solution.py:240
  24.8 1.5 %collective-permute-start.5 = (bf16[432,512]{1,0:T(8,128)(2,1)S(1)}, bf16[432,512]{1,0:T(8,128)(2,1)S(1)}, u32[]{:S(2)}, u32[]{:S(2)}) collective-permute-start(bf16[432,512]{1,0:T(8,128)(2,1)S(1)} %collective-permute-done.2.refs_3_.refs_7_), channel_id=1, source_target_pairs={{0,2},{1,17},{2,0},{3,19},{16,18},{17,1},{18,16},{19,3},{4,6},{5,2... | collective-permute-start | bytes 1327112 | tf_op jit(solution)/shard_map/ppermute | solution.py:260
  26.3 1.5 %collective-permute-start.9 = (bf16[432,512]{1,0:T(8,128)(2,1)S(1)}, bf16[432,512]{1,0:T(8,128)(2,1)S(1)}, u32[]{:S(2)}, u32[]{:S(2)}) collective-permute-start(bf16[432,512]{1,0:T(8,128)(2,1)S(1)} %collective-permute-done.2.refs_3_.refs_7_), channel_id=1, source_target_pairs={{0,16},{1,3},{2,18},{3,1},{16,0},{17,19},{18,2},{19,17},{4,20},{5,... | collective-permute-start | bytes 1327112 | tf_op jit(solution)/shard_map/ppermute | solution.py:261
  27.9 9.9 %collective-permute-done.5.refs_4_.refs_8_ = bf16[432,512]{1,0:T(8,128)(2,1)S(1)} collective-permute-done((bf16[432,512]{1,0:T(8,128)(2,1)S(1)}, bf16[432,512]{1,0:T(8,128)(2,1)S(1)}, u32[]{:S(2)}, u32[]{:S(2)}) %collective-permute-start.5) | collective-permute-done | bytes 442400 | tf_op jit(solution)/shard_map/ppermute | solution.py:260
  38.4 2.1 %collective-permute-done.3.refs_0_ = bf16[4,272,128]{2,1,0:T(8,128)(2,1)S(1)} collective-permute-done((bf16[4,272,128]{2,1,0:T(8,128)(2,1)S(1)}, bf16[4,272,128]{2,1,0:T(8,128)(2,1)S(1)}, u32[]{:S(2)}, u32[]{:S(2)}) %collective-permute-start.3) | collective-permute-done | bytes 278560 | tf_op jit(solution)/shard_map/ppermute | solution.py:259
  40.5 1.3 %collective-permute-start.8 = (bf16[1,1,272,128]{3,2,1,0:T(8,128)(2,1)S(1)}, bf16[1,1,272,128]{3,2,1,0:T(8,128)(2,1)S(1)}, u32[]{:S(2)}, u32[]{:S(2)}) collective-permute-start(bf16[1,1,272,128]{3,2,1,0:T(8,128)(2,1)S(1)} %get-tuple-element.35), channel_id=1, source_target_pairs={{1,0},{2,1},{3,2},{5,4},{6,5},{7,6},{9,8},{10,9},{11,10},{13,12},{... | collective-permute-start | bytes 208904 | tf_op jit(solution)/shard_map/ppermute | solution.py:234
  41.8 3.0 %collective-permute-start.7 = (bf16[1,1,272,128]{3,2,1,0:T(8,128)(2,1)S(1)}, bf16[1,1,272,128]{3,2,1,0:T(8,128)(2,1)S(1)}, u32[]{:S(2)}, u32[]{:S(2)}) collective-permute-start(bf16[1,1,272,128]{3,2,1,0:T(8,128)(2,1)S(1)} %get-tuple-element.36), channel_id=1, source_target_pairs={{0,1},{1,2},{2,3},{4,5},{5,6},{6,7},{8,9},{9,10},{10,11},{12,13},{... | collective-permute-start | bytes 208904 | tf_op jit(solution)/shard_map/ppermute | solution.py:233
  44.9 1.2 %collective-permute-start.10 = (bf16[432,512]{1,0:T(8,128)(2,1)S(1)}, bf16[432,512]{1,0:T(8,128)(2,1)S(1)}, u32[]{:S(2)}, u32[]{:S(2)}) collective-permute-start(bf16[432,512]{1,0:T(8,128)(2,1)S(1)} %collective-permute-done.2.refs_3_.refs_7_), channel_id=1, source_target_pairs={{0,1},{1,0},{2,3},{3,2},{4,5},{5,4},{6,7},{7,6},{8,9},{9,8},{10,11... | collective-permute-start | bytes 1327112 | tf_op jit(solution)/shard_map/ppermute | solution.py:268
  46.6 0.8 collective-permute-start.13
  49.4 7.0 %conv_blocks.4 = bf16[1024,512]{1,0:T(8,128)(2,1)S(1)} custom-call(s32[1]{0:T(128)} %bitcast.where_ref, bf16[4,272,128]{2,1,0:T(8,128)(2,1)S(1)} %collective-permute-done.3.refs_0_, bf16[272,128]{1,0:T(8,128)(2,1)S(1)} %bitcast.31, bf16[272,128]{1,0:T(8,128)(2,1)S(1)} %bitcast.30, bf16[432,512]{1,0:T(8,128)(2,1)S(1)} %collective-permute-done.2.refs_3_.refs_7_, ...), custom_call_target="tpu_custom_call" | custom-call | flops 4000000000 | bytes 10000000 | tf_op jit(solution)/shard_map/conv_blocks/pallas_call | solution.py:161
  56.4 0.7 collective-permute-start.16
  57.1 5.7 %collective-permute-done.4.refs_4_ = bf16[4,272,128]{2,1,0:T(8,128)(2,1)S(1)} collective-permute-done((bf16[4,272,128]{2,1,0:T(8,128)(2,1)S(1)}, bf16[4,272,128]{2,1,0:T(8,128)(2,1)S(1)}, u32[]{:S(2)}, u32[]{:S(2)}) %collective-permute-start.4) | collective-permute-done | bytes 278560 | tf_op jit(solution)/shard_map/ppermute | solution.py:265
  62.8 1.3 %collective-permute-start.15 = (bf16[1,1,272,128]{3,2,1,0:T(8,128)(2,1)S(1)}, bf16[1,1,272,128]{3,2,1,0:T(8,128)(2,1)S(1)}, u32[]{:S(2)}, u32[]{:S(2)}) collective-permute-start(bf16[1,1,272,128]{3,2,1,0:T(8,128)(2,1)S(1)} %get-tuple-element.33), channel_id=1, source_target_pairs={{1,0},{2,1},{3,2},{5,4},{6,5},{7,6},{9,8},{10,9},{11,10},{13,12},{... | collective-permute-start | bytes 208904 | tf_op jit(solution)/shard_map/ppermute | solution.py:234
  64.1 3.2 %collective-permute-start.14 = (bf16[1,1,272,128]{3,2,1,0:T(8,128)(2,1)S(1)}, bf16[1,1,272,128]{3,2,1,0:T(8,128)(2,1)S(1)}, u32[]{:S(2)}, u32[]{:S(2)}) collective-permute-start(bf16[1,1,272,128]{3,2,1,0:T(8,128)(2,1)S(1)} %get-tuple-element.34), channel_id=1, source_target_pairs={{0,1},{1,2},{2,3},{4,5},{5,6},{6,7},{8,9},{9,10},{10,11},{12,13},{... | collective-permute-start | bytes 208904 | tf_op jit(solution)/shard_map/ppermute | solution.py:233
  68.0 11.4 %conv_blocks.5 = f32[1024,512]{1,0:T(8,128)S(1)} custom-call(s32[1]{0:T(128)} %bitcast.where_ref, bf16[4,272,128]{2,1,0:T(8,128)(2,1)S(1)} %get-tuple-element.30.refs_0_, bf16[272,128]{1,0:T(8,128)(2,1)S(1)} %get-tuple-element.40.refs_1_, bf16[272,128]{1,0:T(8,128)(2,1)S(1)} %get-tuple-element.38.refs_2_, bf16[3456,512]{1,0:T(8,128)(2,1)S(1)} %bitcast.29, ...), custom_call_target="tpu_custom_call" | custom-call | flops 8000000000 | bytes 20000000 | tf_op jit(solution)/shard_map/conv_blocks/pallas_call | solution.py:161
  79.4 5.7 %collective-permute-done.16 = bf16[1024,512]{1,0:T(8,128)(2,1)S(1)} collective-permute-done((bf16[1024,512]{1,0:T(8,128)(2,1)S(1)}, bf16[1024,512]{1,0:T(8,128)(2,1)S(1)}, u32[]{:S(2)}, u32[]{:S(2)}) %collective-permute-start.16) | collective-permute-done | bytes 1048608 | tf_op jit(solution)/shard_map/ppermute | solution.py:277
  85.2 4.8 %down_blocks.1 = bf16[4,256,8,256]{3,2,1,0:T(8,128)(2,1)} custom-call(f32[4,256,512]{2,1,0:T(8,128)S(1)} %bitcast.21, bf16[4,256,512]{2,1,0:T(8,128)(2,1)S(1)} %bitcast.24, f32[4,256,512]{2,1,0:T(8,128)S(1)} %fusion.3.slope_ref, bf16[8,256,512]{2,1,0:T(8,128)(2,1)S(1)} %copy-done), custom_call_target="tpu_custom_call" | custom-call | tf_op jit(solution)/shard_map/down_blocks/pallas_call | solution.py:195
  (29 shorter events, 4.2 us)
Async XLA Ops:
  1.0 23.7 %collective-permute-start.2 = (bf16[432,512]{1,0:T(8,128)(2,1)S(1)}, bf16[432,512]{1,0:T(8,128)(2,1)S(1)}, u32[]{:S(2)}, u32[]{:S(2)}) collective-permute-start(bf16[432,512]{1,0:T(8,128)(2,1)S(1)} %constant_dynamic-slice_fusion), channel_id=1, source_target_pairs={{0,8},{4,12},{8,0},{12,4},{1,9},{5,13},{9,1},{13,5},{2,10},{6,14},... | collective-permute-start | bytes 1327112 | tf_op jit(solution)/shard_map/ppermute | solution.py:240
  5.1 6.8 %copy-start.2 = (bf16[4,256,512]{2,1,0:T(8,128)(2,1)S(1)}, bf16[4,256,512]{2,1,0:T(8,128)(2,1)}, u32[]{:S(2)}) copy-start(bf16[4,256,512]{2,1,0:T(8,128)(2,1)} %param.6) | copy-start | bytes 3145732
  7.3 5.6 %copy-start.1 = (bf16[27,128,512]{2,1,0:T(8,128)(2,1)S(1)}, bf16[27,128,512]{2,1,0:T(8,128)(2,1)}, u32[]{:S(2)}) copy-start(bf16[27,128,512]{2,1,0:T(8,128)(2,1)} %param.5) | copy-start | bytes 10616836
  7.3 5.4 %collective-permute-start.1 = (bf16[2,1,272,128]{3,2,1,0:T(8,128)(2,1)S(1)}, bf16[2,1,272,128]{3,2,1,0:T(8,128)(2,1)S(1)}, u32[]{:S(2)}, u32[]{:S(2)}) collective-permute-start(bf16[2,1,272,128]{3,2,1,0:T(8,128)(2,1)S(1)} %get-tuple-element.31), channel_id=1, source_target_pairs={{1,0},{2,1},{3,2},{5,4},{6,5},{7,6},{9,8},{10,9},{11,10},{13,12},{... | collective-permute-start | bytes 417800 | tf_op jit(solution)/shard_map/ppermute | solution.py:234
  8.9 4.0 %collective-permute-start = (bf16[2,1,272,128]{3,2,1,0:T(8,128)(2,1)S(1)}, bf16[2,1,272,128]{3,2,1,0:T(8,128)(2,1)S(1)}, u32[]{:S(2)}, u32[]{:S(2)}) collective-permute-start(bf16[2,1,272,128]{3,2,1,0:T(8,128)(2,1)S(1)} %get-tuple-element.32), channel_id=1, source_target_pairs={{0,1},{1,2},{2,3},{4,5},{5,6},{6,7},{8,9},{9,10},{10,11},{12,13},{... | collective-permute-start | bytes 417800 | tf_op jit(solution)/shard_map/ppermute | solution.py:233
  24.8 13.0 %collective-permute-start.5 = (bf16[432,512]{1,0:T(8,128)(2,1)S(1)}, bf16[432,512]{1,0:T(8,128)(2,1)S(1)}, u32[]{:S(2)}, u32[]{:S(2)}) collective-permute-start(bf16[432,512]{1,0:T(8,128)(2,1)S(1)} %collective-permute-done.2.refs_3_.refs_7_), channel_id=1, source_target_pairs={{0,2},{1,17},{2,0},{3,19},{16,18},{17,1},{18,16},{19,3},{4,6},{5,2... | collective-permute-start | bytes 1327112 | tf_op jit(solution)/shard_map/ppermute | solution.py:260
  26.3 14.2 %collective-permute-start.3 = (bf16[4,272,128]{2,1,0:T(8,128)(2,1)S(1)}, bf16[4,272,128]{2,1,0:T(8,128)(2,1)S(1)}, u32[]{:S(2)}, u32[]{:S(2)}) collective-permute-start(bf16[4,272,128]{2,1,0:T(8,128)(2,1)S(1)} %get-tuple-element.19), channel_id=1, source_target_pairs={{0,8},{4,12},{8,0},{12,4},{1,9},{5,13},{9,1},{13,5},{2,10},{6,14},... | collective-permute-start | bytes 835592 | tf_op jit(solution)/shard_map/ppermute | solution.py:259
  26.3 19.7 %collective-permute-start.9 = (bf16[432,512]{1,0:T(8,128)(2,1)S(1)}, bf16[432,512]{1,0:T(8,128)(2,1)S(1)}, u32[]{:S(2)}, u32[]{:S(2)}) collective-permute-start(bf16[432,512]{1,0:T(8,128)(2,1)S(1)} %collective-permute-done.2.refs_3_.refs_7_), channel_id=1, source_target_pairs={{0,16},{1,3},{2,18},{3,1},{16,0},{17,19},{18,2},{19,17},{4,20},{5,... | collective-permute-start | bytes 1327112 | tf_op jit(solution)/shard_map/ppermute | solution.py:261
  37.8 8.8 %collective-permute-start.6 = (bf16[432,512]{1,0:T(8,128)(2,1)S(1)}, bf16[432,512]{1,0:T(8,128)(2,1)S(1)}, u32[]{:S(2)}, u32[]{:S(2)}) collective-permute-start(bf16[432,512]{1,0:T(8,128)(2,1)S(1)} %collective-permute-done.5.refs_4_.refs_8_), channel_id=1, source_target_pairs={{0,16},{1,3},{2,18},{3,1},{16,0},{17,19},{18,2},{19,17},{4,20},{5,... | collective-permute-start | bytes 1327112 | tf_op jit(solution)/shard_map/ppermute | solution.py:262
  40.5 5.6 %collective-permute-start.8 = (bf16[1,1,272,128]{3,2,1,0:T(8,128)(2,1)S(1)}, bf16[1,1,272,128]{3,2,1,0:T(8,128)(2,1)S(1)}, u32[]{:S(2)}, u32[]{:S(2)}) collective-permute-start(bf16[1,1,272,128]{3,2,1,0:T(8,128)(2,1)S(1)} %get-tuple-element.35), channel_id=1, source_target_pairs={{1,0},{2,1},{3,2},{5,4},{6,5},{7,6},{9,8},{10,9},{11,10},{13,12},{... | collective-permute-start | bytes 208904 | tf_op jit(solution)/shard_map/ppermute | solution.py:234
  41.8 4.7 %collective-permute-start.7 = (bf16[1,1,272,128]{3,2,1,0:T(8,128)(2,1)S(1)}, bf16[1,1,272,128]{3,2,1,0:T(8,128)(2,1)S(1)}, u32[]{:S(2)}, u32[]{:S(2)}) collective-permute-start(bf16[1,1,272,128]{3,2,1,0:T(8,128)(2,1)S(1)} %get-tuple-element.36), channel_id=1, source_target_pairs={{0,1},{1,2},{2,3},{4,5},{5,6},{6,7},{8,9},{9,10},{10,11},{12,13},{... | collective-permute-start | bytes 208904 | tf_op jit(solution)/shard_map/ppermute | solution.py:233
  44.9 2.6 %collective-permute-start.10 = (bf16[432,512]{1,0:T(8,128)(2,1)S(1)}, bf16[432,512]{1,0:T(8,128)(2,1)S(1)}, u32[]{:S(2)}, u32[]{:S(2)}) collective-permute-start(bf16[432,512]{1,0:T(8,128)(2,1)S(1)} %collective-permute-done.2.refs_3_.refs_7_), channel_id=1, source_target_pairs={{0,1},{1,0},{2,3},{3,2},{4,5},{5,4},{6,7},{7,6},{8,9},{9,8},{10,11... | collective-permute-start | bytes 1327112 | tf_op jit(solution)/shard_map/ppermute | solution.py:268
  46.0 2.0 %collective-permute-start.12 = (bf16[432,512]{1,0:T(8,128)(2,1)S(1)}, bf16[432,512]{1,0:T(8,128)(2,1)S(1)}, u32[]{:S(2)}, u32[]{:S(2)}) collective-permute-start(bf16[432,512]{1,0:T(8,128)(2,1)S(1)} %collective-permute-done.9.refs_5_.refs_9_), channel_id=1, source_target_pairs={{0,1},{1,0},{2,3},{3,2},{4,5},{5,4},{6,7},{7,6},{8,9},{9,8},{10,11... | collective-permute-start | bytes 1327112 | tf_op jit(solution)/shard_map/ppermute | solution.py:268
  46.1 2.6 %collective-permute-start.11 = (bf16[432,512]{1,0:T(8,128)(2,1)S(1)}, bf16[432,512]{1,0:T(8,128)(2,1)S(1)}, u32[]{:S(2)}, u32[]{:S(2)}) collective-permute-start(bf16[432,512]{1,0:T(8,128)(2,1)S(1)} %collective-permute-done.5.refs_4_.refs_8_), channel_id=1, source_target_pairs={{0,1},{1,0},{2,3},{3,2},{4,5},{5,4},{6,7},{7,6},{8,9},{9,8},{10,11... | collective-permute-start | bytes 1327112 | tf_op jit(solution)/shard_map/ppermute | solution.py:268
  46.6 2.8 %collective-permute-start.13 = (bf16[432,512]{1,0:T(8,128)(2,1)S(1)}, bf16[432,512]{1,0:T(8,128)(2,1)S(1)}, u32[]{:S(2)}, u32[]{:S(2)}) collective-permute-start(bf16[432,512]{1,0:T(8,128)(2,1)S(1)} %collective-permute-done.6.refs_6_.refs_10_), channel_id=1, source_target_pairs={{0,1},{1,0},{2,3},{3,2},{4,5},{5,4},{6,7},{7,6},{8,9},{9,8},{10,11... | collective-permute-start | bytes 1327112 | tf_op jit(solution)/shard_map/ppermute | solution.py:268
  47.3 15.5 %collective-permute-start.4 = (bf16[4,272,128]{2,1,0:T(8,128)(2,1)S(1)}, bf16[4,272,128]{2,1,0:T(8,128)(2,1)S(1)}, u32[]{:S(2)}, u32[]{:S(2)}) collective-permute-start(bf16[4,272,128]{2,1,0:T(8,128)(2,1)S(1)} %get-tuple-element.20), channel_id=1, source_target_pairs={{0,8},{4,12},{8,0},{12,4},{1,9},{5,13},{9,1},{13,5},{2,10},{6,14},... | collective-permute-start | bytes 835592 | tf_op jit(solution)/shard_map/ppermute | solution.py:265
  56.4 28.8 %collective-permute-start.16 = (bf16[1024,512]{1,0:T(8,128)(2,1)S(1)}, bf16[1024,512]{1,0:T(8,128)(2,1)S(1)}, u32[]{:S(2)}, u32[]{:S(2)}) collective-permute-start(bf16[1024,512]{1,0:T(8,128)(2,1)S(1)} %conv_blocks.4), channel_id=1, source_target_pairs={{0,4},{4,0},{8,12},{12,8},{1,5},{5,1},{9,13},{13,9},{2,6},{6,2},{1... | collective-permute-start | bytes 3145736 | tf_op jit(solution)/shard_map/ppermute | solution.py:277
  62.8 4.5 %collective-permute-start.15 = (bf16[1,1,272,128]{3,2,1,0:T(8,128)(2,1)S(1)}, bf16[1,1,272,128]{3,2,1,0:T(8,128)(2,1)S(1)}, u32[]{:S(2)}, u32[]{:S(2)}) collective-permute-start(bf16[1,1,272,128]{3,2,1,0:T(8,128)(2,1)S(1)} %get-tuple-element.33), channel_id=1, source_target_pairs={{1,0},{2,1},{3,2},{5,4},{6,5},{7,6},{9,8},{10,9},{11,10},{13,12},{... | collective-permute-start | bytes 208904 | tf_op jit(solution)/shard_map/ppermute | solution.py:234
  64.1 3.9 %collective-permute-start.14 = (bf16[1,1,272,128]{3,2,1,0:T(8,128)(2,1)S(1)}, bf16[1,1,272,128]{3,2,1,0:T(8,128)(2,1)S(1)}, u32[]{:S(2)}, u32[]{:S(2)}) collective-permute-start(bf16[1,1,272,128]{3,2,1,0:T(8,128)(2,1)S(1)} %get-tuple-element.34), channel_id=1, source_target_pairs={{0,1},{1,2},{2,3},{4,5},{5,6},{6,7},{8,9},{9,10},{10,11},{12,13},{... | collective-permute-start | bytes 208904 | tf_op jit(solution)/shard_map/ppermute | solution.py:233
  68.0 17.1 %copy-start = (bf16[8,256,512]{2,1,0:T(8,128)(2,1)S(1)}, bf16[8,256,512]{2,1,0:T(8,128)(2,1)}, u32[]{:S(2)}) copy-start(bf16[8,256,512]{2,1,0:T(8,128)(2,1)} %weight_ref.1) | copy-start | bytes 6291460

commit v4 on v3

v4 whole, which is shorter than its diff:
```python
import functools
import math

import jax
import jax.numpy as jnp
from jax import lax
from jax.experimental import pallas as pl
from jax.experimental.pallas import tpu as pltpu
from jax.sharding import PartitionSpec as P

NZ = 8
PLANAR = ("groups", "space", "pair")
SLAB = ("space", "pair")
LIMIT = 20
PART = (1, 1, 1, 4)


def gelu_slope(values):
    return 0.5 * (1.0 + jax.scipy.special.erf(values / math.sqrt(2.0))) + values * jnp.exp(
        -0.5 * values * values
    ) / math.sqrt(2.0 * math.pi)


def with_halo(cells, sides, width):
    for axis, dim in sides:
        count = lax.axis_size(axis)
        ends = count - 1
        head = lax.slice_in_dim(cells, 0, width, axis=dim)
        tail = lax.slice_in_dim(cells, cells.shape[dim] - width, cells.shape[dim], axis=dim)
        cells = jnp.concatenate(
            [
                lax.ppermute(tail, axis, [(i, (i + 1) % count) for i in range(ends)]),
                cells,
                lax.ppermute(head, axis, [((i + 1) % count, i) for i in range(ends)]),
            ],
            axis=dim,
        )
    return cells


def shifted_stack(padded, depth):
    extent = padded.shape[1] - 2
    plane_len = padded.shape[2]
    widened = jnp.pad(padded, ((0, 0), (0, 0), (depth + 1, depth + 1)))
    z_index = jnp.arange(plane_len, dtype=jnp.int32) % depth
    pieces = []
    for step_x in (-1, 0, 1):
        x_rows = widened[:, 1 - step_x : 1 - step_x + extent, :]
        for step_y in (-1, 0, 1):
            for step_z in (-1, 0, 1):
                offset = step_y * depth + step_z
                piece = x_rows[:, :, depth + 1 - offset : depth + 1 - offset + plane_len]
                inside = (z_index - step_z >= 0) & (z_index - step_z < depth)
                pieces.append(jnp.where(inside, piece, jnp.zeros_like(piece)))
    return jnp.stack(pieces)


def general_body(grad_out, conv_weight, pre_act, down_weight):
    padded = with_halo(grad_out, ((SLAB, 1),), 1)
    stacked = shifted_stack(padded, NZ)
    partial_sum = lax.dot_general(
        stacked, conv_weight, (((0, 1), (0, 1)), ((), ())), preferred_element_type=jnp.float32
    )
    owned = lax.psum_scatter(
        partial_sum.astype(jnp.bfloat16), "chan", scatter_dimension=2, tiled=True
    )
    grad_act = lax.all_to_all(owned, "chan", split_axis=1, concat_axis=2, tiled=True)
    values = pre_act.astype(jnp.float32)
    grad_pre = (grad_act.astype(jnp.float32) * gelu_slope(values)).astype(jnp.bfloat16)
    result = lax.dot_general(
        grad_pre, down_weight, (((2,), (2,)), ((), ())), preferred_element_type=jnp.float32
    )
    return result.astype(jnp.bfloat16)


def piece_order(q):
    first = 2 + 2 * (q & 1)
    second = 6 - first
    return [q, q ^ first, q ^ second, q ^ 6, q ^ 1, q ^ 1 ^ second, q ^ 1 ^ first, q ^ 7]


def conv_kernel(where_ref, *refs, sources, added, planes):
    refs = list(refs)
    groups = []
    for margins, pieces in sources:
        cells_refs = refs[: 3 if margins else 1]
        del refs[: len(cells_refs)]
        groups.append((cells_refs, refs[:pieces]))
        del refs[:pieces]
    start_ref = refs.pop(0) if added else None
    out_ref = refs.pop(0)
    for n, (cells_refs, weights) in enumerate(groups):
        if len(weights) == 1:
            groups[n] = (cells_refs, weights[0])
            continue
        table = refs.pop(0)
        for piece, spot in zip(weights, piece_order(where_ref[0])):
            share = piece.shape[0]
            table[pl.ds(pl.multiple_of(spot * share, 16), share), :] = piece[...]
        groups[n] = (cells_refs, table)
    copies = refs.pop(0)

    extent, rows, width = groups[0][0][0].shape
    cells = rows - 2 * NZ
    needed = sorted({plane + step for plane in planes for step in range(3)})
    depth_at = lax.broadcasted_iota(jnp.int32, (rows, width), 0) % NZ
    inner_first = (where_ref[0] & 1) == 0
    totals = [start_ref[plane] if added else None for plane in planes]
    for cells_refs, table in groups:
        for x in needed:
            if x == 0:
                plane = jnp.where(inner_first, cells_refs[2][...], cells_refs[1][...])
            elif x == extent + 1:
                plane = jnp.where(inner_first, cells_refs[1][...], cells_refs[2][...])
            else:
                plane = cells_refs[0][x - 1]
            plane = plane.astype(jnp.float32)
            for step_z in (-1, 0, 1):
                if step_z == 1:
                    moved = jnp.where(depth_at >= 1, pltpu.roll(plane, 1, 0), 0.0)
                elif step_z == -1:
                    moved = jnp.where(depth_at < NZ - 1, pltpu.roll(plane, rows - 1, 0), 0.0)
                else:
                    moved = plane
                for step_y in (-1, 0, 1):
                    at = NZ * (1 - step_y)
                    lane = (3 * (step_y + 1) + step_z + 1) * width
                    copies[needed.index(x), :, lane : lane + width] = moved[
                        at : at + cells
                    ].astype(jnp.bfloat16)
        for step_x in (-1, 0, 1):
            left = jnp.concatenate(
                [copies[needed.index(plane + 1 - step_x)] for plane in planes], axis=0
            )
            right = table[(step_x + 1) * 9 * width : (step_x + 2) * 9 * width]
            term = jnp.dot(left, right, preferred_element_type=jnp.float32)
            for n in range(len(planes)):
                part = term[n * cells : (n + 1) * cells]
                totals[n] = part if totals[n] is None else totals[n] + part
    for n in range(len(planes)):
        out_ref[n] = totals[n].astype(out_ref.dtype)


def conv_blocks(where, sources, start, planes, kind, part=1):
    extent, rows, width = sources[0][0][0].shape
    wide = sources[0][1][0].shape[1]
    table_rows = sum(v.shape[0] for v in sources[0][1])
    cells = rows - 2 * NZ
    needed = len({plane + step for plane in planes for step in range(3)})
    pieces = max(len(v[1]) for v in sources)
    in_specs = [pl.BlockSpec(memory_space=pltpu.SMEM)]
    operands = [where]
    on_chip = pl.BlockSpec(memory_space=pltpu.VMEM)
    for cells_and_margins, weights in sources:
        in_specs += [on_chip] * (len(cells_and_margins) + len(weights))
        operands += [*cells_and_margins, *weights]
    if start is not None:
        in_specs.append(on_chip)
        operands.append(start)
    shape = (len(planes), cells, wide)
    out_shape = [jax.ShapeDtypeStruct(shape, kind)]
    scratch = [pltpu.VMEM((needed, cells, 9 * width), jnp.bfloat16)]
    if pieces > 1:
        out_shape.append(jax.ShapeDtypeStruct((table_rows, wide), jnp.bfloat16))
    return pl.pallas_call(
        functools.partial(
            conv_kernel,
            sources=[(len(v[0]) > 1, len(v[1])) for v in sources],
            added=start is not None,
            planes=planes,
        ),
        in_specs=in_specs,
        out_specs=[on_chip] * len(out_shape),
        out_shape=out_shape,
        scratch_shapes=scratch,
        compiler_params=pltpu.CompilerParams(vmem_limit_bytes=LIMIT * 2**20),
        cost_estimate=pl.CostEstimate(
            flops=2 * math.prod(shape) * table_rows * len(sources) // part,
            transcendentals=0,
            bytes_accessed=(2 * math.prod(shape) + 2 * table_rows * wide * len(sources)) // part,
        ),
        name="conv_blocks",
    )(*operands)


def down_kernel(mine_ref, theirs_ref, slope_ref, weight_ref, *refs):
    out_ref = refs[-1]
    act = (mine_ref[0] + theirs_ref[0].astype(jnp.float32)).astype(jnp.bfloat16)
    pre = (act.astype(jnp.float32) * slope_ref[0]).astype(jnp.bfloat16)
    grown = [
        lax.dot_general(
            pre,
            weight_ref[e],
            (((1,), (1,)), ((), ())),
            preferred_element_type=jnp.float32,
        ).astype(out_ref.dtype)
        for e in range(weight_ref.shape[0])
    ]
    out_ref[0] = jnp.swapaxes(jnp.stack(grown), 0, 1)


def down_blocks(mine, theirs, slope, weight, planes, partly):
    extent, cells, wide = slope.shape
    offsets, fine, _ = weight.shape
    first, step = planes[0], planes[1] - planes[0]
    own_plane = pl.BlockSpec((1, cells, wide), lambda i: (first + step * i, 0, 0))
    in_specs = [
        own_plane,
        pl.BlockSpec((1, cells, wide), lambda i: (i, 0, 0)),
        own_plane,
        pl.BlockSpec((offsets, fine, wide), lambda i: (0, 0, 0)),
    ]
    operands = [mine, theirs, slope, weight]
    if partly is not None:
        in_specs.append(pl.BlockSpec(memory_space=pl.ANY))
        operands.append(partly)
    return pl.pallas_call(
        down_kernel,
        grid=(len(planes),),
        in_specs=in_specs,
        out_specs=pl.BlockSpec(
            (1, cells, offsets, fine), lambda i: (first + step * i, 0, 0, 0)
        ),
        out_shape=jax.ShapeDtypeStruct((extent, cells, offsets, fine), jnp.bfloat16),
        input_output_aliases={} if partly is None else {4: 0},
        compiler_params=pltpu.CompilerParams(vmem_limit_bytes=20 * 2**20),
        cost_estimate=pl.CostEstimate(
            flops=2 * len(planes) * cells * wide * offsets * fine,
            transcendentals=0,
            bytes_accessed=len(planes) * cells * (wide * 10 + offsets * fine * 2),
        ),
        name="down_blocks",
    )(*operands)


def planar_moves(swap):
    return [(q, swap(q)) for q in range(8)]


def two_level_body(grad_out, conv_weight, pre_act, down_weight):
    width, extent, plane = grad_out.shape
    taps, _, wide = conv_weight.shape
    block = plane // 4
    k = lax.axis_index("chan")
    q = lax.axis_index(PLANAR)
    far = [(i, i ^ 2) for i in range(4)]
    near = [(i, i ^ 1) for i in range(4)]
    first = planar_moves(lambda d: d ^ (2 if d & 1 == 0 else 4))
    second = planar_moves(lambda d: d ^ (4 if d & 1 == 0 else 2))
    other = [(0, 1), (1, 0)]
    middle = [(1, 2), (2, 1)]

    def after(value, *others):
        return lax.optimization_barrier((value, *others))[0]

    def margins(part):
        head, tail = part[:, :1], part[:, extent - 1 :]
        inner = lax.ppermute(
            jnp.where(lax.axis_index("pair") == 0, tail, head), "pair", other
        )
        outer = lax.ppermute(
            jnp.where(lax.axis_index("space") == 0, tail, head), SLAB, middle
        )
        return inner, outer

    table = conv_weight.reshape(taps * width, wide)
    share = taps * width // 8
    piece = lax.dynamic_slice_in_dim(table, q * share, share, 0)
    got = lax.ppermute(piece, "chan", far)

    cells = jnp.pad(
        jnp.transpose(after(grad_out, piece), (1, 2, 0)), ((0, 0), (NZ, NZ), (0, 0))
    )

    def window(which):
        return lax.dynamic_slice_in_dim(cells, which * block, block + 2 * NZ, 1)

    where = jnp.reshape(q, (1,)).astype(jnp.int32)
    own_one, own_two = window(k ^ 1), window(k)
    own_inner, own_outer = margins(jnp.stack([own_one, own_two]))
    every, inside, edges = (0, 1, 2, 3), (1, 2), (0, 3)
    begun = conv_blocks(
        where,
        [((own_one, own_inner[0, 0], own_outer[0, 0]), [table])],
        None,
        every,
        jnp.float32,
        PART[0],
    )[0]
    slope = gelu_slope(after(pre_act, piece).astype(jnp.float32))
    got, window_one, window_two = lax.optimization_barrier(
        (got, window(k ^ 3), window(k ^ 2), begun, slope)
    )[:3]
    far_one = lax.ppermute(window_one, "chan", far)
    got_a = lax.ppermute(got, PLANAR, first)
    got_b = lax.ppermute(got, PLANAR, second)
    got_c = lax.ppermute(got_a, PLANAR, second)
    pair_got, pair_a = [lax.ppermute(v, "pair", other) for v in (got, got_a)]
    got_b = after(got_b, far_one)
    pair_b = lax.ppermute(got_b, "pair", other)
    far_two = lax.ppermute(after(window_two, far_one), "chan", far)
    one_inner, one_outer = margins(far_one[None])
    got_c, pair_got, pair_a, one_inner, one_outer = lax.optimization_barrier(
        (got_c, pair_got, pair_a, one_inner, one_outer)
    )
    pair_c = lax.ppermute(got_c, "pair", other)
    pieces = [got, got_a, got_b, got_c, pair_got, pair_a, pair_b, pair_c]

    sent_inside, far_table = conv_blocks(
        where, [((far_one,), pieces)], begun, inside, jnp.bfloat16, PART[1]
    )
    theirs_inside = lax.ppermute(sent_inside, "chan", near)
    far_one = after(far_one, sent_inside)
    sent_edges = conv_blocks(
        where,
        [((far_one, one_inner[0, 0], one_outer[0, 0]), [far_table])],
        begun,
        edges,
        jnp.bfloat16,
        PART[2],
    )[0]
    theirs_edges = lax.ppermute(sent_edges, "chan", near)
    far_two = after(far_two, sent_edges)
    two_inner, two_outer = margins(far_two[None])
    kept = conv_blocks(
        where,
        [
            ((own_two, own_inner[1, 0], own_outer[1, 0]), [table]),
            ((far_two, two_inner[0, 0], two_outer[0, 0]), [far_table]),
        ],
        None,
        every,
        jnp.float32,
        PART[3],
    )[0]
    partly = down_blocks(kept, theirs_inside, slope, down_weight, inside, None)
    return down_blocks(kept, theirs_edges, slope, down_weight, edges, partly)


def solution(mesh):
    sizes = dict(mesh.shape)
    four = sizes["chan"] == 4 and all(sizes[axis] == 2 for axis in PLANAR)

    def run(grad_out, conv_weight, pre_act, down_weight):
        split = grad_out.shape[0] // sizes["chan"]
        body = two_level_body if four and split == 128 and grad_out.shape[1] == 32 else general_body
        in_specs = (
            P("chan", ("groups", "space", "pair"), None),
            P(None, "chan", None),
            P(("groups", "space", "pair"), "chan", None),
            P(),
        )
        out_specs = P(("groups", "space", "pair"), "chan", None, None)
        return jax.shard_map(
            body, mesh=mesh, in_specs=in_specs, out_specs=out_specs, check_vma=False
        )(grad_out, conv_weight, pre_act, down_weight)

    return run
```

time: 90.2 us -> 84.3 us (0.935)
  Pallas kernels: 28.3 us -> 23.5 us
  starting transfers between devices: 24.4 us -> 20.7 us
  waiting for transfers between devices: 33 us -> 35.3 us
    pallas_call x4 -> x6, Pallas kernels: 28.3 us -> 23.5 us  [the longest x4 17.9 us: conv_blocks(): pl.pallas_call(functools.partial(conv_kernel, sources=[(len(v[0]) > 1, le...]
    ppermute x1, waiting for transfers between devices: 6.71 us -> 11 us  [two_level_body(): got = lax.ppermute(piece, 'chan', far)]
    ppermute x11 -> x12, starting transfers between devices: 16.6 us -> 12.7 us  [the longest x3 6.09 us: margins(): lax.ppermute(jnp.where(lax.axis_index('pair') == 0, tail, head), 'pair',...]
    ppermute x11 -> x12, waiting for transfers between devices: 8.58 us -> 5.35 us  [the longest x1 2.55 us: two_level_body(): theirs_edges = lax.ppermute(sent_edges, 'chan', near)]
    ppermute x1, waiting for transfers between devices: 5.72 us -> 7.01 us  [two_level_body(): far_two = lax.ppermute(after(window_two, far_one), 'chan', far)]
  transfers between devices with their start and end apart: 17 -> 18, of which waited for: 11 -> 8; matrix products, arithmetic and copies ran while one was open for 3% -> 4% of each run, Pallas kernels for 26% -> 25%
where the time goes in v4:
time: 84.3 us; the launch traced here: 84.1 us
  waiting for transfers between devices  35.3 us (42%)
  Pallas kernels  23.5 us (28%)
  starting transfers between devices  20.7 us (25%)
  local copies, waits for them, and re-layouts  3.48 us (4%)
  other arithmetic  0.9 us (1%)
    pallas_call x4, Pallas kernels, conv_blocks(): pl.pallas_call(functools.partial(conv_kernel, sources=[(len(v[0]) > 1, le...  17.9 us
    ppermute x1, waiting for transfers between devices, two_level_body(): got = lax.ppermute(piece, 'chan', far)  11 us
    ppermute x1, waiting for transfers between devices, two_level_body(): got_a = lax.ppermute(got, PLANAR, first)  9.28 us
    ppermute x1, waiting for transfers between devices, two_level_body(): far_two = lax.ppermute(after(window_two, far_one), 'chan', far)  7.01 us
    ppermute x3, starting transfers between devices, margins(): lax.ppermute(jnp.where(lax.axis_index('pair') == 0, tail, head), 'pair',...  6.09 us
    pallas_call x2, Pallas kernels, down_blocks(): pl.pallas_call(down_kernel, grid=(len(planes),), in_specs=in_specs, out_s...  5.65 us
    ppermute x1, starting transfers between devices, two_level_body(): got = lax.ppermute(piece, 'chan', far)  4.1 us
    ppermute x1, waiting for transfers between devices, two_level_body(): far_one = lax.ppermute(window_one, 'chan', far)  2.6 us
  transfers between devices with their start and end apart: 18, of which 8 were waited for; matrix products, arithmetic and copies ran while one was open for 4% of the time, Pallas kernels for 25%

profile of v4, /device:TPU:0, one launch (start us, length us, event | category | flops | bytes accessed | tf_op | source)
XLA Modules:
  0.0 84.1 jit_solution(4522438088836496660)
XLA Ops:
  0.0 1.0 %constant_dynamic-slice_fusion = bf16[432,512]{1,0:T(8,128)(2,1)S(1)} fusion(bf16[3456,512]{1,0:T(8,128)(2,1)} %bitcast.19, s32[]{:T(128)S(6)} %select_n.51), kind=kLoop, calls=%fused_computation.26 | loop fusion | bytes 884740 | tf_op jit(solution)/shard_map/dynamic_slice | solution.py:268
  1.0 4.1 %collective-permute-start.2 = (bf16[432,512]{1,0:T(8,128)(2,1)S(1)}, bf16[432,512]{1,0:T(8,128)(2,1)S(1)}, u32[]{:S(2)}, u32[]{:S(2)}) collective-permute-start(bf16[432,512]{1,0:T(8,128)(2,1)S(1)} %constant_dynamic-slice_fusion), channel_id=1, source_target_pairs={{0,8},{4,12},{8,0},{12,4},{1,9},{5,13},{9,1},{13,5},{2,10},{6,14},... | collective-permute-start | bytes 1327112 | tf_op jit(solution)/shard_map/ppermute | solution.py:269
  5.1 1.9 %copy.6 = bf16[128,4,1024]{0,2,1:T(8,128)(2,1)S(1)} copy(bf16[128,4,1024]{2,1,0:T(4,128)(2,1)} %param.4) | data formatting | bytes 2097152 | tf_op jit(solution)/shard_map/optimization_barrier | solution.py:254
  8.3 0.8 fusion.3.slope_ref
  9.4 4.3 %conv_blocks.4.refs_9_.refs_4_ = f32[4,256,512]{2,1,0:T(8,128)S(1)} custom-call(s32[1]{0:T(128)} %bitcast.where_ref, bf16[4,272,128]{2,1,0:T(8,128)(2,1)S(1)} %get-tuple-element.41.refs_0_, bf16[272,128]{1,0:T(8,128)(2,1)S(1)} %get-tuple-element.50.refs_1_, bf16[272,128]{1,0:T(8,128)(2,1)S(1)} %get-tuple-element.48.refs_2_, bf16[3456,512]{1,0:T(8,128)(2,1)S(1)} %bitcast.20), custom_call_target="tpu_custom_call" | custom-call | flops 3623878656 | bytes 4587520 | tf_op jit(solution)/shard_map/conv_blocks/pallas_call | solution.py:165
  13.8 11.0 %collective-permute-done.2.refs_1_ = bf16[432,512]{1,0:T(8,128)(2,1)S(1)} collective-permute-done((bf16[432,512]{1,0:T(8,128)(2,1)S(1)}, bf16[432,512]{1,0:T(8,128)(2,1)S(1)}, u32[]{:S(2)}, u32[]{:S(2)}) %collective-permute-start.2) | collective-permute-done | bytes 442400 | tf_op jit(solution)/shard_map/ppermute | solution.py:269
  24.8 1.5 %collective-permute-start.5 = (bf16[432,512]{1,0:T(8,128)(2,1)S(1)}, bf16[432,512]{1,0:T(8,128)(2,1)S(1)}, u32[]{:S(2)}, u32[]{:S(2)}) collective-permute-start(bf16[432,512]{1,0:T(8,128)(2,1)S(1)} %collective-permute-done.2.refs_1_), channel_id=1, source_target_pairs={{0,2},{1,17},{2,0},{3,19},{16,18},{17,1},{18,16},{19,3},{4,6},{5,2... | collective-permute-start | bytes 1327112 | tf_op jit(solution)/shard_map/ppermute | solution.py:295
  26.3 1.5 %collective-permute-start.6 = (bf16[432,512]{1,0:T(8,128)(2,1)S(1)}, bf16[432,512]{1,0:T(8,128)(2,1)S(1)}, u32[]{:S(2)}, u32[]{:S(2)}) collective-permute-start(bf16[432,512]{1,0:T(8,128)(2,1)S(1)} %collective-permute-done.2.refs_1_), channel_id=1, source_target_pairs={{0,16},{1,3},{2,18},{3,1},{16,0},{17,19},{18,2},{19,17},{4,20},{5,... | collective-permute-start | bytes 1327112 | tf_op jit(solution)/shard_map/ppermute | solution.py:296
  27.9 9.3 %collective-permute-done.5.refs_2_ = bf16[432,512]{1,0:T(8,128)(2,1)S(1)} collective-permute-done((bf16[432,512]{1,0:T(8,128)(2,1)S(1)}, bf16[432,512]{1,0:T(8,128)(2,1)S(1)}, u32[]{:S(2)}, u32[]{:S(2)}) %collective-permute-start.5) | collective-permute-done | bytes 442400 | tf_op jit(solution)/shard_map/ppermute | solution.py:295
  37.9 2.6 %collective-permute-done.3.refs_0_ = bf16[4,272,128]{2,1,0:T(8,128)(2,1)S(1)} collective-permute-done((bf16[4,272,128]{2,1,0:T(8,128)(2,1)S(1)}, bf16[4,272,128]{2,1,0:T(8,128)(2,1)S(1)}, u32[]{:S(2)}, u32[]{:S(2)}) %collective-permute-start.3) | collective-permute-done | bytes 278560 | tf_op jit(solution)/shard_map/ppermute | solution.py:294
  41.2 2.9 %collective-permute-start.10 = (bf16[1,1,272,128]{3,2,1,0:T(8,128)(2,1)S(1)}, bf16[1,1,272,128]{3,2,1,0:T(8,128)(2,1)S(1)}, u32[]{:S(2)}, u32[]{:S(2)}) collective-permute-start(bf16[1,1,272,128]{3,2,1,0:T(8,128)(2,1)S(1)} %get-tuple-element.47), channel_id=1, source_target_pairs={{0,1},{1,0},{2,3},{3,2},{4,5},{5,4},{6,7},{7,6},{8,9},{9,8},{10,11... | collective-permute-start | bytes 208904 | tf_op jit(solution)/shard_map/ppermute | solution.py:258
  44.1 1.9 %collective-permute-start.12 = (bf16[432,512]{1,0:T(8,128)(2,1)S(1)}, bf16[432,512]{1,0:T(8,128)(2,1)S(1)}, u32[]{:S(2)}, u32[]{:S(2)}) collective-permute-start(bf16[432,512]{1,0:T(8,128)(2,1)S(1)} %collective-permute-done.6.refs_3_), channel_id=1, source_target_pairs={{0,1},{1,0},{2,3},{3,2},{4,5},{5,4},{6,7},{7,6},{8,9},{9,8},{10,11... | collective-permute-start | bytes 1327112 | tf_op jit(solution)/shard_map/ppermute | solution.py:300
  46.2 1.2 %collective-permute-done.12.refs_7_ = bf16[432,512]{1,0:T(8,128)(2,1)S(1)} collective-permute-done((bf16[432,512]{1,0:T(8,128)(2,1)S(1)}, bf16[432,512]{1,0:T(8,128)(2,1)S(1)}, u32[]{:S(2)}, u32[]{:S(2)}) %collective-permute-start.12) | collective-permute-done | bytes 442400 | tf_op jit(solution)/shard_map/ppermute | solution.py:300
  48.1 2.5 %conv_blocks.5 = (bf16[2,256,512]{2,1,0:T(8,128)(2,1)S(1)}, bf16[3456,512]{1,0:T(8,128)(2,1)S(1)}) custom-call(s32[1]{0:T(128)} %bitcast.where_ref, bf16[4,272,128]{2,1,0:T(8,128)(2,1)S(1)} %collective-permute-done.3.refs_0_, bf16[432,512]{1,0:T(8,128)(2,1)S(1)} %collective-permute-done.2.refs_1_, bf16[432,512]{1,0:T(8,128)(2,1)S(1)} %collective-permute-done.5.refs_2_, ...), custom_call_target="tpu_custom_call" | custom-call | flops 1811939328 | bytes 4063232 | tf_op jit(solution)/shard_map/conv_blocks/pallas_call | solution.py:165
  50.6 2.2 %collective-permute-start.17 = (bf16[2,256,512]{2,1,0:T(8,128)(2,1)S(1)}, bf16[2,256,512]{2,1,0:T(8,128)(2,1)S(1)}, u32[]{:S(2)}, u32[]{:S(2)}) collective-permute-start(bf16[2,256,512]{2,1,0:T(8,128)(2,1)S(1)} %get-tuple-element.31), channel_id=1, source_target_pairs={{0,4},{4,0},{8,12},{12,8},{1,5},{5,1},{9,13},{13,9},{2,6},{6,2},{1... | collective-permute-start | bytes 1572872 | tf_op jit(solution)/shard_map/ppermute | solution.py:312
  52.8 2.3 %conv_blocks.6 = bf16[2,256,512]{2,1,0:T(8,128)(2,1)S(1)} custom-call(s32[1]{0:T(128)} %bitcast.where_ref, bf16[4,272,128]{2,1,0:T(8,128)(2,1)S(1)} %collective-permute-done.3.refs_0_, bf16[272,128]{1,0:T(8,128)(2,1)S(1)} %bitcast.29, bf16[272,128]{1,0:T(8,128)(2,1)S(1)} %bitcast.28, bf16[3456,512]{1,0:T(8,128)(2,1)S(1)} %get-tuple-element.35.refs_3_.refs_7_, ...), custom_call_target="tpu_custom_call" | custom-call | flops 1811939328 | bytes 4063232 | tf_op jit(solution)/shard_map/conv_blocks/pallas_call | solution.py:165
  55.2 7.0 %collective-permute-done.4.refs_4_ = bf16[4,272,128]{2,1,0:T(8,128)(2,1)S(1)} collective-permute-done((bf16[4,272,128]{2,1,0:T(8,128)(2,1)S(1)}, bf16[4,272,128]{2,1,0:T(8,128)(2,1)S(1)}, u32[]{:S(2)}, u32[]{:S(2)}) %collective-permute-start.4) | collective-permute-done | bytes 278560 | tf_op jit(solution)/shard_map/ppermute | solution.py:301
  62.2 0.8 %collective-permute-start.15 = (bf16[1,1,272,128]{3,2,1,0:T(8,128)(2,1)S(1)}, bf16[1,1,272,128]{3,2,1,0:T(8,128)(2,1)S(1)}, u32[]{:S(2)}, u32[]{:S(2)}) collective-permute-start(bf16[1,1,272,128]{3,2,1,0:T(8,128)(2,1)S(1)} %get-tuple-element.44), channel_id=1, source_target_pairs={{1,2},{2,1},{5,6},{6,5},{9,10},{10,9},{13,14},{14,13},{17,18},{18,... | collective-permute-start | bytes 208904 | tf_op jit(solution)/shard_map/ppermute | solution.py:261
  63.0 3.1 %collective-permute-start.14 = (bf16[1,1,272,128]{3,2,1,0:T(8,128)(2,1)S(1)}, bf16[1,1,272,128]{3,2,1,0:T(8,128)(2,1)S(1)}, u32[]{:S(2)}, u32[]{:S(2)}) collective-permute-start(bf16[1,1,272,128]{3,2,1,0:T(8,128)(2,1)S(1)} %get-tuple-element.45), channel_id=1, source_target_pairs={{0,1},{1,0},{2,3},{3,2},{4,5},{5,4},{6,7},{7,6},{8,9},{9,8},{10,11... | collective-permute-start | bytes 208904 | tf_op jit(solution)/shard_map/ppermute | solution.py:258
  66.2 0.9 %collective-permute-done.14 = bf16[1,1,272,128]{3,2,1,0:T(8,128)(2,1)S(1)} collective-permute-done((bf16[1,1,272,128]{3,2,1,0:T(8,128)(2,1)S(1)}, bf16[1,1,272,128]{3,2,1,0:T(8,128)(2,1)S(1)}, u32[]{:S(2)}, u32[]{:S(2)}) %collective-permute-start.14) | collective-permute-done | bytes 69664 | tf_op jit(solution)/shard_map/ppermute | solution.py:258
  67.1 8.8 %conv_blocks.7.mine_ref = f32[4,256,512]{2,1,0:T(8,128)S(1)} custom-call(s32[1]{0:T(128)} %bitcast.where_ref, bf16[4,272,128]{2,1,0:T(8,128)(2,1)S(1)} %get-tuple-element.43.refs_0_, bf16[272,128]{1,0:T(8,128)(2,1)S(1)} %get-tuple-element.51.refs_1_, bf16[272,128]{1,0:T(8,128)(2,1)S(1)} %get-tuple-element.49.refs_2_, bf16[3456,512]{1,0:T(8,128)(2,1)S(1)} %bitcast.21, ...), custom_call_target="tpu_custom_call" | custom-call | flops 1811939328 | bytes 2031616 | tf_op jit(solution)/shard_map/conv_blocks/pallas_call | solution.py:165
  75.9 2.8 %down_blocks.2.refs_0_ = bf16[4,256,8,256]{3,2,1,0:T(8,128)(2,1)} custom-call(f32[4,256,512]{2,1,0:T(8,128)S(1)} %conv_blocks.7.mine_ref, bf16[2,256,512]{2,1,0:T(8,128)(2,1)S(1)} %collective-permute-done.17.theirs_ref, f32[4,256,512]{2,1,0:T(8,128)S(1)} %fusion.3.slope_ref, bf16[8,256,512]{2,1,0:T(8,128)(2,1)S(1)} %copy-done), custom_call_target="tpu_custom_call" | custom-call | flops 1073741824 | bytes 4718592 | tf_op jit(solution)/shard_map/down_blocks/pallas_call | solution.py:217
  78.8 2.5 %collective-permute-done.16.theirs_ref = bf16[2,256,512]{2,1,0:T(8,128)(2,1)S(1)} collective-permute-done((bf16[2,256,512]{2,1,0:T(8,128)(2,1)S(1)}, bf16[2,256,512]{2,1,0:T(8,128)(2,1)S(1)}, u32[]{:S(2)}, u32[]{:S(2)}) %collective-permute-start.16) | collective-permute-done | bytes 524320 | tf_op jit(solution)/shard_map/ppermute | solution.py:322
  81.3 2.8 %down_blocks.3 = bf16[4,256,8,256]{3,2,1,0:T(8,128)(2,1)} custom-call(f32[4,256,512]{2,1,0:T(8,128)S(1)} %conv_blocks.7.mine_ref, bf16[2,256,512]{2,1,0:T(8,128)(2,1)S(1)} %collective-permute-done.16.theirs_ref, f32[4,256,512]{2,1,0:T(8,128)S(1)} %fusion.3.slope_ref, bf16[8,256,512]{2,1,0:T(8,128)(2,1)S(1)} %copy-done, ...), custom_call_target="tpu_custom_call", output_to_operand_aliasing={{}: (4, {})} | custom-call | flops 1073741824 | bytes 4718592 | tf_op jit(solution)/shard_map/down_blocks/pallas_call | solution.py:217
  (34 shorter events, 3.8 us)
Async XLA Ops:
  1.0 23.7 %collective-permute-start.2 = (bf16[432,512]{1,0:T(8,128)(2,1)S(1)}, bf16[432,512]{1,0:T(8,128)(2,1)S(1)}, u32[]{:S(2)}, u32[]{:S(2)}) collective-permute-start(bf16[432,512]{1,0:T(8,128)(2,1)S(1)} %constant_dynamic-slice_fusion), channel_id=1, source_target_pairs={{0,8},{4,12},{8,0},{12,4},{1,9},{5,13},{9,1},{13,5},{2,10},{6,14},... | collective-permute-start | bytes 1327112 | tf_op jit(solution)/shard_map/ppermute | solution.py:269
  7.1 1.2 %copy-start.2 = (bf16[4,256,512]{2,1,0:T(8,128)(2,1)S(1)}, bf16[4,256,512]{2,1,0:T(8,128)(2,1)}, u32[]{:S(2)}) copy-start(bf16[4,256,512]{2,1,0:T(8,128)(2,1)} %param.6) | copy-start | bytes 3145732
  7.3 2.2 %copy-start.1 = (bf16[27,128,512]{2,1,0:T(8,128)(2,1)S(1)}, bf16[27,128,512]{2,1,0:T(8,128)(2,1)}, u32[]{:S(2)}) copy-start(bf16[27,128,512]{2,1,0:T(8,128)(2,1)} %param.5) | copy-start | bytes 10616836
  7.3 1.8 %collective-permute-start = (bf16[2,1,272,128]{3,2,1,0:T(8,128)(2,1)S(1)}, bf16[2,1,272,128]{3,2,1,0:T(8,128)(2,1)S(1)}, u32[]{:S(2)}, u32[]{:S(2)}) collective-permute-start(bf16[2,1,272,128]{3,2,1,0:T(8,128)(2,1)S(1)} %broadcast_select_fusion.1), channel_id=1, source_target_pairs={{0,1},{1,0},{2,3},{3,2},{4,5},{5,4},{6,7},{7,6},{8,9},{9,8},{10,11... | collective-permute-start | bytes 417800 | tf_op jit(solution)/shard_map/ppermute | solution.py:258
  7.4 1.8 %collective-permute-start.1 = (bf16[2,1,272,128]{3,2,1,0:T(8,128)(2,1)S(1)}, bf16[2,1,272,128]{3,2,1,0:T(8,128)(2,1)S(1)}, u32[]{:S(2)}, u32[]{:S(2)}) collective-permute-start(bf16[2,1,272,128]{3,2,1,0:T(8,128)(2,1)S(1)} %get-tuple-element.37), channel_id=1, source_target_pairs={{1,2},{2,1},{5,6},{6,5},{9,10},{10,9},{13,14},{14,13},{17,18},{18,... | collective-permute-start | bytes 417800 | tf_op jit(solution)/shard_map/ppermute | solution.py:261
  24.8 12.4 %collective-permute-start.5 = (bf16[432,512]{1,0:T(8,128)(2,1)S(1)}, bf16[432,512]{1,0:T(8,128)(2,1)S(1)}, u32[]{:S(2)}, u32[]{:S(2)}) collective-permute-start(bf16[432,512]{1,0:T(8,128)(2,1)S(1)} %collective-permute-done.2.refs_1_), channel_id=1, source_target_pairs={{0,2},{1,17},{2,0},{3,19},{16,18},{17,1},{18,16},{19,3},{4,6},{5,2... | collective-permute-start | bytes 1327112 | tf_op jit(solution)/shard_map/ppermute | solution.py:295
  26.3 14.2 %collective-permute-start.3 = (bf16[4,272,128]{2,1,0:T(8,128)(2,1)S(1)}, bf16[4,272,128]{2,1,0:T(8,128)(2,1)S(1)}, u32[]{:S(2)}, u32[]{:S(2)}) collective-permute-start(bf16[4,272,128]{2,1,0:T(8,128)(2,1)S(1)} %get-tuple-element.24), channel_id=1, source_target_pairs={{0,8},{4,12},{8,0},{12,4},{1,9},{5,13},{9,1},{13,5},{2,10},{6,14},... | collective-permute-start | bytes 835592 | tf_op jit(solution)/shard_map/ppermute | solution.py:294
  26.3 14.9 %collective-permute-start.6 = (bf16[432,512]{1,0:T(8,128)(2,1)S(1)}, bf16[432,512]{1,0:T(8,128)(2,1)S(1)}, u32[]{:S(2)}, u32[]{:S(2)}) collective-permute-start(bf16[432,512]{1,0:T(8,128)(2,1)S(1)} %collective-permute-done.2.refs_1_), channel_id=1, source_target_pairs={{0,16},{1,3},{2,18},{3,1},{16,0},{17,19},{18,2},{19,17},{4,20},{5,... | collective-permute-start | bytes 1327112 | tf_op jit(solution)/shard_map/ppermute | solution.py:296
  27.9 18.2 %collective-permute-start.8 = (bf16[432,512]{1,0:T(8,128)(2,1)S(1)}, bf16[432,512]{1,0:T(8,128)(2,1)S(1)}, u32[]{:S(2)}, u32[]{:S(2)}) collective-permute-start(bf16[432,512]{1,0:T(8,128)(2,1)S(1)} %collective-permute-done.2.refs_1_), channel_id=1, source_target_pairs={{0,1},{1,0},{2,3},{3,2},{4,5},{5,4},{6,7},{7,6},{8,9},{9,8},{10,11... | collective-permute-start | bytes 1327112 | tf_op jit(solution)/shard_map/ppermute | solution.py:298
  37.1 8.9 %collective-permute-start.9 = (bf16[432,512]{1,0:T(8,128)(2,1)S(1)}, bf16[432,512]{1,0:T(8,128)(2,1)S(1)}, u32[]{:S(2)}, u32[]{:S(2)}) collective-permute-start(bf16[432,512]{1,0:T(8,128)(2,1)S(1)} %collective-permute-done.5.refs_2_), channel_id=1, source_target_pairs={{0,1},{1,0},{2,3},{3,2},{4,5},{5,4},{6,7},{7,6},{8,9},{9,8},{10,11... | collective-permute-start | bytes 1327112 | tf_op jit(solution)/shard_map/ppermute | solution.py:298
  37.2 8.9 %collective-permute-start.7 = (bf16[432,512]{1,0:T(8,128)(2,1)S(1)}, bf16[432,512]{1,0:T(8,128)(2,1)S(1)}, u32[]{:S(2)}, u32[]{:S(2)}) collective-permute-start(bf16[432,512]{1,0:T(8,128)(2,1)S(1)} %collective-permute-done.5.refs_2_), channel_id=1, source_target_pairs={{0,16},{1,3},{2,18},{3,1},{16,0},{17,19},{18,2},{19,17},{4,20},{5,... | collective-permute-start | bytes 1327112 | tf_op jit(solution)/shard_map/ppermute | solution.py:297
  40.5 3.6 %collective-permute-start.11 = (bf16[1,1,272,128]{3,2,1,0:T(8,128)(2,1)S(1)}, bf16[1,1,272,128]{3,2,1,0:T(8,128)(2,1)S(1)}, u32[]{:S(2)}, u32[]{:S(2)}) collective-permute-start(bf16[1,1,272,128]{3,2,1,0:T(8,128)(2,1)S(1)} %get-tuple-element.46), channel_id=1, source_target_pairs={{1,2},{2,1},{5,6},{6,5},{9,10},{10,9},{13,14},{14,13},{17,18},{18,... | collective-permute-start | bytes 208904 | tf_op jit(solution)/shard_map/ppermute | solution.py:261
  41.2 4.8 %collective-permute-start.10 = (bf16[1,1,272,128]{3,2,1,0:T(8,128)(2,1)S(1)}, bf16[1,1,272,128]{3,2,1,0:T(8,128)(2,1)S(1)}, u32[]{:S(2)}, u32[]{:S(2)}) collective-permute-start(bf16[1,1,272,128]{3,2,1,0:T(8,128)(2,1)S(1)} %get-tuple-element.47), channel_id=1, source_target_pairs={{0,1},{1,0},{2,3},{3,2},{4,5},{5,4},{6,7},{7,6},{8,9},{9,8},{10,11... | collective-permute-start | bytes 208904 | tf_op jit(solution)/shard_map/ppermute | solution.py:258
  44.1 3.3 %collective-permute-start.12 = (bf16[432,512]{1,0:T(8,128)(2,1)S(1)}, bf16[432,512]{1,0:T(8,128)(2,1)S(1)}, u32[]{:S(2)}, u32[]{:S(2)}) collective-permute-start(bf16[432,512]{1,0:T(8,128)(2,1)S(1)} %collective-permute-done.6.refs_3_), channel_id=1, source_target_pairs={{0,1},{1,0},{2,3},{3,2},{4,5},{5,4},{6,7},{7,6},{8,9},{9,8},{10,11... | collective-permute-start | bytes 1327112 | tf_op jit(solution)/shard_map/ppermute | solution.py:300
  46.0 2.0 %collective-permute-start.13 = (bf16[432,512]{1,0:T(8,128)(2,1)S(1)}, bf16[432,512]{1,0:T(8,128)(2,1)S(1)}, u32[]{:S(2)}, u32[]{:S(2)}) collective-permute-start(bf16[432,512]{1,0:T(8,128)(2,1)S(1)} %collective-permute-done.7.refs_4_), channel_id=1, source_target_pairs={{0,1},{1,0},{2,3},{3,2},{4,5},{5,4},{6,7},{7,6},{8,9},{9,8},{10,11... | collective-permute-start | bytes 1327112 | tf_op jit(solution)/shard_map/ppermute | solution.py:306
  46.1 16.0 %collective-permute-start.4 = (bf16[4,272,128]{2,1,0:T(8,128)(2,1)S(1)}, bf16[4,272,128]{2,1,0:T(8,128)(2,1)S(1)}, u32[]{:S(2)}, u32[]{:S(2)}) collective-permute-start(bf16[4,272,128]{2,1,0:T(8,128)(2,1)S(1)} %get-tuple-element.25), channel_id=1, source_target_pairs={{0,8},{4,12},{8,0},{12,4},{1,9},{5,13},{9,1},{13,5},{2,10},{6,14},... | collective-permute-start | bytes 835592 | tf_op jit(solution)/shard_map/ppermute | solution.py:301
  50.6 25.4 %collective-permute-start.17 = (bf16[2,256,512]{2,1,0:T(8,128)(2,1)S(1)}, bf16[2,256,512]{2,1,0:T(8,128)(2,1)S(1)}, u32[]{:S(2)}, u32[]{:S(2)}) collective-permute-start(bf16[2,256,512]{2,1,0:T(8,128)(2,1)S(1)} %get-tuple-element.31), channel_id=1, source_target_pairs={{0,4},{4,0},{8,12},{12,8},{1,5},{5,1},{9,13},{13,9},{2,6},{6,2},{1... | collective-permute-start | bytes 1572872 | tf_op jit(solution)/shard_map/ppermute | solution.py:312
  55.1 26.2 %collective-permute-start.16 = (bf16[2,256,512]{2,1,0:T(8,128)(2,1)S(1)}, bf16[2,256,512]{2,1,0:T(8,128)(2,1)S(1)}, u32[]{:S(2)}, u32[]{:S(2)}) collective-permute-start(bf16[2,256,512]{2,1,0:T(8,128)(2,1)S(1)} %conv_blocks.6), channel_id=1, source_target_pairs={{0,4},{4,0},{8,12},{12,8},{1,5},{5,1},{9,13},{13,9},{2,6},{6,2},{1... | collective-permute-start | bytes 1572872 | tf_op jit(solution)/shard_map/ppermute | solution.py:322
  62.2 4.0 %collective-permute-start.15 = (bf16[1,1,272,128]{3,2,1,0:T(8,128)(2,1)S(1)}, bf16[1,1,272,128]{3,2,1,0:T(8,128)(2,1)S(1)}, u32[]{:S(2)}, u32[]{:S(2)}) collective-permute-start(bf16[1,1,272,128]{3,2,1,0:T(8,128)(2,1)S(1)} %get-tuple-element.44), channel_id=1, source_target_pairs={{1,2},{2,1},{5,6},{6,5},{9,10},{10,9},{13,14},{14,13},{17,18},{18,... | collective-permute-start | bytes 208904 | tf_op jit(solution)/shard_map/ppermute | solution.py:261
  63.0 4.0 %collective-permute-start.14 = (bf16[1,1,272,128]{3,2,1,0:T(8,128)(2,1)S(1)}, bf16[1,1,272,128]{3,2,1,0:T(8,128)(2,1)S(1)}, u32[]{:S(2)}, u32[]{:S(2)}) collective-permute-start(bf16[1,1,272,128]{3,2,1,0:T(8,128)(2,1)S(1)} %get-tuple-element.45), channel_id=1, source_target_pairs={{0,1},{1,0},{2,3},{3,2},{4,5},{5,4},{6,7},{7,6},{8,9},{9,8},{10,11... | collective-permute-start | bytes 208904 | tf_op jit(solution)/shard_map/ppermute | solution.py:258
  67.1 8.9 %copy-start = (bf16[8,256,512]{2,1,0:T(8,128)(2,1)S(1)}, bf16[8,256,512]{2,1,0:T(8,128)(2,1)}, u32[]{:S(2)}) copy-start(bf16[8,256,512]{2,1,0:T(8,128)(2,1)} %weight_ref.3) | copy-start | bytes 6291460

commit v5 on v4

--- a/solution.py
+++ b/solution.py
@@ -12,7 +12,8 @@
 PLANAR = ("groups", "space", "pair")
 SLAB = ("space", "pair")
 LIMIT = 20
-PART = (1, 1, 1, 4)
+PART = (1, 1, 1, 2)
+GROUPS = ((1,), (2, 0), (3,))
 
 
 def gelu_slope(values):
@@ -183,10 +184,12 @@
     )(*operands)
 
 
-def down_kernel(mine_ref, theirs_ref, slope_ref, weight_ref, *refs):
+def down_kernel(mine_ref, theirs_ref, slope_ref, weight_ref, *refs, first, step):
     out_ref = refs[-1]
-    act = (mine_ref[0] + theirs_ref[0].astype(jnp.float32)).astype(jnp.bfloat16)
-    pre = (act.astype(jnp.float32) * slope_ref[0]).astype(jnp.bfloat16)
+    at = pl.program_id(0)
+    plane = first + step * at
+    act = (mine_ref[plane] + theirs_ref[at].astype(jnp.float32)).astype(jnp.bfloat16)
+    pre = (act.astype(jnp.float32) * slope_ref[plane]).astype(jnp.bfloat16)
     grown = [
         lax.dot_general(
             pre,
@@ -202,20 +205,16 @@
 def down_blocks(mine, theirs, slope, weight, planes, partly):
     extent, cells, wide = slope.shape
     offsets, fine, _ = weight.shape
-    first, step = planes[0], planes[1] - planes[0]
-    own_plane = pl.BlockSpec((1, cells, wide), lambda i: (first + step * i, 0, 0))
-    in_specs = [
-        own_plane,
-        pl.BlockSpec((1, cells, wide), lambda i: (i, 0, 0)),
-        own_plane,
-        pl.BlockSpec((offsets, fine, wide), lambda i: (0, 0, 0)),
-    ]
+    first = planes[0]
+    step = planes[1] - first if len(planes) > 1 else 0
+    on_chip = pl.BlockSpec(memory_space=pltpu.VMEM)
+    in_specs = [on_chip] * 4
     operands = [mine, theirs, slope, weight]
     if partly is not None:
         in_specs.append(pl.BlockSpec(memory_space=pl.ANY))
         operands.append(partly)
     return pl.pallas_call(
-        down_kernel,
+        functools.partial(down_kernel, first=first, step=step),
         grid=(len(planes),),
         in_specs=in_specs,
         out_specs=pl.BlockSpec(
@@ -278,18 +277,21 @@
     where = jnp.reshape(q, (1,)).astype(jnp.int32)
     own_one, own_two = window(k ^ 1), window(k)
     own_inner, own_outer = margins(jnp.stack([own_one, own_two]))
-    every, inside, edges = (0, 1, 2, 3), (1, 2), (0, 3)
-    begun = conv_blocks(
-        where,
-        [((own_one, own_inner[0, 0], own_outer[0, 0]), [table])],
-        None,
-        every,
-        jnp.float32,
-        PART[0],
-    )[0]
+    every = (0, 1, 2, 3)
+    begun, kept = [
+        conv_blocks(
+            where,
+            [((cells_of, own_inner[n, 0], own_outer[n, 0]), [table])],
+            None,
+            every,
+            jnp.float32,
+            PART[0],
+        )[0]
+        for n, cells_of in enumerate((own_one, own_two))
+    ]
     slope = gelu_slope(after(pre_act, piece).astype(jnp.float32))
     got, window_one, window_two = lax.optimization_barrier(
-        (got, window(k ^ 3), window(k ^ 2), begun, slope)
+        (got, window(k ^ 3), window(k ^ 2), begun, kept, slope)
     )[:3]
     far_one = lax.ppermute(window_one, "chan", far)
     got_a = lax.ppermute(got, PLANAR, first)
@@ -306,35 +308,25 @@
     pair_c = lax.ppermute(got_c, "pair", other)
     pieces = [got, got_a, got_b, got_c, pair_got, pair_a, pair_b, pair_c]
 
-    sent_inside, far_table = conv_blocks(
-        where, [((far_one,), pieces)], begun, inside, jnp.bfloat16, PART[1]
-    )
-    theirs_inside = lax.ppermute(sent_inside, "chan", near)
-    far_one = after(far_one, sent_inside)
-    sent_edges = conv_blocks(
-        where,
-        [((far_one, one_inner[0, 0], one_outer[0, 0]), [far_table])],
-        begun,
-        edges,
-        jnp.bfloat16,
-        PART[2],
-    )[0]
-    theirs_edges = lax.ppermute(sent_edges, "chan", near)
-    far_two = after(far_two, sent_edges)
+    sent, far_table = conv_blocks(
+        where, [((far_one,), pieces)], begun, GROUPS[0], jnp.bfloat16, PART[1]
+    )
+    theirs = [lax.ppermute(sent, "chan", near)]
+    for planes in GROUPS[1:]:
+        far_one = after(far_one, sent)
+        one = (far_one, one_inner[0, 0], one_outer[0, 0])
+        sent = conv_blocks(
+            where, [(one, [far_table])], begun, planes, jnp.bfloat16, PART[2]
+        )[0]
+        theirs.append(lax.ppermute(sent, "chan", near))
+    far_two = after(far_two, sent)
     two_inner, two_outer = margins(far_two[None])
-    kept = conv_blocks(
-        where,
-        [
-            ((own_two, own_inner[1, 0], own_outer[1, 0]), [table]),
-            ((far_two, two_inner[0, 0], two_outer[0, 0]), [far_table]),
-        ],
-        None,
-        every,
-        jnp.float32,
-        PART[3],
-    )[0]
-    partly = down_blocks(kept, theirs_inside, slope, down_weight, inside, None)
-    return down_blocks(kept, theirs_edges, slope, down_weight, edges, partly)
+    two = (far_two, two_inner[0, 0], two_outer[0, 0])
+    kept = conv_blocks(where, [(two, [far_table])], kept, every, jnp.float32, PART[3])[0]
+    result = None
+    for planes, part in zip(GROUPS, theirs):
+        result = down_blocks(kept, part, slope, down_weight, planes, result)
+    return result
 
 
 def solution(mesh):

time: 84.3 us -> 82.5 us (0.979)
  waiting for transfers between devices: 35.3 us -> 32.4 us
  Pallas kernels: 23.5 us -> 24.6 us
    ppermute x1, waiting for transfers between devices: 11 us -> 6.71 us  [two_level_body(): got = lax.ppermute(piece, 'chan', far)]
    ppermute x2 -> x3, waiting for transfers between devices: 2.55 us -> 4.21 us  [the longest x2 4.21 us: two_level_body(): theirs.append(lax.ppermute(sent, 'chan', near))]
    pallas_call x2 -> x3, Pallas kernels: 5.65 us -> 6.63 us  [down_blocks(): pl.pallas_call(functools.partial(down_kernel, first=first, step=step), gr...]
    pallas_call x4 -> x6, Pallas kernels: 17.9 us -> 17.9 us  [conv_blocks(): pl.pallas_call(functools.partial(conv_kernel, sources=[(len(v[0]) > 1, le...]
    ppermute x2 -> x3, starting transfers between devices: 2.32 us -> 2.32 us  [the longest x1 2.24 us: two_level_body(): theirs = [lax.ppermute(sent, 'chan', near)]]
  transfers between devices with their start and end apart: 18 -> 19, of which waited for: 8 -> 9; matrix products, arithmetic and copies ran while one was open for 4% -> 4% of each run, Pallas kernels for 25% -> 28%
where the time goes in v5:
time: 82.5 us; the launch traced here: 82.2 us
  waiting for transfers between devices  32.4 us (39%)
  Pallas kernels  24.6 us (30%)
  starting transfers between devices  20.7 us (25%)
  local copies, waits for them, and re-layouts  3.48 us (4%)
  other arithmetic  0.9 us (1%)
    pallas_call x6, Pallas kernels, conv_blocks(): pl.pallas_call(functools.partial(conv_kernel, sources=[(len(v[0]) > 1, le...  17.9 us
    ppermute x1, waiting for transfers between devices, two_level_body(): got_a = lax.ppermute(got, PLANAR, first)  9.28 us
    ppermute x1, waiting for transfers between devices, two_level_body(): far_two = lax.ppermute(after(window_two, far_one), 'chan', far)  6.78 us
    ppermute x1, waiting for transfers between devices, two_level_body(): got = lax.ppermute(piece, 'chan', far)  6.71 us
    pallas_call x3, Pallas kernels, down_blocks(): pl.pallas_call(functools.partial(down_kernel, first=first, step=step), gr...  6.63 us
    ppermute x3, starting transfers between devices, margins(): lax.ppermute(jnp.where(lax.axis_index('pair') == 0, tail, head), 'pair',...  6.09 us
    ppermute x2, waiting for transfers between devices, two_level_body(): theirs.append(lax.ppermute(sent, 'chan', near))  4.21 us
    ppermute x1, starting transfers between devices, two_level_body(): got = lax.ppermute(piece, 'chan', far)  4.1 us
  transfers between devices with their start and end apart: 19, of which 9 were waited for; matrix products, arithmetic and copies ran while one was open for 4% of the time, Pallas kernels for 28%

profile of v5, /device:TPU:0, one launch (start us, length us, event | category | flops | bytes accessed | tf_op | source)
XLA Modules:
  0.0 82.2 jit_solution(18119812661639573225)
XLA Ops:
  1.0 4.1 %collective-permute-start = (bf16[432,512]{1,0:T(8,128)(2,1)S(1)}, bf16[432,512]{1,0:T(8,128)(2,1)S(1)}, u32[]{:S(2)}, u32[]{:S(2)}) collective-permute-start(bf16[432,512]{1,0:T(8,128)(2,1)S(1)} %constant_dynamic-slice_fusion), channel_id=1, source_target_pairs={{0,8},{4,12},{8,0},{12,4},{1,9},{5,13},{9,1},{13,5},{2,10},{6,14},... | collective-permute-start | bytes 1327112 | tf_op jit(solution)/shard_map/ppermute | solution.py:268
  5.1 1.9 %copy.7 = bf16[128,4,1024]{0,2,1:T(8,128)(2,1)S(1)} copy(bf16[128,4,1024]{2,1,0:T(4,128)(2,1)} %param.4) | data formatting | bytes 2097152 | tf_op jit(solution)/shard_map/optimization_barrier | solution.py:253
  9.4 4.3 %conv_blocks.7.refs_4_ = f32[4,256,512]{2,1,0:T(8,128)S(1)} custom-call(s32[1]{0:T(128)} %bitcast.where_ref, bf16[4,272,128]{2,1,0:T(8,128)(2,1)S(1)} %get-tuple-element.42.refs_0_, bf16[272,128]{1,0:T(8,128)(2,1)S(1)} %get-tuple-element.52.refs_1_, bf16[272,128]{1,0:T(8,128)(2,1)S(1)} %get-tuple-element.50.refs_2_, bf16[3456,512]{1,0:T(8,128)(2,1)S(1)} %bitcast.30), custom_call_target="tpu_custom_call" | custom-call | flops 3623878656 | bytes 4587520 | tf_op jit(solution)/shard_map/conv_blocks/pallas_call | solution.py:166
  13.8 4.3 %conv_blocks.6.refs_9_.refs_4_ = f32[4,256,512]{2,1,0:T(8,128)S(1)} custom-call(s32[1]{0:T(128)} %bitcast.where_ref, bf16[4,272,128]{2,1,0:T(8,128)(2,1)S(1)} %get-tuple-element.44.refs_0_, bf16[272,128]{1,0:T(8,128)(2,1)S(1)} %get-tuple-element.53.refs_1_, bf16[272,128]{1,0:T(8,128)(2,1)S(1)} %get-tuple-element.51.refs_2_, bf16[3456,512]{1,0:T(8,128)(2,1)S(1)} %bitcast.31), custom_call_target="tpu_custom_call" | custom-call | flops 3623878656 | bytes 4587520 | tf_op jit(solution)/shard_map/conv_blocks/pallas_call | solution.py:166
  18.1 6.7 %collective-permute-done.refs_1_ = bf16[432,512]{1,0:T(8,128)(2,1)S(1)} collective-permute-done((bf16[432,512]{1,0:T(8,128)(2,1)S(1)}, bf16[432,512]{1,0:T(8,128)(2,1)S(1)}, u32[]{:S(2)}, u32[]{:S(2)}) %collective-permute-start) | collective-permute-done | bytes 442400 | tf_op jit(solution)/shard_map/ppermute | solution.py:268
  24.8 1.5 %collective-permute-start.5 = (bf16[432,512]{1,0:T(8,128)(2,1)S(1)}, bf16[432,512]{1,0:T(8,128)(2,1)S(1)}, u32[]{:S(2)}, u32[]{:S(2)}) collective-permute-start(bf16[432,512]{1,0:T(8,128)(2,1)S(1)} %collective-permute-done.refs_1_), channel_id=1, source_target_pairs={{0,2},{1,17},{2,0},{3,19},{16,18},{17,1},{18,16},{19,3},{4,6},{5,2... | collective-permute-start | bytes 1327112 | tf_op jit(solution)/shard_map/ppermute | solution.py:297
  26.3 1.5 %collective-permute-start.6 = (bf16[432,512]{1,0:T(8,128)(2,1)S(1)}, bf16[432,512]{1,0:T(8,128)(2,1)S(1)}, u32[]{:S(2)}, u32[]{:S(2)}) collective-permute-start(bf16[432,512]{1,0:T(8,128)(2,1)S(1)} %collective-permute-done.refs_1_), channel_id=1, source_target_pairs={{0,16},{1,3},{2,18},{3,1},{16,0},{17,19},{18,2},{19,17},{4,20},{5,... | collective-permute-start | bytes 1327112 | tf_op jit(solution)/shard_map/ppermute | solution.py:298
  27.9 9.3 %collective-permute-done.5.refs_2_ = bf16[432,512]{1,0:T(8,128)(2,1)S(1)} collective-permute-done((bf16[432,512]{1,0:T(8,128)(2,1)S(1)}, bf16[432,512]{1,0:T(8,128)(2,1)S(1)}, u32[]{:S(2)}, u32[]{:S(2)}) %collective-permute-start.5) | collective-permute-done | bytes 442400 | tf_op jit(solution)/shard_map/ppermute | solution.py:297
  37.9 2.6 %collective-permute-done.3.refs_0_ = bf16[4,272,128]{2,1,0:T(8,128)(2,1)S(1)} collective-permute-done((bf16[4,272,128]{2,1,0:T(8,128)(2,1)S(1)}, bf16[4,272,128]{2,1,0:T(8,128)(2,1)S(1)}, u32[]{:S(2)}, u32[]{:S(2)}) %collective-permute-start.3) | collective-permute-done | bytes 278560 | tf_op jit(solution)/shard_map/ppermute | solution.py:296
  41.2 2.9 %collective-permute-start.10 = (bf16[1,1,272,128]{3,2,1,0:T(8,128)(2,1)S(1)}, bf16[1,1,272,128]{3,2,1,0:T(8,128)(2,1)S(1)}, u32[]{:S(2)}, u32[]{:S(2)}) collective-permute-start(bf16[1,1,272,128]{3,2,1,0:T(8,128)(2,1)S(1)} %get-tuple-element.49), channel_id=1, source_target_pairs={{0,1},{1,0},{2,3},{3,2},{4,5},{5,4},{6,7},{7,6},{8,9},{9,8},{10,11... | collective-permute-start | bytes 208904 | tf_op jit(solution)/shard_map/ppermute | solution.py:257
  44.1 1.9 %collective-permute-start.12 = (bf16[432,512]{1,0:T(8,128)(2,1)S(1)}, bf16[432,512]{1,0:T(8,128)(2,1)S(1)}, u32[]{:S(2)}, u32[]{:S(2)}) collective-permute-start(bf16[432,512]{1,0:T(8,128)(2,1)S(1)} %collective-permute-done.6.refs_3_), channel_id=1, source_target_pairs={{0,1},{1,0},{2,3},{3,2},{4,5},{5,4},{6,7},{7,6},{8,9},{9,8},{10,11... | collective-permute-start | bytes 1327112 | tf_op jit(solution)/shard_map/ppermute | solution.py:302
  46.2 1.2 %collective-permute-done.12.refs_7_ = bf16[432,512]{1,0:T(8,128)(2,1)S(1)} collective-permute-done((bf16[432,512]{1,0:T(8,128)(2,1)S(1)}, bf16[432,512]{1,0:T(8,128)(2,1)S(1)}, u32[]{:S(2)}, u32[]{:S(2)}) %collective-permute-start.12) | collective-permute-done | bytes 442400 | tf_op jit(solution)/shard_map/ppermute | solution.py:302
  48.1 1.5 %conv_blocks.8 = (bf16[1,256,512]{2,1,0:T(8,128)(2,1)S(1)}, bf16[3456,512]{1,0:T(8,128)(2,1)S(1)}) custom-call(s32[1]{0:T(128)} %bitcast.where_ref, bf16[4,272,128]{2,1,0:T(8,128)(2,1)S(1)} %collective-permute-done.3.refs_0_, bf16[432,512]{1,0:T(8,128)(2,1)S(1)} %collective-permute-done.refs_1_, bf16[432,512]{1,0:T(8,128)(2,1)S(1)} %collective-permute-done.5.refs_2_, ...), custom_call_target="tpu_custom_call" | custom-call | flops 905969664 | bytes 3801088 | tf_op jit(solution)/shard_map/conv_blocks/pallas_call | solution.py:166
  49.6 2.2 %collective-permute-start.18 = (bf16[1,256,512]{2,1,0:T(8,128)(2,1)S(1)}, bf16[1,256,512]{2,1,0:T(8,128)(2,1)S(1)}, u32[]{:S(2)}, u32[]{:S(2)}) collective-permute-start(bf16[1,256,512]{2,1,0:T(8,128)(2,1)S(1)} %get-tuple-element.32), channel_id=1, source_target_pairs={{0,4},{4,0},{8,12},{12,8},{1,5},{5,1},{9,13},{13,9},{2,6},{6,2},{1... | collective-permute-start | bytes 786440 | tf_op jit(solution)/shard_map/ppermute | solution.py:314
  51.8 2.3 %conv_blocks.9 = bf16[2,256,512]{2,1,0:T(8,128)(2,1)S(1)} custom-call(s32[1]{0:T(128)} %bitcast.where_ref, bf16[4,272,128]{2,1,0:T(8,128)(2,1)S(1)} %collective-permute-done.3.refs_0_, bf16[272,128]{1,0:T(8,128)(2,1)S(1)} %bitcast.25, bf16[272,128]{1,0:T(8,128)(2,1)S(1)} %bitcast.23, bf16[3456,512]{1,0:T(8,128)(2,1)S(1)} %get-tuple-element.36.refs_3_, ...), custom_call_target="tpu_custom_call" | custom-call | flops 1811939328 | bytes 4063232 | tf_op jit(solution)/shard_map/conv_blocks/pallas_call | solution.py:166
  54.1 1.2 %conv_blocks.10 = bf16[1,256,512]{2,1,0:T(8,128)(2,1)S(1)} custom-call(s32[1]{0:T(128)} %bitcast.where_ref, bf16[4,272,128]{2,1,0:T(8,128)(2,1)S(1)} %collective-permute-done.3.refs_0_, bf16[272,128]{1,0:T(8,128)(2,1)S(1)} %bitcast.26, bf16[272,128]{1,0:T(8,128)(2,1)S(1)} %bitcast.24, bf16[3456,512]{1,0:T(8,128)(2,1)S(1)} %get-tuple-element.36.refs_3_, ...), custom_call_target="tpu_custom_call" | custom-call | flops 905969664 | bytes 3801088 | tf_op jit(solution)/shard_map/conv_blocks/pallas_call | solution.py:166
  55.4 6.8 %collective-permute-done.4.refs_0_ = bf16[4,272,128]{2,1,0:T(8,128)(2,1)S(1)} collective-permute-done((bf16[4,272,128]{2,1,0:T(8,128)(2,1)S(1)}, bf16[4,272,128]{2,1,0:T(8,128)(2,1)S(1)}, u32[]{:S(2)}, u32[]{:S(2)}) %collective-permute-start.4) | collective-permute-done | bytes 278560 | tf_op jit(solution)/shard_map/ppermute | solution.py:303
  63.0 3.1 %collective-permute-start.14 = (bf16[1,1,272,128]{3,2,1,0:T(8,128)(2,1)S(1)}, bf16[1,1,272,128]{3,2,1,0:T(8,128)(2,1)S(1)}, u32[]{:S(2)}, u32[]{:S(2)}) collective-permute-start(bf16[1,1,272,128]{3,2,1,0:T(8,128)(2,1)S(1)} %get-tuple-element.47), channel_id=1, source_target_pairs={{0,1},{1,0},{2,3},{3,2},{4,5},{5,4},{6,7},{7,6},{8,9},{9,8},{10,11... | collective-permute-start | bytes 208904 | tf_op jit(solution)/shard_map/ppermute | solution.py:257
  67.1 4.3 %conv_blocks.11.mine_ref = f32[4,256,512]{2,1,0:T(8,128)S(1)} custom-call(s32[1]{0:T(128)} %bitcast.where_ref, bf16[4,272,128]{2,1,0:T(8,128)(2,1)S(1)} %collective-permute-done.4.refs_0_, bf16[272,128]{1,0:T(8,128)(2,1)S(1)} %bitcast.28, bf16[272,128]{1,0:T(8,128)(2,1)S(1)} %bitcast.27, bf16[3456,512]{1,0:T(8,128)(2,1)S(1)} %get-tuple-element.36.refs_3_, ...), custom_call_target="tpu_custom_call" | custom-call | flops 1811939328 | bytes 2293760 | tf_op jit(solution)/shard_map/conv_blocks/pallas_call | solution.py:166
  71.4 1.9 %down_blocks.3.refs_0_ = bf16[4,256,8,256]{3,2,1,0:T(8,128)(2,1)} custom-call(f32[4,256,512]{2,1,0:T(8,128)S(1)} %conv_blocks.11.mine_ref, bf16[1,256,512]{2,1,0:T(8,128)(2,1)S(1)} %collective-permute-done.18.theirs_ref, f32[4,256,512]{2,1,0:T(8,128)S(1)} %fusion.3.slope_ref, bf16[8,256,512]{2,1,0:T(8,128)(2,1)S(1)} %copy-done), custom_call_target="tpu_custom_call" | custom-call | flops 536870912 | bytes 2359296 | tf_op jit(solution)/shard_map/down_blocks/pallas_call | solution.py:216
  73.3 1.9 %collective-permute-done.17.theirs_ref = bf16[2,256,512]{2,1,0:T(8,128)(2,1)S(1)} collective-permute-done((bf16[2,256,512]{2,1,0:T(8,128)(2,1)S(1)}, bf16[2,256,512]{2,1,0:T(8,128)(2,1)S(1)}, u32[]{:S(2)}, u32[]{:S(2)}) %collective-permute-start.17) | collective-permute-done | bytes 524320 | tf_op jit(solution)/shard_map/ppermute | solution.py:321
  75.2 2.8 %down_blocks.4.refs_0_ = bf16[4,256,8,256]{3,2,1,0:T(8,128)(2,1)} custom-call(f32[4,256,512]{2,1,0:T(8,128)S(1)} %conv_blocks.11.mine_ref, bf16[2,256,512]{2,1,0:T(8,128)(2,1)S(1)} %collective-permute-done.17.theirs_ref, f32[4,256,512]{2,1,0:T(8,128)S(1)} %fusion.3.slope_ref, bf16[8,256,512]{2,1,0:T(8,128)(2,1)S(1)} %copy-done, ...), custom_call_target="tpu_custom_call", output_to_operand_aliasing={{}: (4, {})} | custom-call | flops 1073741824 | bytes 4718592 | tf_op jit(solution)/shard_map/down_blocks/pallas_call | solution.py:216
  78.0 2.4 %collective-permute-done.16.theirs_ref = bf16[1,256,512]{2,1,0:T(8,128)(2,1)S(1)} collective-permute-done((bf16[1,256,512]{2,1,0:T(8,128)(2,1)S(1)}, bf16[1,256,512]{2,1,0:T(8,128)(2,1)S(1)}, u32[]{:S(2)}, u32[]{:S(2)}) %collective-permute-start.16) | collective-permute-done | bytes 262176 | tf_op jit(solution)/shard_map/ppermute | solution.py:321
  80.3 1.9 %down_blocks.5 = bf16[4,256,8,256]{3,2,1,0:T(8,128)(2,1)} custom-call(f32[4,256,512]{2,1,0:T(8,128)S(1)} %conv_blocks.11.mine_ref, bf16[1,256,512]{2,1,0:T(8,128)(2,1)S(1)} %collective-permute-done.16.theirs_ref, f32[4,256,512]{2,1,0:T(8,128)S(1)} %fusion.3.slope_ref, bf16[8,256,512]{2,1,0:T(8,128)(2,1)S(1)} %copy-done, ...), custom_call_target="tpu_custom_call", output_to_operand_aliasing={{}: (4, {})} | custom-call | flops 536870912 | bytes 2359296 | tf_op jit(solution)/shard_map/down_blocks/pallas_call | solution.py:216
  (39 shorter events, 7.4 us)
Async XLA Ops:
  1.0 23.7 %collective-permute-start = (bf16[432,512]{1,0:T(8,128)(2,1)S(1)}, bf16[432,512]{1,0:T(8,128)(2,1)S(1)}, u32[]{:S(2)}, u32[]{:S(2)}) collective-permute-start(bf16[432,512]{1,0:T(8,128)(2,1)S(1)} %constant_dynamic-slice_fusion), channel_id=1, source_target_pairs={{0,8},{4,12},{8,0},{12,4},{1,9},{5,13},{9,1},{13,5},{2,10},{6,14},... | collective-permute-start | bytes 1327112 | tf_op jit(solution)/shard_map/ppermute | solution.py:268
  7.1 1.2 %copy-start.2 = (bf16[4,256,512]{2,1,0:T(8,128)(2,1)S(1)}, bf16[4,256,512]{2,1,0:T(8,128)(2,1)}, u32[]{:S(2)}) copy-start(bf16[4,256,512]{2,1,0:T(8,128)(2,1)} %param.6) | copy-start | bytes 3145732
  7.3 2.2 %copy-start.1 = (bf16[27,128,512]{2,1,0:T(8,128)(2,1)S(1)}, bf16[27,128,512]{2,1,0:T(8,128)(2,1)}, u32[]{:S(2)}) copy-start(bf16[27,128,512]{2,1,0:T(8,128)(2,1)} %param.5) | copy-start | bytes 10616836
  7.3 1.8 %collective-permute-start.1 = (bf16[2,1,272,128]{3,2,1,0:T(8,128)(2,1)S(1)}, bf16[2,1,272,128]{3,2,1,0:T(8,128)(2,1)S(1)}, u32[]{:S(2)}, u32[]{:S(2)}) collective-permute-start(bf16[2,1,272,128]{3,2,1,0:T(8,128)(2,1)S(1)} %broadcast_select_fusion.1), channel_id=1, source_target_pairs={{0,1},{1,0},{2,3},{3,2},{4,5},{5,4},{6,7},{7,6},{8,9},{9,8},{10,11... | collective-permute-start | bytes 417800 | tf_op jit(solution)/shard_map/ppermute | solution.py:257
  7.4 1.8 %collective-permute-start.2 = (bf16[2,1,272,128]{3,2,1,0:T(8,128)(2,1)S(1)}, bf16[2,1,272,128]{3,2,1,0:T(8,128)(2,1)S(1)}, u32[]{:S(2)}, u32[]{:S(2)}) collective-permute-start(bf16[2,1,272,128]{3,2,1,0:T(8,128)(2,1)S(1)} %get-tuple-element.39), channel_id=1, source_target_pairs={{1,2},{2,1},{5,6},{6,5},{9,10},{10,9},{13,14},{14,13},{17,18},{18,... | collective-permute-start | bytes 417800 | tf_op jit(solution)/shard_map/ppermute | solution.py:260
  24.8 12.4 %collective-permute-start.5 = (bf16[432,512]{1,0:T(8,128)(2,1)S(1)}, bf16[432,512]{1,0:T(8,128)(2,1)S(1)}, u32[]{:S(2)}, u32[]{:S(2)}) collective-permute-start(bf16[432,512]{1,0:T(8,128)(2,1)S(1)} %collective-permute-done.refs_1_), channel_id=1, source_target_pairs={{0,2},{1,17},{2,0},{3,19},{16,18},{17,1},{18,16},{19,3},{4,6},{5,2... | collective-permute-start | bytes 1327112 | tf_op jit(solution)/shard_map/ppermute | solution.py:297
  26.3 14.2 %collective-permute-start.3 = (bf16[4,272,128]{2,1,0:T(8,128)(2,1)S(1)}, bf16[4,272,128]{2,1,0:T(8,128)(2,1)S(1)}, u32[]{:S(2)}, u32[]{:S(2)}) collective-permute-start(bf16[4,272,128]{2,1,0:T(8,128)(2,1)S(1)} %get-tuple-element.25), channel_id=1, source_target_pairs={{0,8},{4,12},{8,0},{12,4},{1,9},{5,13},{9,1},{13,5},{2,10},{6,14},... | collective-permute-start | bytes 835592 | tf_op jit(solution)/shard_map/ppermute | solution.py:296
  26.3 14.9 %collective-permute-start.6 = (bf16[432,512]{1,0:T(8,128)(2,1)S(1)}, bf16[432,512]{1,0:T(8,128)(2,1)S(1)}, u32[]{:S(2)}, u32[]{:S(2)}) collective-permute-start(bf16[432,512]{1,0:T(8,128)(2,1)S(1)} %collective-permute-done.refs_1_), channel_id=1, source_target_pairs={{0,16},{1,3},{2,18},{3,1},{16,0},{17,19},{18,2},{19,17},{4,20},{5,... | collective-permute-start | bytes 1327112 | tf_op jit(solution)/shard_map/ppermute | solution.py:298
  27.9 18.2 %collective-permute-start.8 = (bf16[432,512]{1,0:T(8,128)(2,1)S(1)}, bf16[432,512]{1,0:T(8,128)(2,1)S(1)}, u32[]{:S(2)}, u32[]{:S(2)}) collective-permute-start(bf16[432,512]{1,0:T(8,128)(2,1)S(1)} %collective-permute-done.refs_1_), channel_id=1, source_target_pairs={{0,1},{1,0},{2,3},{3,2},{4,5},{5,4},{6,7},{7,6},{8,9},{9,8},{10,11... | collective-permute-start | bytes 1327112 | tf_op jit(solution)/shard_map/ppermute | solution.py:300
  37.1 8.9 %collective-permute-start.9 = (bf16[432,512]{1,0:T(8,128)(2,1)S(1)}, bf16[432,512]{1,0:T(8,128)(2,1)S(1)}, u32[]{:S(2)}, u32[]{:S(2)}) collective-permute-start(bf16[432,512]{1,0:T(8,128)(2,1)S(1)} %collective-permute-done.5.refs_2_), channel_id=1, source_target_pairs={{0,1},{1,0},{2,3},{3,2},{4,5},{5,4},{6,7},{7,6},{8,9},{9,8},{10,11... | collective-permute-start | bytes 1327112 | tf_op jit(solution)/shard_map/ppermute | solution.py:300
  37.2 8.9 %collective-permute-start.7 = (bf16[432,512]{1,0:T(8,128)(2,1)S(1)}, bf16[432,512]{1,0:T(8,128)(2,1)S(1)}, u32[]{:S(2)}, u32[]{:S(2)}) collective-permute-start(bf16[432,512]{1,0:T(8,128)(2,1)S(1)} %collective-permute-done.5.refs_2_), channel_id=1, source_target_pairs={{0,16},{1,3},{2,18},{3,1},{16,0},{17,19},{18,2},{19,17},{4,20},{5,... | collective-permute-start | bytes 1327112 | tf_op jit(solution)/shard_map/ppermute | solution.py:299
  40.5 3.6 %collective-permute-start.11 = (bf16[1,1,272,128]{3,2,1,0:T(8,128)(2,1)S(1)}, bf16[1,1,272,128]{3,2,1,0:T(8,128)(2,1)S(1)}, u32[]{:S(2)}, u32[]{:S(2)}) collective-permute-start(bf16[1,1,272,128]{3,2,1,0:T(8,128)(2,1)S(1)} %get-tuple-element.48), channel_id=1, source_target_pairs={{1,2},{2,1},{5,6},{6,5},{9,10},{10,9},{13,14},{14,13},{17,18},{18,... | collective-permute-start | bytes 208904 | tf_op jit(solution)/shard_map/ppermute | solution.py:260
  41.2 4.8 %collective-permute-start.10 = (bf16[1,1,272,128]{3,2,1,0:T(8,128)(2,1)S(1)}, bf16[1,1,272,128]{3,2,1,0:T(8,128)(2,1)S(1)}, u32[]{:S(2)}, u32[]{:S(2)}) collective-permute-start(bf16[1,1,272,128]{3,2,1,0:T(8,128)(2,1)S(1)} %get-tuple-element.49), channel_id=1, source_target_pairs={{0,1},{1,0},{2,3},{3,2},{4,5},{5,4},{6,7},{7,6},{8,9},{9,8},{10,11... | collective-permute-start | bytes 208904 | tf_op jit(solution)/shard_map/ppermute | solution.py:257
  44.1 3.3 %collective-permute-start.12 = (bf16[432,512]{1,0:T(8,128)(2,1)S(1)}, bf16[432,512]{1,0:T(8,128)(2,1)S(1)}, u32[]{:S(2)}, u32[]{:S(2)}) collective-permute-start(bf16[432,512]{1,0:T(8,128)(2,1)S(1)} %collective-permute-done.6.refs_3_), channel_id=1, source_target_pairs={{0,1},{1,0},{2,3},{3,2},{4,5},{5,4},{6,7},{7,6},{8,9},{9,8},{10,11... | collective-permute-start | bytes 1327112 | tf_op jit(solution)/shard_map/ppermute | solution.py:302
  46.0 2.0 %collective-permute-start.13 = (bf16[432,512]{1,0:T(8,128)(2,1)S(1)}, bf16[432,512]{1,0:T(8,128)(2,1)S(1)}, u32[]{:S(2)}, u32[]{:S(2)}) collective-permute-start(bf16[432,512]{1,0:T(8,128)(2,1)S(1)} %collective-permute-done.7.refs_4_), channel_id=1, source_target_pairs={{0,1},{1,0},{2,3},{3,2},{4,5},{5,4},{6,7},{7,6},{8,9},{9,8},{10,11... | collective-permute-start | bytes 1327112 | tf_op jit(solution)/shard_map/ppermute | solution.py:308
  46.1 16.0 %collective-permute-start.4 = (bf16[4,272,128]{2,1,0:T(8,128)(2,1)S(1)}, bf16[4,272,128]{2,1,0:T(8,128)(2,1)S(1)}, u32[]{:S(2)}, u32[]{:S(2)}) collective-permute-start(bf16[4,272,128]{2,1,0:T(8,128)(2,1)S(1)} %get-tuple-element.26), channel_id=1, source_target_pairs={{0,8},{4,12},{8,0},{12,4},{1,9},{5,13},{9,1},{13,5},{2,10},{6,14},... | collective-permute-start | bytes 835592 | tf_op jit(solution)/shard_map/ppermute | solution.py:303
  49.6 21.8 %collective-permute-start.18 = (bf16[1,256,512]{2,1,0:T(8,128)(2,1)S(1)}, bf16[1,256,512]{2,1,0:T(8,128)(2,1)S(1)}, u32[]{:S(2)}, u32[]{:S(2)}) collective-permute-start(bf16[1,256,512]{2,1,0:T(8,128)(2,1)S(1)} %get-tuple-element.32), channel_id=1, source_target_pairs={{0,4},{4,0},{8,12},{12,8},{1,5},{5,1},{9,13},{13,9},{2,6},{6,2},{1... | collective-permute-start | bytes 786440 | tf_op jit(solution)/shard_map/ppermute | solution.py:314
  54.1 21.1 %collective-permute-start.17 = (bf16[2,256,512]{2,1,0:T(8,128)(2,1)S(1)}, bf16[2,256,512]{2,1,0:T(8,128)(2,1)S(1)}, u32[]{:S(2)}, u32[]{:S(2)}) collective-permute-start(bf16[2,256,512]{2,1,0:T(8,128)(2,1)S(1)} %conv_blocks.9), channel_id=1, source_target_pairs={{0,4},{4,0},{8,12},{12,8},{1,5},{5,1},{9,13},{13,9},{2,6},{6,2},{1... | collective-permute-start | bytes 1572872 | tf_op jit(solution)/shard_map/ppermute | solution.py:321
  62.2 4.0 %collective-permute-start.15 = (bf16[1,1,272,128]{3,2,1,0:T(8,128)(2,1)S(1)}, bf16[1,1,272,128]{3,2,1,0:T(8,128)(2,1)S(1)}, u32[]{:S(2)}, u32[]{:S(2)}) collective-permute-start(bf16[1,1,272,128]{3,2,1,0:T(8,128)(2,1)S(1)} %get-tuple-element.46), channel_id=1, source_target_pairs={{1,2},{2,1},{5,6},{6,5},{9,10},{10,9},{13,14},{14,13},{17,18},{18,... | collective-permute-start | bytes 208904 | tf_op jit(solution)/shard_map/ppermute | solution.py:260
  63.0 4.0 %collective-permute-start.14 = (bf16[1,1,272,128]{3,2,1,0:T(8,128)(2,1)S(1)}, bf16[1,1,272,128]{3,2,1,0:T(8,128)(2,1)S(1)}, u32[]{:S(2)}, u32[]{:S(2)}) collective-permute-start(bf16[1,1,272,128]{3,2,1,0:T(8,128)(2,1)S(1)} %get-tuple-element.47), channel_id=1, source_target_pairs={{0,1},{1,0},{2,3},{3,2},{4,5},{5,4},{6,7},{7,6},{8,9},{9,8},{10,11... | collective-permute-start | bytes 208904 | tf_op jit(solution)/shard_map/ppermute | solution.py:257
  66.1 14.2 %collective-permute-start.16 = (bf16[1,256,512]{2,1,0:T(8,128)(2,1)S(1)}, bf16[1,256,512]{2,1,0:T(8,128)(2,1)S(1)}, u32[]{:S(2)}, u32[]{:S(2)}) collective-permute-start(bf16[1,256,512]{2,1,0:T(8,128)(2,1)S(1)} %conv_blocks.10), channel_id=1, source_target_pairs={{0,4},{4,0},{8,12},{12,8},{1,5},{5,1},{9,13},{13,9},{2,6},{6,2},{1... | collective-permute-start | bytes 786440 | tf_op jit(solution)/shard_map/ppermute | solution.py:321
  67.1 4.3 %copy-start = (bf16[8,256,512]{2,1,0:T(8,128)(2,1)S(1)}, bf16[8,256,512]{2,1,0:T(8,128)(2,1)}, u32[]{:S(2)}) copy-start(bf16[8,256,512]{2,1,0:T(8,128)(2,1)} %weight_ref.5) | copy-start | bytes 6291460

commit v6 on v5

--- a/solution.py
+++ b/solution.py
@@ -184,43 +184,55 @@
     )(*operands)
 
 
-def down_kernel(mine_ref, theirs_ref, slope_ref, weight_ref, *refs, first, step):
-    out_ref = refs[-1]
-    at = pl.program_id(0)
-    plane = first + step * at
-    act = (mine_ref[plane] + theirs_ref[at].astype(jnp.float32)).astype(jnp.bfloat16)
-    pre = (act.astype(jnp.float32) * slope_ref[plane]).astype(jnp.bfloat16)
-    grown = [
-        lax.dot_general(
-            pre,
-            weight_ref[e],
-            (((1,), (1,)), ((), ())),
-            preferred_element_type=jnp.float32,
-        ).astype(out_ref.dtype)
-        for e in range(weight_ref.shape[0])
-    ]
-    out_ref[0] = jnp.swapaxes(jnp.stack(grown), 0, 1)
+def down_kernel(mine_ref, theirs_ref, slope_ref, weight_ref, *refs, planes):
+    out_ref, ready, sems = refs[-3:]
+    cells = ready.shape[1]
+    step = cells // 4
+    copies = []
+    for at, plane in enumerate(planes):
+        act = (mine_ref[plane] + theirs_ref[at].astype(jnp.float32)).astype(jnp.bfloat16)
+        pre = (act.astype(jnp.float32) * slope_ref[plane]).astype(jnp.bfloat16)
+        grown = [
+            lax.dot_general(
+                pre,
+                weight_ref[e],
+                (((1,), (1,)), ((), ())),
+                preferred_element_type=jnp.float32,
+            ).astype(out_ref.dtype)
+            for e in range(weight_ref.shape[0])
+        ]
+        for low in range(0, cells, step):
+            part = jnp.stack([v[low : low + step] for v in grown])
+            ready[at, low : low + step] = jnp.swapaxes(part, 0, 1)
+            copies.append(
+                pltpu.make_async_copy(
+                    ready.at[at, pl.ds(low, step)],
+                    out_ref.at[plane, pl.ds(low, step)],
+                    sems.at[len(copies)],
+                )
+            )
+            copies[-1].start()
+    for copy in copies:
+        copy.wait()
 
 
 def down_blocks(mine, theirs, slope, weight, planes, partly):
     extent, cells, wide = slope.shape
     offsets, fine, _ = weight.shape
-    first = planes[0]
-    step = planes[1] - first if len(planes) > 1 else 0
-    on_chip = pl.BlockSpec(memory_space=pltpu.VMEM)
-    in_specs = [on_chip] * 4
+    in_specs = [pl.BlockSpec(memory_space=pltpu.VMEM)] * 4
     operands = [mine, theirs, slope, weight]
     if partly is not None:
         in_specs.append(pl.BlockSpec(memory_space=pl.ANY))
         operands.append(partly)
     return pl.pallas_call(
-        functools.partial(down_kernel, first=first, step=step),
-        grid=(len(planes),),
+        functools.partial(down_kernel, planes=planes),
         in_specs=in_specs,
-        out_specs=pl.BlockSpec(
-            (1, cells, offsets, fine), lambda i: (first + step * i, 0, 0, 0)
-        ),
+        out_specs=pl.BlockSpec(memory_space=pl.ANY),
         out_shape=jax.ShapeDtypeStruct((extent, cells, offsets, fine), jnp.bfloat16),
+        scratch_shapes=[
+            pltpu.VMEM((len(planes), cells, offsets, fine), jnp.bfloat16),
+            pltpu.SemaphoreType.DMA((4 * len(planes),)),
+        ],
         input_output_aliases={} if partly is None else {4: 0},
         compiler_params=pltpu.CompilerParams(vmem_limit_bytes=20 * 2**20),
         cost_estimate=pl.CostEstimate(
@@ -302,8 +314,8 @@
     pair_b = lax.ppermute(got_b, "pair", other)
     far_two = lax.ppermute(after(window_two, far_one), "chan", far)
     one_inner, one_outer = margins(far_one[None])
-    got_c, pair_got, pair_a, one_inner, one_outer = lax.optimization_barrier(
-        (got_c, pair_got, pair_a, one_inner, one_outer)
+    got_c, pair_got, pair_a, one_outer = lax.optimization_barrier(
+        (got_c, pair_got, pair_a, one_outer)
     )
     pair_c = lax.ppermute(got_c, "pair", other)
     pieces = [got, got_a, got_b, got_c, pair_got, pair_a, pair_b, pair_c]

time: 82.5 us -> 82.4 us (level)
    ppermute x3, starting transfers between devices: 6.09 us -> 3.26 us  [margins(): lax.ppermute(jnp.where(lax.axis_index('pair') == 0, tail, head), 'pair',...]
    ppermute x1, waiting for transfers between devices: 0.01 us -> 1.32 us  [two_level_body(): got_c = lax.ppermute(got_a, PLANAR, second)]
    ppermute x1, waiting for transfers between devices: 1.24 us -> 0.01 us  [two_level_body(): pair_b = lax.ppermute(got_b, 'pair', other)]
    ppermute x1, starting transfers between devices: 1.9 us -> 2.91 us  [two_level_body(): pair_b = lax.ppermute(got_b, 'pair', other)]
  transfers between devices with their start and end apart: 19 -> 19, of which waited for: 9 -> 9; matrix products, arithmetic and copies ran while one was open for 4% -> 4% of each run, Pallas kernels for 28% -> 27%
where the time goes in v6:
time: 82.4 us; the launch traced here: 82.2 us
  waiting for transfers between devices  33.2 us (40%)
  Pallas kernels  24.1 us (29%)
  starting transfers between devices  20.2 us (25%)
  local copies, waits for them, and re-layouts  3.48 us (4%)
  other arithmetic  0.9 us (1%)
    pallas_call x6, Pallas kernels, conv_blocks(): pl.pallas_call(functools.partial(conv_kernel, sources=[(len(v[0]) > 1, le...  17.9 us
    ppermute x1, waiting for transfers between devices, two_level_body(): got_a = lax.ppermute(got, PLANAR, first)  9.28 us
    ppermute x1, waiting for transfers between devices, two_level_body(): got = lax.ppermute(piece, 'chan', far)  6.71 us
    ppermute x1, waiting for transfers between devices, two_level_body(): far_two = lax.ppermute(after(window_two, far_one), 'chan', far)  6.53 us
    pallas_call x3, Pallas kernels, down_blocks(): pl.pallas_call(functools.partial(down_kernel, planes=planes), in_specs=in...  6.16 us
    ppermute x2, waiting for transfers between devices, two_level_body(): theirs.append(lax.ppermute(sent, 'chan', near))  4.5 us
    ppermute x1, starting transfers between devices, two_level_body(): got = lax.ppermute(piece, 'chan', far)  4.1 us
    ppermute x3, starting transfers between devices, margins(): lax.ppermute(jnp.where(lax.axis_index('pair') == 0, tail, head), 'pair',...  3.26 us
  transfers between devices with their start and end apart: 19, of which 9 were waited for; matrix products, arithmetic and copies ran while one was open for 4% of the time, Pallas kernels for 27%

profile of v6, /device:TPU:0, one launch (start us, length us, event | category | flops | bytes accessed | tf_op | source)
XLA Modules:
  0.0 82.2 jit_solution(14056215899239537236)
XLA Ops:
  1.0 4.1 %collective-permute-start = (bf16[432,512]{1,0:T(8,128)(2,1)S(1)}, bf16[432,512]{1,0:T(8,128)(2,1)S(1)}, u32[]{:S(2)}, u32[]{:S(2)}) collective-permute-start(bf16[432,512]{1,0:T(8,128)(2,1)S(1)} %constant_dynamic-slice_fusion), channel_id=1, source_target_pairs={{0,8},{4,12},{8,0},{12,4},{1,9},{5,13},{9,1},{13,5},{2,10},{6,14},... | collective-permute-start | bytes 1327112 | tf_op jit(solution)/shard_map/ppermute | solution.py:280
  5.1 1.9 %copy.7 = bf16[128,4,1024]{0,2,1:T(8,128)(2,1)S(1)} copy(bf16[128,4,1024]{2,1,0:T(4,128)(2,1)} %param.4) | data formatting | bytes 2097152 | tf_op jit(solution)/shard_map/optimization_barrier | solution.py:265
  9.4 4.3 %conv_blocks.7.refs_4_ = f32[4,256,512]{2,1,0:T(8,128)S(1)} custom-call(s32[1]{0:T(128)} %bitcast.where_ref, bf16[4,272,128]{2,1,0:T(8,128)(2,1)S(1)} %get-tuple-element.40.refs_0_, bf16[272,128]{1,0:T(8,128)(2,1)S(1)} %get-tuple-element.50.refs_1_, bf16[272,128]{1,0:T(8,128)(2,1)S(1)} %get-tuple-element.48.refs_2_, bf16[3456,512]{1,0:T(8,128)(2,1)S(1)} %bitcast.30), custom_call_target="tpu_custom_call" | custom-call | flops 3623878656 | bytes 4587520 | tf_op jit(solution)/shard_map/conv_blocks/pallas_call | solution.py:166
  13.8 4.3 %conv_blocks.6.refs_9_.refs_4_ = f32[4,256,512]{2,1,0:T(8,128)S(1)} custom-call(s32[1]{0:T(128)} %bitcast.where_ref, bf16[4,272,128]{2,1,0:T(8,128)(2,1)S(1)} %get-tuple-element.42.refs_0_, bf16[272,128]{1,0:T(8,128)(2,1)S(1)} %get-tuple-element.51.refs_1_, bf16[272,128]{1,0:T(8,128)(2,1)S(1)} %get-tuple-element.49.refs_2_, bf16[3456,512]{1,0:T(8,128)(2,1)S(1)} %bitcast.31), custom_call_target="tpu_custom_call" | custom-call | flops 3623878656 | bytes 4587520 | tf_op jit(solution)/shard_map/conv_blocks/pallas_call | solution.py:166
  18.1 6.7 %collective-permute-done.refs_1_ = bf16[432,512]{1,0:T(8,128)(2,1)S(1)} collective-permute-done((bf16[432,512]{1,0:T(8,128)(2,1)S(1)}, bf16[432,512]{1,0:T(8,128)(2,1)S(1)}, u32[]{:S(2)}, u32[]{:S(2)}) %collective-permute-start) | collective-permute-done | bytes 442400 | tf_op jit(solution)/shard_map/ppermute | solution.py:280
  24.8 1.5 %collective-permute-start.5 = (bf16[432,512]{1,0:T(8,128)(2,1)S(1)}, bf16[432,512]{1,0:T(8,128)(2,1)S(1)}, u32[]{:S(2)}, u32[]{:S(2)}) collective-permute-start(bf16[432,512]{1,0:T(8,128)(2,1)S(1)} %collective-permute-done.refs_1_), channel_id=1, source_target_pairs={{0,2},{1,17},{2,0},{3,19},{16,18},{17,1},{18,16},{19,3},{4,6},{5,2... | collective-permute-start | bytes 1327112 | tf_op jit(solution)/shard_map/ppermute | solution.py:309
  26.3 1.5 %collective-permute-start.6 = (bf16[432,512]{1,0:T(8,128)(2,1)S(1)}, bf16[432,512]{1,0:T(8,128)(2,1)S(1)}, u32[]{:S(2)}, u32[]{:S(2)}) collective-permute-start(bf16[432,512]{1,0:T(8,128)(2,1)S(1)} %collective-permute-done.refs_1_), channel_id=1, source_target_pairs={{0,16},{1,3},{2,18},{3,1},{16,0},{17,19},{18,2},{19,17},{4,20},{5,... | collective-permute-start | bytes 1327112 | tf_op jit(solution)/shard_map/ppermute | solution.py:310
  27.9 9.3 %collective-permute-done.5.refs_2_ = bf16[432,512]{1,0:T(8,128)(2,1)S(1)} collective-permute-done((bf16[432,512]{1,0:T(8,128)(2,1)S(1)}, bf16[432,512]{1,0:T(8,128)(2,1)S(1)}, u32[]{:S(2)}, u32[]{:S(2)}) %collective-permute-start.5) | collective-permute-done | bytes 442400 | tf_op jit(solution)/shard_map/ppermute | solution.py:309
  37.9 2.6 %collective-permute-done.3.refs_0_ = bf16[4,272,128]{2,1,0:T(8,128)(2,1)S(1)} collective-permute-done((bf16[4,272,128]{2,1,0:T(8,128)(2,1)S(1)}, bf16[4,272,128]{2,1,0:T(8,128)(2,1)S(1)}, u32[]{:S(2)}, u32[]{:S(2)}) %collective-permute-start.3) | collective-permute-done | bytes 278560 | tf_op jit(solution)/shard_map/ppermute | solution.py:308
  41.2 2.9 %collective-permute-start.11 = (bf16[432,512]{1,0:T(8,128)(2,1)S(1)}, bf16[432,512]{1,0:T(8,128)(2,1)S(1)}, u32[]{:S(2)}, u32[]{:S(2)}) collective-permute-start(bf16[432,512]{1,0:T(8,128)(2,1)S(1)} %collective-permute-done.6.refs_3_), channel_id=1, source_target_pairs={{0,1},{1,0},{2,3},{3,2},{4,5},{5,4},{6,7},{7,6},{8,9},{9,8},{10,11... | collective-permute-start | bytes 1327112 | tf_op jit(solution)/shard_map/ppermute | solution.py:314
  44.1 1.3 %collective-permute-done.7.refs_4_ = bf16[432,512]{1,0:T(8,128)(2,1)S(1)} collective-permute-done((bf16[432,512]{1,0:T(8,128)(2,1)S(1)}, bf16[432,512]{1,0:T(8,128)(2,1)S(1)}, u32[]{:S(2)}, u32[]{:S(2)}) %collective-permute-start.7) | collective-permute-done | bytes 442400 | tf_op jit(solution)/shard_map/ppermute | solution.py:311
  46.2 1.3 %collective-permute-done.12.refs_8_ = bf16[432,512]{1,0:T(8,128)(2,1)S(1)} collective-permute-done((bf16[432,512]{1,0:T(8,128)(2,1)S(1)}, bf16[432,512]{1,0:T(8,128)(2,1)S(1)}, u32[]{:S(2)}, u32[]{:S(2)}) %collective-permute-start.12) | collective-permute-done | bytes 442400 | tf_op jit(solution)/shard_map/ppermute | solution.py:320
  47.5 1.5 %conv_blocks.8 = (bf16[1,256,512]{2,1,0:T(8,128)(2,1)S(1)}, bf16[3456,512]{1,0:T(8,128)(2,1)S(1)}) custom-call(s32[1]{0:T(128)} %bitcast.where_ref, bf16[4,272,128]{2,1,0:T(8,128)(2,1)S(1)} %collective-permute-done.3.refs_0_, bf16[432,512]{1,0:T(8,128)(2,1)S(1)} %collective-permute-done.refs_1_, bf16[432,512]{1,0:T(8,128)(2,1)S(1)} %collective-permute-done.5.refs_2_, ...), custom_call_target="tpu_custom_call" | custom-call | flops 905969664 | bytes 3801088 | tf_op jit(solution)/shard_map/conv_blocks/pallas_call | solution.py:166
  49.0 3.0 %collective-permute-start.18 = (bf16[1,256,512]{2,1,0:T(8,128)(2,1)S(1)}, bf16[1,256,512]{2,1,0:T(8,128)(2,1)S(1)}, u32[]{:S(2)}, u32[]{:S(2)}) collective-permute-start(bf16[1,256,512]{2,1,0:T(8,128)(2,1)S(1)} %get-tuple-element.31), channel_id=1, source_target_pairs={{0,4},{4,0},{8,12},{12,8},{1,5},{5,1},{9,13},{13,9},{2,6},{6,2},{1... | collective-permute-start | bytes 786440 | tf_op jit(solution)/shard_map/ppermute | solution.py:326
  52.0 2.3 %conv_blocks.9 = bf16[2,256,512]{2,1,0:T(8,128)(2,1)S(1)} custom-call(s32[1]{0:T(128)} %bitcast.where_ref, bf16[4,272,128]{2,1,0:T(8,128)(2,1)S(1)} %collective-permute-done.3.refs_0_, bf16[272,128]{1,0:T(8,128)(2,1)S(1)} %bitcast.25, bf16[272,128]{1,0:T(8,128)(2,1)S(1)} %bitcast.23, bf16[3456,512]{1,0:T(8,128)(2,1)S(1)} %get-tuple-element.34.refs_3_, ...), custom_call_target="tpu_custom_call" | custom-call | flops 1811939328 | bytes 4063232 | tf_op jit(solution)/shard_map/conv_blocks/pallas_call | solution.py:166
  54.4 1.2 %conv_blocks.10 = bf16[1,256,512]{2,1,0:T(8,128)(2,1)S(1)} custom-call(s32[1]{0:T(128)} %bitcast.where_ref, bf16[4,272,128]{2,1,0:T(8,128)(2,1)S(1)} %collective-permute-done.3.refs_0_, bf16[272,128]{1,0:T(8,128)(2,1)S(1)} %bitcast.26, bf16[272,128]{1,0:T(8,128)(2,1)S(1)} %bitcast.24, bf16[3456,512]{1,0:T(8,128)(2,1)S(1)} %get-tuple-element.34.refs_3_, ...), custom_call_target="tpu_custom_call" | custom-call | flops 905969664 | bytes 3801088 | tf_op jit(solution)/shard_map/conv_blocks/pallas_call | solution.py:166
  55.6 6.5 %collective-permute-done.4.refs_0_ = bf16[4,272,128]{2,1,0:T(8,128)(2,1)S(1)} collective-permute-done((bf16[4,272,128]{2,1,0:T(8,128)(2,1)S(1)}, bf16[4,272,128]{2,1,0:T(8,128)(2,1)S(1)}, u32[]{:S(2)}, u32[]{:S(2)}) %collective-permute-start.4) | collective-permute-done | bytes 278560 | tf_op jit(solution)/shard_map/ppermute | solution.py:315
  63.0 3.1 %collective-permute-start.14 = (bf16[1,1,272,128]{3,2,1,0:T(8,128)(2,1)S(1)}, bf16[1,1,272,128]{3,2,1,0:T(8,128)(2,1)S(1)}, u32[]{:S(2)}, u32[]{:S(2)}) collective-permute-start(bf16[1,1,272,128]{3,2,1,0:T(8,128)(2,1)S(1)} %get-tuple-element.45), channel_id=1, source_target_pairs={{0,1},{1,0},{2,3},{3,2},{4,5},{5,4},{6,7},{7,6},{8,9},{9,8},{10,11... | collective-permute-start | bytes 208904 | tf_op jit(solution)/shard_map/ppermute | solution.py:269
  67.1 4.3 %conv_blocks.11.mine_ref = f32[4,256,512]{2,1,0:T(8,128)S(1)} custom-call(s32[1]{0:T(128)} %bitcast.where_ref, bf16[4,272,128]{2,1,0:T(8,128)(2,1)S(1)} %collective-permute-done.4.refs_0_, bf16[272,128]{1,0:T(8,128)(2,1)S(1)} %bitcast.28, bf16[272,128]{1,0:T(8,128)(2,1)S(1)} %bitcast.27, bf16[3456,512]{1,0:T(8,128)(2,1)S(1)} %get-tuple-element.34.refs_3_, ...), custom_call_target="tpu_custom_call" | custom-call | flops 1811939328 | bytes 2293760 | tf_op jit(solution)/shard_map/conv_blocks/pallas_call | solution.py:166
  71.4 1.8 %down_blocks.3.refs_0_ = bf16[4,256,8,256]{3,2,1,0:T(8,128)(2,1)} custom-call(f32[4,256,512]{2,1,0:T(8,128)S(1)} %conv_blocks.11.mine_ref, bf16[1,256,512]{2,1,0:T(8,128)(2,1)S(1)} %collective-permute-done.18.theirs_ref, f32[4,256,512]{2,1,0:T(8,128)S(1)} %fusion.3.slope_ref, bf16[8,256,512]{2,1,0:T(8,128)(2,1)S(1)} %copy-done), custom_call_target="tpu_custom_call" | custom-call | flops 536870912 | bytes 2359296 | tf_op jit(solution)/shard_map/down_blocks/pallas_call | solution.py:227
  73.2 2.3 %collective-permute-done.17.theirs_ref = bf16[2,256,512]{2,1,0:T(8,128)(2,1)S(1)} collective-permute-done((bf16[2,256,512]{2,1,0:T(8,128)(2,1)S(1)}, bf16[2,256,512]{2,1,0:T(8,128)(2,1)S(1)}, u32[]{:S(2)}, u32[]{:S(2)}) %collective-permute-start.17) | collective-permute-done | bytes 524320 | tf_op jit(solution)/shard_map/ppermute | solution.py:333
  75.4 2.6 %down_blocks.4.refs_0_ = bf16[4,256,8,256]{3,2,1,0:T(8,128)(2,1)} custom-call(f32[4,256,512]{2,1,0:T(8,128)S(1)} %conv_blocks.11.mine_ref, bf16[2,256,512]{2,1,0:T(8,128)(2,1)S(1)} %collective-permute-done.17.theirs_ref, f32[4,256,512]{2,1,0:T(8,128)S(1)} %fusion.3.slope_ref, bf16[8,256,512]{2,1,0:T(8,128)(2,1)S(1)} %copy-done, ...), custom_call_target="tpu_custom_call", output_to_operand_aliasing={{}: (4, {})} | custom-call | flops 1073741824 | bytes 4718592 | tf_op jit(solution)/shard_map/down_blocks/pallas_call | solution.py:227
  78.1 2.2 %collective-permute-done.16.theirs_ref = bf16[1,256,512]{2,1,0:T(8,128)(2,1)S(1)} collective-permute-done((bf16[1,256,512]{2,1,0:T(8,128)(2,1)S(1)}, bf16[1,256,512]{2,1,0:T(8,128)(2,1)S(1)}, u32[]{:S(2)}, u32[]{:S(2)}) %collective-permute-start.16) | collective-permute-done | bytes 262176 | tf_op jit(solution)/shard_map/ppermute | solution.py:333
  80.3 1.8 %down_blocks.5 = bf16[4,256,8,256]{3,2,1,0:T(8,128)(2,1)} custom-call(f32[4,256,512]{2,1,0:T(8,128)S(1)} %conv_blocks.11.mine_ref, bf16[1,256,512]{2,1,0:T(8,128)(2,1)S(1)} %collective-permute-done.16.theirs_ref, f32[4,256,512]{2,1,0:T(8,128)S(1)} %fusion.3.slope_ref, bf16[8,256,512]{2,1,0:T(8,128)(2,1)S(1)} %copy-done, ...), custom_call_target="tpu_custom_call", output_to_operand_aliasing={{}: (4, {})} | custom-call | flops 536870912 | bytes 2359296 | tf_op jit(solution)/shard_map/down_blocks/pallas_call | solution.py:227
  (39 shorter events, 7.3 us)
Async XLA Ops:
  1.0 23.7 %collective-permute-start = (bf16[432,512]{1,0:T(8,128)(2,1)S(1)}, bf16[432,512]{1,0:T(8,128)(2,1)S(1)}, u32[]{:S(2)}, u32[]{:S(2)}) collective-permute-start(bf16[432,512]{1,0:T(8,128)(2,1)S(1)} %constant_dynamic-slice_fusion), channel_id=1, source_target_pairs={{0,8},{4,12},{8,0},{12,4},{1,9},{5,13},{9,1},{13,5},{2,10},{6,14},... | collective-permute-start | bytes 1327112 | tf_op jit(solution)/shard_map/ppermute | solution.py:280
  7.1 1.2 %copy-start.2 = (bf16[4,256,512]{2,1,0:T(8,128)(2,1)S(1)}, bf16[4,256,512]{2,1,0:T(8,128)(2,1)}, u32[]{:S(2)}) copy-start(bf16[4,256,512]{2,1,0:T(8,128)(2,1)} %param.6) | copy-start | bytes 3145732
  7.3 2.2 %copy-start.1 = (bf16[27,128,512]{2,1,0:T(8,128)(2,1)S(1)}, bf16[27,128,512]{2,1,0:T(8,128)(2,1)}, u32[]{:S(2)}) copy-start(bf16[27,128,512]{2,1,0:T(8,128)(2,1)} %param.5) | copy-start | bytes 10616836
  7.3 1.8 %collective-permute-start.1 = (bf16[2,1,272,128]{3,2,1,0:T(8,128)(2,1)S(1)}, bf16[2,1,272,128]{3,2,1,0:T(8,128)(2,1)S(1)}, u32[]{:S(2)}, u32[]{:S(2)}) collective-permute-start(bf16[2,1,272,128]{3,2,1,0:T(8,128)(2,1)S(1)} %broadcast_select_fusion.1), channel_id=1, source_target_pairs={{0,1},{1,0},{2,3},{3,2},{4,5},{5,4},{6,7},{7,6},{8,9},{9,8},{10,11... | collective-permute-start | bytes 417800 | tf_op jit(solution)/shard_map/ppermute | solution.py:269
  7.4 1.8 %collective-permute-start.2 = (bf16[2,1,272,128]{3,2,1,0:T(8,128)(2,1)S(1)}, bf16[2,1,272,128]{3,2,1,0:T(8,128)(2,1)S(1)}, u32[]{:S(2)}, u32[]{:S(2)}) collective-permute-start(bf16[2,1,272,128]{3,2,1,0:T(8,128)(2,1)S(1)} %get-tuple-element.37), channel_id=1, source_target_pairs={{1,2},{2,1},{5,6},{6,5},{9,10},{10,9},{13,14},{14,13},{17,18},{18,... | collective-permute-start | bytes 417800 | tf_op jit(solution)/shard_map/ppermute | solution.py:272
  24.8 12.4 %collective-permute-start.5 = (bf16[432,512]{1,0:T(8,128)(2,1)S(1)}, bf16[432,512]{1,0:T(8,128)(2,1)S(1)}, u32[]{:S(2)}, u32[]{:S(2)}) collective-permute-start(bf16[432,512]{1,0:T(8,128)(2,1)S(1)} %collective-permute-done.refs_1_), channel_id=1, source_target_pairs={{0,2},{1,17},{2,0},{3,19},{16,18},{17,1},{18,16},{19,3},{4,6},{5,2... | collective-permute-start | bytes 1327112 | tf_op jit(solution)/shard_map/ppermute | solution.py:309
  26.3 14.2 %collective-permute-start.3 = (bf16[4,272,128]{2,1,0:T(8,128)(2,1)S(1)}, bf16[4,272,128]{2,1,0:T(8,128)(2,1)S(1)}, u32[]{:S(2)}, u32[]{:S(2)}) collective-permute-start(bf16[4,272,128]{2,1,0:T(8,128)(2,1)S(1)} %get-tuple-element.24), channel_id=1, source_target_pairs={{0,8},{4,12},{8,0},{12,4},{1,9},{5,13},{9,1},{13,5},{2,10},{6,14},... | collective-permute-start | bytes 835592 | tf_op jit(solution)/shard_map/ppermute | solution.py:308
  26.3 14.9 %collective-permute-start.6 = (bf16[432,512]{1,0:T(8,128)(2,1)S(1)}, bf16[432,512]{1,0:T(8,128)(2,1)S(1)}, u32[]{:S(2)}, u32[]{:S(2)}) collective-permute-start(bf16[432,512]{1,0:T(8,128)(2,1)S(1)} %collective-permute-done.refs_1_), channel_id=1, source_target_pairs={{0,16},{1,3},{2,18},{3,1},{16,0},{17,19},{18,2},{19,17},{4,20},{5,... | collective-permute-start | bytes 1327112 | tf_op jit(solution)/shard_map/ppermute | solution.py:310
  27.9 16.3 %collective-permute-start.8 = (bf16[432,512]{1,0:T(8,128)(2,1)S(1)}, bf16[432,512]{1,0:T(8,128)(2,1)S(1)}, u32[]{:S(2)}, u32[]{:S(2)}) collective-permute-start(bf16[432,512]{1,0:T(8,128)(2,1)S(1)} %collective-permute-done.refs_1_), channel_id=1, source_target_pairs={{0,1},{1,0},{2,3},{3,2},{4,5},{5,4},{6,7},{7,6},{8,9},{9,8},{10,11... | collective-permute-start | bytes 1327112 | tf_op jit(solution)/shard_map/ppermute | solution.py:312
  37.1 7.0 %collective-permute-start.9 = (bf16[432,512]{1,0:T(8,128)(2,1)S(1)}, bf16[432,512]{1,0:T(8,128)(2,1)S(1)}, u32[]{:S(2)}, u32[]{:S(2)}) collective-permute-start(bf16[432,512]{1,0:T(8,128)(2,1)S(1)} %collective-permute-done.5.refs_2_), channel_id=1, source_target_pairs={{0,1},{1,0},{2,3},{3,2},{4,5},{5,4},{6,7},{7,6},{8,9},{9,8},{10,11... | collective-permute-start | bytes 1327112 | tf_op jit(solution)/shard_map/ppermute | solution.py:312
  37.2 8.3 %collective-permute-start.7 = (bf16[432,512]{1,0:T(8,128)(2,1)S(1)}, bf16[432,512]{1,0:T(8,128)(2,1)S(1)}, u32[]{:S(2)}, u32[]{:S(2)}) collective-permute-start(bf16[432,512]{1,0:T(8,128)(2,1)S(1)} %collective-permute-done.5.refs_2_), channel_id=1, source_target_pairs={{0,16},{1,3},{2,18},{3,1},{16,0},{17,19},{18,2},{19,17},{4,20},{5,... | collective-permute-start | bytes 1327112 | tf_op jit(solution)/shard_map/ppermute | solution.py:311
  40.5 3.6 %collective-permute-start.10 = (bf16[1,1,272,128]{3,2,1,0:T(8,128)(2,1)S(1)}, bf16[1,1,272,128]{3,2,1,0:T(8,128)(2,1)S(1)}, u32[]{:S(2)}, u32[]{:S(2)}) collective-permute-start(bf16[1,1,272,128]{3,2,1,0:T(8,128)(2,1)S(1)} %get-tuple-element.47), channel_id=1, source_target_pairs={{1,2},{2,1},{5,6},{6,5},{9,10},{10,9},{13,14},{14,13},{17,18},{18,... | collective-permute-start | bytes 208904 | tf_op jit(solution)/shard_map/ppermute | solution.py:272
  41.2 5.0 %collective-permute-start.11 = (bf16[432,512]{1,0:T(8,128)(2,1)S(1)}, bf16[432,512]{1,0:T(8,128)(2,1)S(1)}, u32[]{:S(2)}, u32[]{:S(2)}) collective-permute-start(bf16[432,512]{1,0:T(8,128)(2,1)S(1)} %collective-permute-done.6.refs_3_), channel_id=1, source_target_pairs={{0,1},{1,0},{2,3},{3,2},{4,5},{5,4},{6,7},{7,6},{8,9},{9,8},{10,11... | collective-permute-start | bytes 1327112 | tf_op jit(solution)/shard_map/ppermute | solution.py:314
  45.5 2.1 %collective-permute-start.12 = (bf16[432,512]{1,0:T(8,128)(2,1)S(1)}, bf16[432,512]{1,0:T(8,128)(2,1)S(1)}, u32[]{:S(2)}, u32[]{:S(2)}) collective-permute-start(bf16[432,512]{1,0:T(8,128)(2,1)S(1)} %collective-permute-done.7.refs_4_), channel_id=1, source_target_pairs={{0,1},{1,0},{2,3},{3,2},{4,5},{5,4},{6,7},{7,6},{8,9},{9,8},{10,11... | collective-permute-start | bytes 1327112 | tf_op jit(solution)/shard_map/ppermute | solution.py:320
  46.1 5.9 %collective-permute-start.13 = (bf16[1,1,272,128]{3,2,1,0:T(8,128)(2,1)S(1)}, bf16[1,1,272,128]{3,2,1,0:T(8,128)(2,1)S(1)}, u32[]{:S(2)}, u32[]{:S(2)}) collective-permute-start(bf16[1,1,272,128]{3,2,1,0:T(8,128)(2,1)S(1)} %get-tuple-element.46), channel_id=1, source_target_pairs={{0,1},{1,0},{2,3},{3,2},{4,5},{5,4},{6,7},{7,6},{8,9},{9,8},{10,11... | collective-permute-start | bytes 208904 | tf_op jit(solution)/shard_map/ppermute | solution.py:269
  46.2 16.0 %collective-permute-start.4 = (bf16[4,272,128]{2,1,0:T(8,128)(2,1)S(1)}, bf16[4,272,128]{2,1,0:T(8,128)(2,1)S(1)}, u32[]{:S(2)}, u32[]{:S(2)}) collective-permute-start(bf16[4,272,128]{2,1,0:T(8,128)(2,1)S(1)} %get-tuple-element.25), channel_id=1, source_target_pairs={{0,8},{4,12},{8,0},{12,4},{1,9},{5,13},{9,1},{13,5},{2,10},{6,14},... | collective-permute-start | bytes 835592 | tf_op jit(solution)/shard_map/ppermute | solution.py:315
  49.0 22.4 %collective-permute-start.18 = (bf16[1,256,512]{2,1,0:T(8,128)(2,1)S(1)}, bf16[1,256,512]{2,1,0:T(8,128)(2,1)S(1)}, u32[]{:S(2)}, u32[]{:S(2)}) collective-permute-start(bf16[1,256,512]{2,1,0:T(8,128)(2,1)S(1)} %get-tuple-element.31), channel_id=1, source_target_pairs={{0,4},{4,0},{8,12},{12,8},{1,5},{5,1},{9,13},{13,9},{2,6},{6,2},{1... | collective-permute-start | bytes 786440 | tf_op jit(solution)/shard_map/ppermute | solution.py:326
  54.3 21.1 %collective-permute-start.17 = (bf16[2,256,512]{2,1,0:T(8,128)(2,1)S(1)}, bf16[2,256,512]{2,1,0:T(8,128)(2,1)S(1)}, u32[]{:S(2)}, u32[]{:S(2)}) collective-permute-start(bf16[2,256,512]{2,1,0:T(8,128)(2,1)S(1)} %conv_blocks.9), channel_id=1, source_target_pairs={{0,4},{4,0},{8,12},{12,8},{1,5},{5,1},{9,13},{13,9},{2,6},{6,2},{1... | collective-permute-start | bytes 1572872 | tf_op jit(solution)/shard_map/ppermute | solution.py:333
  62.2 4.0 %collective-permute-start.15 = (bf16[1,1,272,128]{3,2,1,0:T(8,128)(2,1)S(1)}, bf16[1,1,272,128]{3,2,1,0:T(8,128)(2,1)S(1)}, u32[]{:S(2)}, u32[]{:S(2)}) collective-permute-start(bf16[1,1,272,128]{3,2,1,0:T(8,128)(2,1)S(1)} %get-tuple-element.44), channel_id=1, source_target_pairs={{1,2},{2,1},{5,6},{6,5},{9,10},{10,9},{13,14},{14,13},{17,18},{18,... | collective-permute-start | bytes 208904 | tf_op jit(solution)/shard_map/ppermute | solution.py:272
  63.0 4.0 %collective-permute-start.14 = (bf16[1,1,272,128]{3,2,1,0:T(8,128)(2,1)S(1)}, bf16[1,1,272,128]{3,2,1,0:T(8,128)(2,1)S(1)}, u32[]{:S(2)}, u32[]{:S(2)}) collective-permute-start(bf16[1,1,272,128]{3,2,1,0:T(8,128)(2,1)S(1)} %get-tuple-element.45), channel_id=1, source_target_pairs={{0,1},{1,0},{2,3},{3,2},{4,5},{5,4},{6,7},{7,6},{8,9},{9,8},{10,11... | collective-permute-start | bytes 208904 | tf_op jit(solution)/shard_map/ppermute | solution.py:269
  66.1 14.2 %collective-permute-start.16 = (bf16[1,256,512]{2,1,0:T(8,128)(2,1)S(1)}, bf16[1,256,512]{2,1,0:T(8,128)(2,1)S(1)}, u32[]{:S(2)}, u32[]{:S(2)}) collective-permute-start(bf16[1,256,512]{2,1,0:T(8,128)(2,1)S(1)} %conv_blocks.10), channel_id=1, source_target_pairs={{0,4},{4,0},{8,12},{12,8},{1,5},{5,1},{9,13},{13,9},{2,6},{6,2},{1... | collective-permute-start | bytes 786440 | tf_op jit(solution)/shard_map/ppermute | solution.py:333
  67.0 4.3 %copy-start = (bf16[8,256,512]{2,1,0:T(8,128)(2,1)S(1)}, bf16[8,256,512]{2,1,0:T(8,128)(2,1)}, u32[]{:S(2)}) copy-start(bf16[8,256,512]{2,1,0:T(8,128)(2,1)} %weight_ref.5) | copy-start | bytes 6291460

commit v7 on v5

--- a/solution.py
+++ b/solution.py
@@ -302,8 +302,8 @@
     pair_b = lax.ppermute(got_b, "pair", other)
     far_two = lax.ppermute(after(window_two, far_one), "chan", far)
     one_inner, one_outer = margins(far_one[None])
-    got_c, pair_got, pair_a, one_inner, one_outer = lax.optimization_barrier(
-        (got_c, pair_got, pair_a, one_inner, one_outer)
+    got_c, pair_got, pair_a, one_outer = lax.optimization_barrier(
+        (got_c, pair_got, pair_a, one_outer)
     )
     pair_c = lax.ppermute(got_c, "pair", other)
     pieces = [got, got_a, got_b, got_c, pair_got, pair_a, pair_b, pair_c]

time: 82.5 us -> 82.4 us (level)
    ppermute x3, starting transfers between devices: 6.09 us -> 3.26 us  [margins(): lax.ppermute(jnp.where(lax.axis_index('pair') == 0, tail, head), 'pair',...]
    ppermute x1, waiting for transfers between devices: 0.01 us -> 1.32 us  [two_level_body(): got_c = lax.ppermute(got_a, PLANAR, second)]
    ppermute x1, waiting for transfers between devices: 1.24 us -> 0.01 us  [two_level_body(): pair_b = lax.ppermute(got_b, 'pair', other)]
    ppermute x1, starting transfers between devices: 1.9 us -> 2.91 us  [two_level_body(): pair_b = lax.ppermute(got_b, 'pair', other)]
where the time goes in v7:
time: 82.4 us; the launch traced here: 82.2 us
  waiting for transfers between devices  32.9 us (40%)
  Pallas kernels  24.5 us (30%)
  starting transfers between devices  20.2 us (25%)
  local copies, waits for them, and re-layouts  3.48 us (4%)
  other arithmetic  0.9 us (1%)
    pallas_call x6, Pallas kernels, conv_blocks(): pl.pallas_call(functools.partial(conv_kernel, sources=[(len(v[0]) > 1, le...  17.9 us
    ppermute x1, waiting for transfers between devices, two_level_body(): got_a = lax.ppermute(got, PLANAR, first)  9.28 us
    ppermute x1, waiting for transfers between devices, two_level_body(): got = lax.ppermute(piece, 'chan', far)  6.71 us
    pallas_call x3, Pallas kernels, down_blocks(): pl.pallas_call(functools.partial(down_kernel, first=first, step=step), gr...  6.63 us
    ppermute x1, waiting for transfers between devices, two_level_body(): far_two = lax.ppermute(after(window_two, far_one), 'chan', far)  6.53 us
    ppermute x2, waiting for transfers between devices, two_level_body(): theirs.append(lax.ppermute(sent, 'chan', near))  4.19 us
    ppermute x1, starting transfers between devices, two_level_body(): got = lax.ppermute(piece, 'chan', far)  4.1 us
    ppermute x3, starting transfers between devices, margins(): lax.ppermute(jnp.where(lax.axis_index('pair') == 0, tail, head), 'pair',...  3.26 us
  transfers between devices with their start and end apart: 19, of which 9 were waited for; matrix products, arithmetic and copies ran while one was open for 4% of the time, Pallas kernels for 28%

profile of v7, /device:TPU:0, one launch (start us, length us, event | category | flops | bytes accessed | tf_op | source)
XLA Modules:
  0.0 82.2 jit_solution(9171125169224766702)
XLA Ops:
  1.0 4.1 %collective-permute-start = (bf16[432,512]{1,0:T(8,128)(2,1)S(1)}, bf16[432,512]{1,0:T(8,128)(2,1)S(1)}, u32[]{:S(2)}, u32[]{:S(2)}) collective-permute-start(bf16[432,512]{1,0:T(8,128)(2,1)S(1)} %constant_dynamic-slice_fusion), channel_id=1, source_target_pairs={{0,8},{4,12},{8,0},{12,4},{1,9},{5,13},{9,1},{13,5},{2,10},{6,14},... | collective-permute-start | bytes 1327112 | tf_op jit(solution)/shard_map/ppermute | solution.py:268
  5.1 1.9 %copy.7 = bf16[128,4,1024]{0,2,1:T(8,128)(2,1)S(1)} copy(bf16[128,4,1024]{2,1,0:T(4,128)(2,1)} %param.4) | data formatting | bytes 2097152 | tf_op jit(solution)/shard_map/optimization_barrier | solution.py:253
  9.4 4.3 %conv_blocks.7.refs_4_ = f32[4,256,512]{2,1,0:T(8,128)S(1)} custom-call(s32[1]{0:T(128)} %bitcast.where_ref, bf16[4,272,128]{2,1,0:T(8,128)(2,1)S(1)} %get-tuple-element.40.refs_0_, bf16[272,128]{1,0:T(8,128)(2,1)S(1)} %get-tuple-element.50.refs_1_, bf16[272,128]{1,0:T(8,128)(2,1)S(1)} %get-tuple-element.48.refs_2_, bf16[3456,512]{1,0:T(8,128)(2,1)S(1)} %bitcast.30), custom_call_target="tpu_custom_call" | custom-call | flops 3623878656 | bytes 4587520 | tf_op jit(solution)/shard_map/conv_blocks/pallas_call | solution.py:166
  13.8 4.3 %conv_blocks.6.refs_9_.refs_4_ = f32[4,256,512]{2,1,0:T(8,128)S(1)} custom-call(s32[1]{0:T(128)} %bitcast.where_ref, bf16[4,272,128]{2,1,0:T(8,128)(2,1)S(1)} %get-tuple-element.42.refs_0_, bf16[272,128]{1,0:T(8,128)(2,1)S(1)} %get-tuple-element.51.refs_1_, bf16[272,128]{1,0:T(8,128)(2,1)S(1)} %get-tuple-element.49.refs_2_, bf16[3456,512]{1,0:T(8,128)(2,1)S(1)} %bitcast.31), custom_call_target="tpu_custom_call" | custom-call | flops 3623878656 | bytes 4587520 | tf_op jit(solution)/shard_map/conv_blocks/pallas_call | solution.py:166
  18.1 6.7 %collective-permute-done.refs_1_ = bf16[432,512]{1,0:T(8,128)(2,1)S(1)} collective-permute-done((bf16[432,512]{1,0:T(8,128)(2,1)S(1)}, bf16[432,512]{1,0:T(8,128)(2,1)S(1)}, u32[]{:S(2)}, u32[]{:S(2)}) %collective-permute-start) | collective-permute-done | bytes 442400 | tf_op jit(solution)/shard_map/ppermute | solution.py:268
  24.8 1.5 %collective-permute-start.5 = (bf16[432,512]{1,0:T(8,128)(2,1)S(1)}, bf16[432,512]{1,0:T(8,128)(2,1)S(1)}, u32[]{:S(2)}, u32[]{:S(2)}) collective-permute-start(bf16[432,512]{1,0:T(8,128)(2,1)S(1)} %collective-permute-done.refs_1_), channel_id=1, source_target_pairs={{0,2},{1,17},{2,0},{3,19},{16,18},{17,1},{18,16},{19,3},{4,6},{5,2... | collective-permute-start | bytes 1327112 | tf_op jit(solution)/shard_map/ppermute | solution.py:297
  26.3 1.5 %collective-permute-start.6 = (bf16[432,512]{1,0:T(8,128)(2,1)S(1)}, bf16[432,512]{1,0:T(8,128)(2,1)S(1)}, u32[]{:S(2)}, u32[]{:S(2)}) collective-permute-start(bf16[432,512]{1,0:T(8,128)(2,1)S(1)} %collective-permute-done.refs_1_), channel_id=1, source_target_pairs={{0,16},{1,3},{2,18},{3,1},{16,0},{17,19},{18,2},{19,17},{4,20},{5,... | collective-permute-start | bytes 1327112 | tf_op jit(solution)/shard_map/ppermute | solution.py:298
  27.9 9.3 %collective-permute-done.5.refs_2_ = bf16[432,512]{1,0:T(8,128)(2,1)S(1)} collective-permute-done((bf16[432,512]{1,0:T(8,128)(2,1)S(1)}, bf16[432,512]{1,0:T(8,128)(2,1)S(1)}, u32[]{:S(2)}, u32[]{:S(2)}) %collective-permute-start.5) | collective-permute-done | bytes 442400 | tf_op jit(solution)/shard_map/ppermute | solution.py:297
  37.9 2.6 %collective-permute-done.3.refs_0_ = bf16[4,272,128]{2,1,0:T(8,128)(2,1)S(1)} collective-permute-done((bf16[4,272,128]{2,1,0:T(8,128)(2,1)S(1)}, bf16[4,272,128]{2,1,0:T(8,128)(2,1)S(1)}, u32[]{:S(2)}, u32[]{:S(2)}) %collective-permute-start.3) | collective-permute-done | bytes 278560 | tf_op jit(solution)/shard_map/ppermute | solution.py:296
  41.2 2.9 %collective-permute-start.11 = (bf16[432,512]{1,0:T(8,128)(2,1)S(1)}, bf16[432,512]{1,0:T(8,128)(2,1)S(1)}, u32[]{:S(2)}, u32[]{:S(2)}) collective-permute-start(bf16[432,512]{1,0:T(8,128)(2,1)S(1)} %collective-permute-done.6.refs_3_), channel_id=1, source_target_pairs={{0,1},{1,0},{2,3},{3,2},{4,5},{5,4},{6,7},{7,6},{8,9},{9,8},{10,11... | collective-permute-start | bytes 1327112 | tf_op jit(solution)/shard_map/ppermute | solution.py:302
  44.1 1.3 %collective-permute-done.7.refs_4_ = bf16[432,512]{1,0:T(8,128)(2,1)S(1)} collective-permute-done((bf16[432,512]{1,0:T(8,128)(2,1)S(1)}, bf16[432,512]{1,0:T(8,128)(2,1)S(1)}, u32[]{:S(2)}, u32[]{:S(2)}) %collective-permute-start.7) | collective-permute-done | bytes 442400 | tf_op jit(solution)/shard_map/ppermute | solution.py:299
  46.2 1.3 %collective-permute-done.12.refs_8_ = bf16[432,512]{1,0:T(8,128)(2,1)S(1)} collective-permute-done((bf16[432,512]{1,0:T(8,128)(2,1)S(1)}, bf16[432,512]{1,0:T(8,128)(2,1)S(1)}, u32[]{:S(2)}, u32[]{:S(2)}) %collective-permute-start.12) | collective-permute-done | bytes 442400 | tf_op jit(solution)/shard_map/ppermute | solution.py:308
  47.5 1.5 %conv_blocks.8 = (bf16[1,256,512]{2,1,0:T(8,128)(2,1)S(1)}, bf16[3456,512]{1,0:T(8,128)(2,1)S(1)}) custom-call(s32[1]{0:T(128)} %bitcast.where_ref, bf16[4,272,128]{2,1,0:T(8,128)(2,1)S(1)} %collective-permute-done.3.refs_0_, bf16[432,512]{1,0:T(8,128)(2,1)S(1)} %collective-permute-done.refs_1_, bf16[432,512]{1,0:T(8,128)(2,1)S(1)} %collective-permute-done.5.refs_2_, ...), custom_call_target="tpu_custom_call" | custom-call | flops 905969664 | bytes 3801088 | tf_op jit(solution)/shard_map/conv_blocks/pallas_call | solution.py:166
  49.0 3.0 %collective-permute-start.18 = (bf16[1,256,512]{2,1,0:T(8,128)(2,1)S(1)}, bf16[1,256,512]{2,1,0:T(8,128)(2,1)S(1)}, u32[]{:S(2)}, u32[]{:S(2)}) collective-permute-start(bf16[1,256,512]{2,1,0:T(8,128)(2,1)S(1)} %get-tuple-element.31), channel_id=1, source_target_pairs={{0,4},{4,0},{8,12},{12,8},{1,5},{5,1},{9,13},{13,9},{2,6},{6,2},{1... | collective-permute-start | bytes 786440 | tf_op jit(solution)/shard_map/ppermute | solution.py:314
  52.0 2.3 %conv_blocks.9 = bf16[2,256,512]{2,1,0:T(8,128)(2,1)S(1)} custom-call(s32[1]{0:T(128)} %bitcast.where_ref, bf16[4,272,128]{2,1,0:T(8,128)(2,1)S(1)} %collective-permute-done.3.refs_0_, bf16[272,128]{1,0:T(8,128)(2,1)S(1)} %bitcast.25, bf16[272,128]{1,0:T(8,128)(2,1)S(1)} %bitcast.23, bf16[3456,512]{1,0:T(8,128)(2,1)S(1)} %get-tuple-element.34.refs_3_, ...), custom_call_target="tpu_custom_call" | custom-call | flops 1811939328 | bytes 4063232 | tf_op jit(solution)/shard_map/conv_blocks/pallas_call | solution.py:166
  54.4 1.2 %conv_blocks.10 = bf16[1,256,512]{2,1,0:T(8,128)(2,1)S(1)} custom-call(s32[1]{0:T(128)} %bitcast.where_ref, bf16[4,272,128]{2,1,0:T(8,128)(2,1)S(1)} %collective-permute-done.3.refs_0_, bf16[272,128]{1,0:T(8,128)(2,1)S(1)} %bitcast.26, bf16[272,128]{1,0:T(8,128)(2,1)S(1)} %bitcast.24, bf16[3456,512]{1,0:T(8,128)(2,1)S(1)} %get-tuple-element.34.refs_3_, ...), custom_call_target="tpu_custom_call" | custom-call | flops 905969664 | bytes 3801088 | tf_op jit(solution)/shard_map/conv_blocks/pallas_call | solution.py:166
  55.6 6.5 %collective-permute-done.4.refs_0_ = bf16[4,272,128]{2,1,0:T(8,128)(2,1)S(1)} collective-permute-done((bf16[4,272,128]{2,1,0:T(8,128)(2,1)S(1)}, bf16[4,272,128]{2,1,0:T(8,128)(2,1)S(1)}, u32[]{:S(2)}, u32[]{:S(2)}) %collective-permute-start.4) | collective-permute-done | bytes 278560 | tf_op jit(solution)/shard_map/ppermute | solution.py:303
  63.0 3.1 %collective-permute-start.14 = (bf16[1,1,272,128]{3,2,1,0:T(8,128)(2,1)S(1)}, bf16[1,1,272,128]{3,2,1,0:T(8,128)(2,1)S(1)}, u32[]{:S(2)}, u32[]{:S(2)}) collective-permute-start(bf16[1,1,272,128]{3,2,1,0:T(8,128)(2,1)S(1)} %get-tuple-element.45), channel_id=1, source_target_pairs={{0,1},{1,0},{2,3},{3,2},{4,5},{5,4},{6,7},{7,6},{8,9},{9,8},{10,11... | collective-permute-start | bytes 208904 | tf_op jit(solution)/shard_map/ppermute | solution.py:257
  67.1 4.3 %conv_blocks.11.mine_ref = f32[4,256,512]{2,1,0:T(8,128)S(1)} custom-call(s32[1]{0:T(128)} %bitcast.where_ref, bf16[4,272,128]{2,1,0:T(8,128)(2,1)S(1)} %collective-permute-done.4.refs_0_, bf16[272,128]{1,0:T(8,128)(2,1)S(1)} %bitcast.28, bf16[272,128]{1,0:T(8,128)(2,1)S(1)} %bitcast.27, bf16[3456,512]{1,0:T(8,128)(2,1)S(1)} %get-tuple-element.34.refs_3_, ...), custom_call_target="tpu_custom_call" | custom-call | flops 1811939328 | bytes 2293760 | tf_op jit(solution)/shard_map/conv_blocks/pallas_call | solution.py:166
  71.4 1.9 %down_blocks.3.refs_0_ = bf16[4,256,8,256]{3,2,1,0:T(8,128)(2,1)} custom-call(f32[4,256,512]{2,1,0:T(8,128)S(1)} %conv_blocks.11.mine_ref, bf16[1,256,512]{2,1,0:T(8,128)(2,1)S(1)} %collective-permute-done.18.theirs_ref, f32[4,256,512]{2,1,0:T(8,128)S(1)} %fusion.3.slope_ref, bf16[8,256,512]{2,1,0:T(8,128)(2,1)S(1)} %copy-done), custom_call_target="tpu_custom_call" | custom-call | flops 536870912 | bytes 2359296 | tf_op jit(solution)/shard_map/down_blocks/pallas_call | solution.py:216
  73.3 2.1 %collective-permute-done.17.theirs_ref = bf16[2,256,512]{2,1,0:T(8,128)(2,1)S(1)} collective-permute-done((bf16[2,256,512]{2,1,0:T(8,128)(2,1)S(1)}, bf16[2,256,512]{2,1,0:T(8,128)(2,1)S(1)}, u32[]{:S(2)}, u32[]{:S(2)}) %collective-permute-start.17) | collective-permute-done | bytes 524320 | tf_op jit(solution)/shard_map/ppermute | solution.py:321
  75.4 2.8 %down_blocks.4.refs_0_ = bf16[4,256,8,256]{3,2,1,0:T(8,128)(2,1)} custom-call(f32[4,256,512]{2,1,0:T(8,128)S(1)} %conv_blocks.11.mine_ref, bf16[2,256,512]{2,1,0:T(8,128)(2,1)S(1)} %collective-permute-done.17.theirs_ref, f32[4,256,512]{2,1,0:T(8,128)S(1)} %fusion.3.slope_ref, bf16[8,256,512]{2,1,0:T(8,128)(2,1)S(1)} %copy-done, ...), custom_call_target="tpu_custom_call", output_to_operand_aliasing={{}: (4, {})} | custom-call | flops 1073741824 | bytes 4718592 | tf_op jit(solution)/shard_map/down_blocks/pallas_call | solution.py:216
  78.3 2.0 %collective-permute-done.16.theirs_ref = bf16[1,256,512]{2,1,0:T(8,128)(2,1)S(1)} collective-permute-done((bf16[1,256,512]{2,1,0:T(8,128)(2,1)S(1)}, bf16[1,256,512]{2,1,0:T(8,128)(2,1)S(1)}, u32[]{:S(2)}, u32[]{:S(2)}) %collective-permute-start.16) | collective-permute-done | bytes 262176 | tf_op jit(solution)/shard_map/ppermute | solution.py:321
  80.3 1.9 %down_blocks.5 = bf16[4,256,8,256]{3,2,1,0:T(8,128)(2,1)} custom-call(f32[4,256,512]{2,1,0:T(8,128)S(1)} %conv_blocks.11.mine_ref, bf16[1,256,512]{2,1,0:T(8,128)(2,1)S(1)} %collective-permute-done.16.theirs_ref, f32[4,256,512]{2,1,0:T(8,128)S(1)} %fusion.3.slope_ref, bf16[8,256,512]{2,1,0:T(8,128)(2,1)S(1)} %copy-done, ...), custom_call_target="tpu_custom_call", output_to_operand_aliasing={{}: (4, {})} | custom-call | flops 536870912 | bytes 2359296 | tf_op jit(solution)/shard_map/down_blocks/pallas_call | solution.py:216
  (39 shorter events, 7.3 us)
Async XLA Ops:
  1.0 23.7 %collective-permute-start = (bf16[432,512]{1,0:T(8,128)(2,1)S(1)}, bf16[432,512]{1,0:T(8,128)(2,1)S(1)}, u32[]{:S(2)}, u32[]{:S(2)}) collective-permute-start(bf16[432,512]{1,0:T(8,128)(2,1)S(1)} %constant_dynamic-slice_fusion), channel_id=1, source_target_pairs={{0,8},{4,12},{8,0},{12,4},{1,9},{5,13},{9,1},{13,5},{2,10},{6,14},... | collective-permute-start | bytes 1327112 | tf_op jit(solution)/shard_map/ppermute | solution.py:268
  7.1 1.2 %copy-start.2 = (bf16[4,256,512]{2,1,0:T(8,128)(2,1)S(1)}, bf16[4,256,512]{2,1,0:T(8,128)(2,1)}, u32[]{:S(2)}) copy-start(bf16[4,256,512]{2,1,0:T(8,128)(2,1)} %param.6) | copy-start | bytes 3145732
  7.3 2.2 %copy-start.1 = (bf16[27,128,512]{2,1,0:T(8,128)(2,1)S(1)}, bf16[27,128,512]{2,1,0:T(8,128)(2,1)}, u32[]{:S(2)}) copy-start(bf16[27,128,512]{2,1,0:T(8,128)(2,1)} %param.5) | copy-start | bytes 10616836
  7.3 1.8 %collective-permute-start.1 = (bf16[2,1,272,128]{3,2,1,0:T(8,128)(2,1)S(1)}, bf16[2,1,272,128]{3,2,1,0:T(8,128)(2,1)S(1)}, u32[]{:S(2)}, u32[]{:S(2)}) collective-permute-start(bf16[2,1,272,128]{3,2,1,0:T(8,128)(2,1)S(1)} %broadcast_select_fusion.1), channel_id=1, source_target_pairs={{0,1},{1,0},{2,3},{3,2},{4,5},{5,4},{6,7},{7,6},{8,9},{9,8},{10,11... | collective-permute-start | bytes 417800 | tf_op jit(solution)/shard_map/ppermute | solution.py:257
  7.4 1.8 %collective-permute-start.2 = (bf16[2,1,272,128]{3,2,1,0:T(8,128)(2,1)S(1)}, bf16[2,1,272,128]{3,2,1,0:T(8,128)(2,1)S(1)}, u32[]{:S(2)}, u32[]{:S(2)}) collective-permute-start(bf16[2,1,272,128]{3,2,1,0:T(8,128)(2,1)S(1)} %get-tuple-element.37), channel_id=1, source_target_pairs={{1,2},{2,1},{5,6},{6,5},{9,10},{10,9},{13,14},{14,13},{17,18},{18,... | collective-permute-start | bytes 417800 | tf_op jit(solution)/shard_map/ppermute | solution.py:260
  24.8 12.4 %collective-permute-start.5 = (bf16[432,512]{1,0:T(8,128)(2,1)S(1)}, bf16[432,512]{1,0:T(8,128)(2,1)S(1)}, u32[]{:S(2)}, u32[]{:S(2)}) collective-permute-start(bf16[432,512]{1,0:T(8,128)(2,1)S(1)} %collective-permute-done.refs_1_), channel_id=1, source_target_pairs={{0,2},{1,17},{2,0},{3,19},{16,18},{17,1},{18,16},{19,3},{4,6},{5,2... | collective-permute-start | bytes 1327112 | tf_op jit(solution)/shard_map/ppermute | solution.py:297
  26.3 14.2 %collective-permute-start.3 = (bf16[4,272,128]{2,1,0:T(8,128)(2,1)S(1)}, bf16[4,272,128]{2,1,0:T(8,128)(2,1)S(1)}, u32[]{:S(2)}, u32[]{:S(2)}) collective-permute-start(bf16[4,272,128]{2,1,0:T(8,128)(2,1)S(1)} %get-tuple-element.24), channel_id=1, source_target_pairs={{0,8},{4,12},{8,0},{12,4},{1,9},{5,13},{9,1},{13,5},{2,10},{6,14},... | collective-permute-start | bytes 835592 | tf_op jit(solution)/shard_map/ppermute | solution.py:296
  26.3 14.9 %collective-permute-start.6 = (bf16[432,512]{1,0:T(8,128)(2,1)S(1)}, bf16[432,512]{1,0:T(8,128)(2,1)S(1)}, u32[]{:S(2)}, u32[]{:S(2)}) collective-permute-start(bf16[432,512]{1,0:T(8,128)(2,1)S(1)} %collective-permute-done.refs_1_), channel_id=1, source_target_pairs={{0,16},{1,3},{2,18},{3,1},{16,0},{17,19},{18,2},{19,17},{4,20},{5,... | collective-permute-start | bytes 1327112 | tf_op jit(solution)/shard_map/ppermute | solution.py:298
  27.9 16.3 %collective-permute-start.8 = (bf16[432,512]{1,0:T(8,128)(2,1)S(1)}, bf16[432,512]{1,0:T(8,128)(2,1)S(1)}, u32[]{:S(2)}, u32[]{:S(2)}) collective-permute-start(bf16[432,512]{1,0:T(8,128)(2,1)S(1)} %collective-permute-done.refs_1_), channel_id=1, source_target_pairs={{0,1},{1,0},{2,3},{3,2},{4,5},{5,4},{6,7},{7,6},{8,9},{9,8},{10,11... | collective-permute-start | bytes 1327112 | tf_op jit(solution)/shard_map/ppermute | solution.py:300
  37.1 7.0 %collective-permute-start.9 = (bf16[432,512]{1,0:T(8,128)(2,1)S(1)}, bf16[432,512]{1,0:T(8,128)(2,1)S(1)}, u32[]{:S(2)}, u32[]{:S(2)}) collective-permute-start(bf16[432,512]{1,0:T(8,128)(2,1)S(1)} %collective-permute-done.5.refs_2_), channel_id=1, source_target_pairs={{0,1},{1,0},{2,3},{3,2},{4,5},{5,4},{6,7},{7,6},{8,9},{9,8},{10,11... | collective-permute-start | bytes 1327112 | tf_op jit(solution)/shard_map/ppermute | solution.py:300
  37.2 8.3 %collective-permute-start.7 = (bf16[432,512]{1,0:T(8,128)(2,1)S(1)}, bf16[432,512]{1,0:T(8,128)(2,1)S(1)}, u32[]{:S(2)}, u32[]{:S(2)}) collective-permute-start(bf16[432,512]{1,0:T(8,128)(2,1)S(1)} %collective-permute-done.5.refs_2_), channel_id=1, source_target_pairs={{0,16},{1,3},{2,18},{3,1},{16,0},{17,19},{18,2},{19,17},{4,20},{5,... | collective-permute-start | bytes 1327112 | tf_op jit(solution)/shard_map/ppermute | solution.py:299
  40.5 3.6 %collective-permute-start.10 = (bf16[1,1,272,128]{3,2,1,0:T(8,128)(2,1)S(1)}, bf16[1,1,272,128]{3,2,1,0:T(8,128)(2,1)S(1)}, u32[]{:S(2)}, u32[]{:S(2)}) collective-permute-start(bf16[1,1,272,128]{3,2,1,0:T(8,128)(2,1)S(1)} %get-tuple-element.47), channel_id=1, source_target_pairs={{1,2},{2,1},{5,6},{6,5},{9,10},{10,9},{13,14},{14,13},{17,18},{18,... | collective-permute-start | bytes 208904 | tf_op jit(solution)/shard_map/ppermute | solution.py:260
  41.2 5.0 %collective-permute-start.11 = (bf16[432,512]{1,0:T(8,128)(2,1)S(1)}, bf16[432,512]{1,0:T(8,128)(2,1)S(1)}, u32[]{:S(2)}, u32[]{:S(2)}) collective-permute-start(bf16[432,512]{1,0:T(8,128)(2,1)S(1)} %collective-permute-done.6.refs_3_), channel_id=1, source_target_pairs={{0,1},{1,0},{2,3},{3,2},{4,5},{5,4},{6,7},{7,6},{8,9},{9,8},{10,11... | collective-permute-start | bytes 1327112 | tf_op jit(solution)/shard_map/ppermute | solution.py:302
  45.5 2.1 %collective-permute-start.12 = (bf16[432,512]{1,0:T(8,128)(2,1)S(1)}, bf16[432,512]{1,0:T(8,128)(2,1)S(1)}, u32[]{:S(2)}, u32[]{:S(2)}) collective-permute-start(bf16[432,512]{1,0:T(8,128)(2,1)S(1)} %collective-permute-done.7.refs_4_), channel_id=1, source_target_pairs={{0,1},{1,0},{2,3},{3,2},{4,5},{5,4},{6,7},{7,6},{8,9},{9,8},{10,11... | collective-permute-start | bytes 1327112 | tf_op jit(solution)/shard_map/ppermute | solution.py:308
  46.1 5.9 %collective-permute-start.13 = (bf16[1,1,272,128]{3,2,1,0:T(8,128)(2,1)S(1)}, bf16[1,1,272,128]{3,2,1,0:T(8,128)(2,1)S(1)}, u32[]{:S(2)}, u32[]{:S(2)}) collective-permute-start(bf16[1,1,272,128]{3,2,1,0:T(8,128)(2,1)S(1)} %get-tuple-element.46), channel_id=1, source_target_pairs={{0,1},{1,0},{2,3},{3,2},{4,5},{5,4},{6,7},{7,6},{8,9},{9,8},{10,11... | collective-permute-start | bytes 208904 | tf_op jit(solution)/shard_map/ppermute | solution.py:257
  46.2 16.0 %collective-permute-start.4 = (bf16[4,272,128]{2,1,0:T(8,128)(2,1)S(1)}, bf16[4,272,128]{2,1,0:T(8,128)(2,1)S(1)}, u32[]{:S(2)}, u32[]{:S(2)}) collective-permute-start(bf16[4,272,128]{2,1,0:T(8,128)(2,1)S(1)} %get-tuple-element.25), channel_id=1, source_target_pairs={{0,8},{4,12},{8,0},{12,4},{1,9},{5,13},{9,1},{13,5},{2,10},{6,14},... | collective-permute-start | bytes 835592 | tf_op jit(solution)/shard_map/ppermute | solution.py:303
  49.0 22.4 %collective-permute-start.18 = (bf16[1,256,512]{2,1,0:T(8,128)(2,1)S(1)}, bf16[1,256,512]{2,1,0:T(8,128)(2,1)S(1)}, u32[]{:S(2)}, u32[]{:S(2)}) collective-permute-start(bf16[1,256,512]{2,1,0:T(8,128)(2,1)S(1)} %get-tuple-element.31), channel_id=1, source_target_pairs={{0,4},{4,0},{8,12},{12,8},{1,5},{5,1},{9,13},{13,9},{2,6},{6,2},{1... | collective-permute-start | bytes 786440 | tf_op jit(solution)/shard_map/ppermute | solution.py:314
  54.3 21.1 %collective-permute-start.17 = (bf16[2,256,512]{2,1,0:T(8,128)(2,1)S(1)}, bf16[2,256,512]{2,1,0:T(8,128)(2,1)S(1)}, u32[]{:S(2)}, u32[]{:S(2)}) collective-permute-start(bf16[2,256,512]{2,1,0:T(8,128)(2,1)S(1)} %conv_blocks.9), channel_id=1, source_target_pairs={{0,4},{4,0},{8,12},{12,8},{1,5},{5,1},{9,13},{13,9},{2,6},{6,2},{1... | collective-permute-start | bytes 1572872 | tf_op jit(solution)/shard_map/ppermute | solution.py:321
  62.2 4.0 %collective-permute-start.15 = (bf16[1,1,272,128]{3,2,1,0:T(8,128)(2,1)S(1)}, bf16[1,1,272,128]{3,2,1,0:T(8,128)(2,1)S(1)}, u32[]{:S(2)}, u32[]{:S(2)}) collective-permute-start(bf16[1,1,272,128]{3,2,1,0:T(8,128)(2,1)S(1)} %get-tuple-element.44), channel_id=1, source_target_pairs={{1,2},{2,1},{5,6},{6,5},{9,10},{10,9},{13,14},{14,13},{17,18},{18,... | collective-permute-start | bytes 208904 | tf_op jit(solution)/shard_map/ppermute | solution.py:260
  63.0 4.0 %collective-permute-start.14 = (bf16[1,1,272,128]{3,2,1,0:T(8,128)(2,1)S(1)}, bf16[1,1,272,128]{3,2,1,0:T(8,128)(2,1)S(1)}, u32[]{:S(2)}, u32[]{:S(2)}) collective-permute-start(bf16[1,1,272,128]{3,2,1,0:T(8,128)(2,1)S(1)} %get-tuple-element.45), channel_id=1, source_target_pairs={{0,1},{1,0},{2,3},{3,2},{4,5},{5,4},{6,7},{7,6},{8,9},{9,8},{10,11... | collective-permute-start | bytes 208904 | tf_op jit(solution)/shard_map/ppermute | solution.py:257
  66.1 14.2 %collective-permute-start.16 = (bf16[1,256,512]{2,1,0:T(8,128)(2,1)S(1)}, bf16[1,256,512]{2,1,0:T(8,128)(2,1)S(1)}, u32[]{:S(2)}, u32[]{:S(2)}) collective-permute-start(bf16[1,256,512]{2,1,0:T(8,128)(2,1)S(1)} %conv_blocks.10), channel_id=1, source_target_pairs={{0,4},{4,0},{8,12},{12,8},{1,5},{5,1},{9,13},{13,9},{2,6},{6,2},{1... | collective-permute-start | bytes 786440 | tf_op jit(solution)/shard_map/ppermute | solution.py:321
  67.0 4.3 %copy-start = (bf16[8,256,512]{2,1,0:T(8,128)(2,1)S(1)}, bf16[8,256,512]{2,1,0:T(8,128)(2,1)}, u32[]{:S(2)}) copy-start(bf16[8,256,512]{2,1,0:T(8,128)(2,1)} %weight_ref.5) | copy-start | bytes 6291460
